TPU v7x, 128 devices: a whole 4x4x4 slice. The times are simulated.
128 devices in a mesh: grp: 2 (over core), reg: 64 (over z, x, y).
Axes of the slice: x: 4, y: 4, z: 4, core: 2. Of those that a mesh axis runs over, the one named last changes fastest.
Arguments:
- cam_jacobian: bfloat16 [18, 262144], P(None, ('grp', 'reg')), may hold values from -6 to 6
- point_jacobian: bfloat16 [6, 262144], P(None, ('grp', 'reg')), may hold values from -6 to 6
- residuals: float32 [2, 262144], P(None, ('grp', 'reg')), may hold values from -48 to 48
- obs_camera: int32 [262144], P(('grp', 'reg')), may hold values from 0 to 16383, as said below
- obs_point: int32 [262144], P(('grp', 'reg')), may hold values from 0 to 255
Outputs:
- cam_step: float32 [9, 16384], P(None, ('grp', 'reg'))
- point_step: float32 [3, 32768], P(None, ('grp', 'reg'))
Inputs may be any that keep to these rules, and one draw needn't show every extreme that they name: `obs_camera`: an observation in block d of 2048 rows sees a camera of block e = camera // 128 such that d // (number of reg devices) and e // (number of reg devices) may differ, but d and e differ by at most one modulo the number of reg devices (the same, the previous or the next region, never across the ends); every such block is seen.
All inputs are finite; a program needn't handle non-finite values.
Results may differ from a plain program's by a relative error of at most 0.0003.
Values sent between devices are 32-bit elements; how exact they have to be, the bound alone decides.
No kernel may reach another device: no remote copies, remote signals or barrier semaphores. Data moves between devices by JAX's collectives and lax.ppermute only.
A program may use at most 64 MiB of HBM per device.

v0:
```python
import jax
import jax.numpy as jnp
from jax import lax
from jax.sharding import Mesh
from jax.sharding import PartitionSpec as P

C_DEV = 128
P_DEV = 256
ITERS = 3
REG = ("reg_0", "reg_1", "reg_2")
GRP_REG = ("grp", "reg_0", "reg_1", "reg_2")


DAMPING = 4.0


def padded(x, sides, width):
    for axis, dim in sides:
        peers, length = (lax.axis_size(axis), x.shape[dim])
        up = [(i, (i + 1) % peers) for i in range(peers - 1)]
        down = [(j, i) for i, j in up]
        last = lax.slice_in_dim(x, length - width, length, axis=dim)
        initial = lax.slice_in_dim(x, 0, width, axis=dim)
        before = lax.ppermute(last, axis, up)
        after = lax.ppermute(initial, axis, down)
        x = jnp.concatenate([before, x, after], axis=dim)
    return x


def in_blocks(x, dim, peers):
    before, after = (x.shape[:dim], x.shape[dim + 1 :])
    return jnp.moveaxis(x.reshape(*before, peers, -1, *after), dim, 0)


def sum_at_owner(x, axis, dim):
    peers = lax.axis_size(axis)
    tiles = lax.all_to_all(in_blocks(x, dim, peers), axis, 0, 0, tiled=True)
    return jnp.sum(tiles, axis=0)


def in_one_piece(arrays, axis, dim, along):
    ends, at = ([], 0)
    for a in arrays[:-1]:
        at += a.shape[along]
        ends.append(at)
    both = jnp.concatenate(arrays, axis=along)
    return tuple(jnp.split(sum_at_owner(both, axis, dim), ends, axis=along))


def from_behind(value, axis, steps):
    count = lax.axis_size(axis)
    initial, last = (max(0, -steps), min(count, count - steps))
    return lax.ppermute(value, axis, [(source, source + steps) for source in range(initial, last)])


def one_axis_at_a_time(x, axes):
    for axis in axes:
        x = lax.psum(x, axis)
    return x


def inverse_three(matrix):
    a, b, c, d, e, f, g, h, i = [matrix[k] for k in range(9)]
    adjoint = [
        e * i - f * h,
        c * h - b * i,
        b * f - c * e,
        f * g - d * i,
        a * i - c * g,
        c * d - a * f,
        d * h - e * g,
        b * g - a * h,
        a * e - b * d,
    ]
    determinant = a * adjoint[0] + b * adjoint[3] + c * adjoint[6]
    return jnp.stack(adjoint) / determinant


def apply_three(inverse, vector):
    return jnp.stack(
        [
            inverse[3 * i] * vector[0]
            + inverse[3 * i + 1] * vector[1]
            + inverse[3 * i + 2] * vector[2]
            for i in range(3)
        ]
    )


def cholesky_rows(blocks):
    factor = [[None] * 9 for i in range(9)]
    for i in range(9):
        for j in range(i + 1):
            total = blocks[9 * i + j]
            for k in range(j):
                total = total - factor[i][k] * factor[j][k]
            if i == j:
                factor[i][i] = jnp.sqrt(total)
            else:
                factor[i][j] = total / factor[j][j]
    return factor


def cholesky_apply(factor, right):
    forward = []
    for i in range(9):
        total = right[i]
        for k in range(i):
            total = total - factor[i][k] * forward[k]
        forward.append(total / factor[i][i])
    backward = [None] * 9
    for i in range(8, -1, -1):
        total = forward[i]
        for k in range(i + 1, 9):
            total = total - factor[k][i] * backward[k]
        backward[i] = total / factor[i][i]
    return jnp.stack(backward)


def sum_into(terms, onehot):
    return jnp.dot(
        terms, onehot, preferred_element_type=jnp.float32, precision=lax.Precision.HIGHEST
    )


def pick_from(field, onehot):
    return lax.dot_general(
        field,
        onehot,
        (((1,), (1,)), ((), ())),
        preferred_element_type=jnp.float32,
        precision=lax.Precision.HIGHEST,
    )


def eliminate(values, cam_rows, point_rows, point_hot, inverse):
    gathered = sum_into(jnp.sum(point_rows * values[:, None], 0), point_hot)
    solved = apply_three(inverse, gathered)
    remain = values - jnp.sum(point_rows * pick_from(solved, point_hot)[None], 1)
    return jnp.sum(cam_rows * remain[:, None], 0)


def spread(field):
    cameras = field.shape[1]
    both_groups = lax.all_gather(field, "grp", axis=1, tiled=True)
    return padded(both_groups, ((REG, 1),), 2 * cameras)


def return_normal(partial_value):
    span = partial_value.shape[1] // 3
    lower_part = partial_value[:, :span]
    middle = partial_value[:, span : 2 * span]
    upper_part = partial_value[:, 2 * span :]
    lower_part, middle, upper_part = in_one_piece((lower_part, middle, upper_part), "grp", 1, 0)
    from_above = from_behind(lower_part, REG, -1)
    from_below = from_behind(upper_part, REG, 1)
    return middle + from_above + from_below


def return_product(partial_value):
    span = partial_value.shape[1] // 3
    lower_part = partial_value[:, :span]
    middle = partial_value[:, span : 2 * span]
    upper_part = partial_value[:, 2 * span :]
    lower_part, middle, upper_part = in_one_piece((lower_part, middle, upper_part), "grp", 1, 0)
    from_above = from_behind(lower_part, REG, -1)
    from_below = from_behind(upper_part, REG, 1)
    return middle + from_above + from_below


def precon_inner(residual, precon):
    return one_axis_at_a_time(jnp.sum(residual * precon), GRP_REG)


def local(cam_jacobian, point_jacobian, residuals, obs_camera, obs_point):
    cameras = C_DEV
    points = P_DEV
    regions = lax.axis_size(REG)
    region = lax.axis_index(REG)
    owners = obs_camera // cameras
    column = (
        (owners % regions - region + 1) * (2 * cameras)
        + owners // regions * cameras
        + obs_camera % cameras
    )
    wide_count = 6 * cameras
    point_hot = (obs_point[:, None] == jnp.arange(points, dtype=jnp.int32)[None, :]).astype(
        jnp.float32
    )
    camera_hot = (column[:, None] == jnp.arange(wide_count, dtype=jnp.int32)[None, :]).astype(
        jnp.float32
    )
    cam_rows = cam_jacobian.astype(jnp.float32).reshape(2, 9, -1)
    point_rows = point_jacobian.astype(jnp.float32).reshape(2, 3, -1)
    pairs = jnp.sum(point_rows[:, :, None] * point_rows[:, None, :], 0).reshape(9, -1)
    point_blocks = sum_into(pairs, point_hot)
    point_blocks = point_blocks + DAMPING * jnp.eye(3, dtype=jnp.float32).reshape(9, 1)
    inverse = inverse_three(point_blocks)
    outer = jnp.sum(cam_rows[:, :, None] * cam_rows[:, None, :], 0).reshape(81, -1)
    gradient_terms = eliminate(residuals, cam_rows, point_rows, point_hot, inverse)
    partial_value = sum_into(jnp.concatenate([outer, gradient_terms], 0), camera_hot)
    summed = return_normal(partial_value)
    blocks = summed[:81] + DAMPING * jnp.eye(9, dtype=jnp.float32).reshape(81, 1)
    right = -summed[81:]
    factor = cholesky_rows(blocks)
    cam_step = jnp.zeros((9, cameras), jnp.float32)
    residual = right
    precon = cholesky_apply(factor, residual)
    direction = precon
    current = precon_inner(residual, precon)
    for turn in range(ITERS):
        wide = spread(direction)
        reduced_values = jnp.sum(cam_rows * pick_from(wide, camera_hot)[None], 1)
        terms = eliminate(reduced_values, cam_rows, point_rows, point_hot, inverse)
        partial_terms = sum_into(terms, camera_hot)
        product = DAMPING * direction + return_product(partial_terms)
        curvature = one_axis_at_a_time(jnp.sum(direction * product), GRP_REG)
        step_size = current / curvature
        cam_step = cam_step + step_size * direction
        if turn + 1 < ITERS:
            residual = residual - step_size * product
            precon = cholesky_apply(factor, residual)
            following = precon_inner(residual, precon)
            direction = precon + following / current * direction
            current = following
    wide_step = spread(cam_step)
    values = residuals + jnp.sum(cam_rows * pick_from(wide_step, camera_hot)[None], 1)
    gathered = sum_into(jnp.sum(point_rows * values[:, None], 0), point_hot)
    point_step = -apply_three(inverse, gathered)
    return (cam_step, point_step)


def solution(mesh):
    torus = Mesh(
        mesh.devices.reshape(mesh.shape["grp"], 4, 4, 4), ("grp", "reg_0", "reg_1", "reg_2")
    )
    return jax.shard_map(
        local,
        mesh=torus,
        in_specs=(P(None, GRP_REG), P(None, GRP_REG), P(None, GRP_REG), P(GRP_REG), P(GRP_REG)),
        out_specs=(P(None, GRP_REG), P(None, GRP_REG)),
        check_vma=False,
    )
```

profile of v0, /device:TPU:1, one launch (start us, length us, event | category | flops | bytes accessed | tf_op | source)
XLA Modules:
  0.0 341.9 jit_solution(4697323244290613533)
XLA Ops:
  10.5 4.9 %all_to_all.20 = f32[2,270,128]{2,1,0:T(8,128)S(1)} all-to-all(f32[2,270,128]{2,1,0:T(8,128)S(1)} %bitcast.22), channel_id=1, replica_groups=mesh['grp'=2,'reg_0'=4,'reg_1'=4,'reg_2'=4] {'grp'}, dimensions={0} | all-to-all | bytes 552960 | tf_op jit(solution)/shard_map/all_to_all | solution.py:37
  16.8 4.0 %collective-permute-start.1 = (f32[90,128]{1,0:T(8,128)S(1)}, f32[90,128]{1,0:T(8,128)S(1)}, u32[]{:S(2)}, u32[]{:S(2)}) collective-permute-start(f32[90,128]{1,0:T(8,128)S(1)} %get-tuple-element.113), channel_id=1, source_target_pairs={{0,1},{1,2},{2,3},{3,4},{4,5},{5,6},{6,7},{7,8},{8,9},{9,10},{10,1... | collective-permute-start | bytes 138248 | tf_op jit(solution)/shard_map/ppermute | solution.py:53
  25.3 4.0 %collective-permute-start.2 = (f32[9,256]{1,0:T(8,128)S(1)}, f32[9,256]{1,0:T(8,128)S(1)}, u32[]{:S(2)}, u32[]{:S(2)}) collective-permute-start(f32[9,256]{1,0:T(8,128)S(1)} %all_gather.12), channel_id=1, source_target_pairs={{0,1},{1,2},{2,3},{3,4},{4,5},{5,6},{6,7},{7,8},{8,9},{9,10},{10,1... | collective-permute-start | bytes 27656 | tf_op jit(solution)/shard_map/ppermute | solution.py:24
  41.0 5.2 %all_to_all.21 = f32[2,27,128]{2,1,0:T(8,128)S(1)} all-to-all(f32[2,27,128]{2,1,0:T(8,128)S(1)} %bitcast.23), channel_id=1, replica_groups=mesh['grp'=2,'reg_0'=4,'reg_1'=4,'reg_2'=4] {'grp'}, dimensions={0} | all-to-all | bytes 55296 | tf_op jit(solution)/shard_map/all_to_all | solution.py:37
  47.4 4.6 %collective-permute-start.5 = (f32[9,128]{1,0:T(8,128)S(1)}, f32[9,128]{1,0:T(8,128)S(1)}, u32[]{:S(2)}, u32[]{:S(2)}) collective-permute-start(f32[9,128]{1,0:T(8,128)S(1)} %get-tuple-element.143), channel_id=1, source_target_pairs={{0,1},{1,2},{2,3},{3,4},{4,5},{5,6},{6,7},{7,8},{8,9},{9,10},{10,1... | collective-permute-start | bytes 13832 | tf_op jit(solution)/shard_map/ppermute | solution.py:53
  53.4 3.9 %all-reduce.3 = (f32[]{:T(128)}, f32[]{:T(128)}) all-reduce(f32[]{:T(128)} %get-tuple-element.3, f32[]{:T(128)} %get-tuple-element.2), channel_id=1, replica_groups=mesh['grp'=2,'reg_0'=4,'reg_1'=4,'reg_2'=4] {'grp'}, use_global_device_ids=true, to_apply=%region_7.8 | all-reduce | flops 2 | bytes 16 | tf_op jit(solution)/shard_map/psum | solution.py:58
  57.3 32.4 %all-reduce.2 = (f32[]{:T(128)}, f32[]{:T(128)}) all-reduce(f32[]{:T(128)} %get-tuple-element.10, f32[]{:T(128)} %get-tuple-element.11), channel_id=1, replica_groups=mesh['grp'=2,'reg_0'=4,'reg_1'=4,'reg_2'=4] {'reg_0'}, use_global_device_ids=true, to_apply=%region_8.9 | all-reduce | flops 2 | bytes 16 | tf_op jit(solution)/shard_map/psum | solution.py:58
  89.7 6.6 %all-reduce.1 = (f32[]{:T(128)}, f32[]{:T(128)}) all-reduce(f32[]{:T(128)} %get-tuple-element.8, f32[]{:T(128)} %get-tuple-element.9), channel_id=1, replica_groups=mesh['grp'=2,'reg_0'=4,'reg_1'=4,'reg_2'=4] {'reg_1'}, use_global_device_ids=true, to_apply=%region_9.10 | all-reduce | flops 2 | bytes 16 | tf_op jit(solution)/shard_map/psum | solution.py:58
  96.3 6.6 %all-reduce = (f32[]{:T(128)}, f32[]{:T(128)}) all-reduce(f32[]{:T(128)} %get-tuple-element.6, f32[]{:T(128)} %get-tuple-element.7), channel_id=1, replica_groups=mesh['grp'=2,'reg_0'=4,'reg_1'=4,'reg_2'=4] {'reg_2'}, use_global_device_ids=true, to_apply=%region_10.11 | all-reduce | flops 2 | bytes 16 | tf_op jit(solution)/shard_map/psum | solution.py:58
  105.1 8.6 %psum.176 = f32[]{:T(128)} all-reduce(f32[]{:T(128)} %multiply_reduce_fusion.21), channel_id=1, replica_groups=mesh['grp'=2,'reg_0'=4,'reg_1'=4,'reg_2'=4] {'grp'}, use_global_device_ids=true, to_apply=%region_22.23 | all-reduce | flops 1 | bytes 8 | tf_op jit(solution)/shard_map/psum | solution.py:58
  113.7 6.7 %psum.177 = f32[]{:T(128)} all-reduce(f32[]{:T(128)} %psum.176), channel_id=1, replica_groups=mesh['grp'=2,'reg_0'=4,'reg_1'=4,'reg_2'=4] {'reg_0'}, use_global_device_ids=true, to_apply=%region_23.24 | all-reduce | flops 1 | bytes 8 | tf_op jit(solution)/shard_map/psum | solution.py:58
  120.4 8.3 %psum.178 = f32[]{:T(128)} all-reduce(f32[]{:T(128)} %psum.177), channel_id=1, replica_groups=mesh['grp'=2,'reg_0'=4,'reg_1'=4,'reg_2'=4] {'reg_1'}, use_global_device_ids=true, to_apply=%region_24.25 | all-reduce | flops 1 | bytes 8 | tf_op jit(solution)/shard_map/psum | solution.py:58
  128.7 8.3 %psum.179 = f32[]{:T(128)} all-reduce(f32[]{:T(128)} %psum.178), channel_id=1, replica_groups=mesh['grp'=2,'reg_0'=4,'reg_1'=4,'reg_2'=4] {'reg_2'}, use_global_device_ids=true, to_apply=%region_25.26 | all-reduce | flops 1 | bytes 8 | tf_op jit(solution)/shard_map/psum | solution.py:58
  138.4 7.5 %all_gather.13 = f32[9,256]{1,0:T(8,128)S(1)} all-gather(f32[9,128]{1,0:T(8,128)S(1)} %multiply_add_fusion.2), channel_id=1, replica_groups=mesh['grp'=2,'reg_0'=4,'reg_1'=4,'reg_2'=4] {'grp'}, dimensions={1}, use_global_device_ids=true | all-gather | bytes 13824 | tf_op jit(solution)/shard_map/all_gather | solution.py:145
  159.2 5.2 %all_to_all.22 = f32[2,27,128]{2,1,0:T(8,128)S(1)} all-to-all(f32[2,27,128]{2,1,0:T(8,128)S(1)} %bitcast.24), channel_id=1, replica_groups=mesh['grp'=2,'reg_0'=4,'reg_1'=4,'reg_2'=4] {'grp'}, dimensions={0} | all-to-all | bytes 55296 | tf_op jit(solution)/shard_map/all_to_all | solution.py:37
  165.7 4.0 %collective-permute-start.9 = (f32[9,128]{1,0:T(8,128)S(1)}, f32[9,128]{1,0:T(8,128)S(1)}, u32[]{:S(2)}, u32[]{:S(2)}) collective-permute-start(f32[9,128]{1,0:T(8,128)S(1)} %get-tuple-element.141), channel_id=1, source_target_pairs={{0,1},{1,2},{2,3},{3,4},{4,5},{5,6},{6,7},{7,8},{8,9},{9,10},{10,1... | collective-permute-start | bytes 13832 | tf_op jit(solution)/shard_map/ppermute | solution.py:53
  171.1 4.2 %psum.180 = f32[]{:T(128)} all-reduce(f32[]{:T(128)} %multiply_reduce_fusion.20), channel_id=1, replica_groups=mesh['grp'=2,'reg_0'=4,'reg_1'=4,'reg_2'=4] {'grp'}, use_global_device_ids=true, to_apply=%region_32.33 | all-reduce | flops 1 | bytes 8 | tf_op jit(solution)/shard_map/psum | solution.py:58
  175.3 23.3 %psum.181 = f32[]{:T(128)} all-reduce(f32[]{:T(128)} %psum.180), channel_id=1, replica_groups=mesh['grp'=2,'reg_0'=4,'reg_1'=4,'reg_2'=4] {'reg_0'}, use_global_device_ids=true, to_apply=%region_33.34 | all-reduce | flops 1 | bytes 8 | tf_op jit(solution)/shard_map/psum | solution.py:58
  198.5 6.6 %psum.182 = f32[]{:T(128)} all-reduce(f32[]{:T(128)} %psum.181), channel_id=1, replica_groups=mesh['grp'=2,'reg_0'=4,'reg_1'=4,'reg_2'=4] {'reg_1'}, use_global_device_ids=true, to_apply=%region_34.35 | all-reduce | flops 1 | bytes 8 | tf_op jit(solution)/shard_map/psum | solution.py:58
  205.1 6.6 %psum.183 = f32[]{:T(128)} all-reduce(f32[]{:T(128)} %psum.182), channel_id=1, replica_groups=mesh['grp'=2,'reg_0'=4,'reg_1'=4,'reg_2'=4] {'reg_2'}, use_global_device_ids=true, to_apply=%region_35.36 | all-reduce | flops 1 | bytes 8 | tf_op jit(solution)/shard_map/psum | solution.py:58
  213.9 8.6 %psum.184 = f32[]{:T(128)} all-reduce(f32[]{:T(128)} %multiply_reduce_fusion.19), channel_id=1, replica_groups=mesh['grp'=2,'reg_0'=4,'reg_1'=4,'reg_2'=4] {'grp'}, use_global_device_ids=true, to_apply=%region_37.38 | all-reduce | flops 1 | bytes 8 | tf_op jit(solution)/shard_map/psum | solution.py:58
  222.5 7.2 %psum.185 = f32[]{:T(128)} all-reduce(f32[]{:T(128)} %psum.184), channel_id=1, replica_groups=mesh['grp'=2,'reg_0'=4,'reg_1'=4,'reg_2'=4] {'reg_0'}, use_global_device_ids=true, to_apply=%region_38.39 | all-reduce | flops 1 | bytes 8 | tf_op jit(solution)/shard_map/psum | solution.py:58
  229.7 7.9 %psum.186 = f32[]{:T(128)} all-reduce(f32[]{:T(128)} %psum.185), channel_id=1, replica_groups=mesh['grp'=2,'reg_0'=4,'reg_1'=4,'reg_2'=4] {'reg_1'}, use_global_device_ids=true, to_apply=%region_39.40 | all-reduce | flops 1 | bytes 8 | tf_op jit(solution)/shard_map/psum | solution.py:58
  237.5 8.3 %psum.187 = f32[]{:T(128)} all-reduce(f32[]{:T(128)} %psum.186), channel_id=1, replica_groups=mesh['grp'=2,'reg_0'=4,'reg_1'=4,'reg_2'=4] {'reg_2'}, use_global_device_ids=true, to_apply=%region_40.41 | all-reduce | flops 1 | bytes 8 | tf_op jit(solution)/shard_map/psum | solution.py:58
  247.2 7.5 %all_gather.14 = f32[9,256]{1,0:T(8,128)S(1)} all-gather(f32[9,128]{1,0:T(8,128)S(1)} %multiply_add_fusion.1), channel_id=1, replica_groups=mesh['grp'=2,'reg_0'=4,'reg_1'=4,'reg_2'=4] {'grp'}, dimensions={1}, use_global_device_ids=true | all-gather | bytes 13824 | tf_op jit(solution)/shard_map/all_gather | solution.py:145
  268.0 5.2 %all_to_all.23 = f32[2,27,128]{2,1,0:T(8,128)S(1)} all-to-all(f32[2,27,128]{2,1,0:T(8,128)S(1)} %bitcast.25), channel_id=1, replica_groups=mesh['grp'=2,'reg_0'=4,'reg_1'=4,'reg_2'=4] {'grp'}, dimensions={0} | all-to-all | bytes 55296 | tf_op jit(solution)/shard_map/all_to_all | solution.py:37
  274.5 4.0 %collective-permute-start.13 = (f32[9,128]{1,0:T(8,128)S(1)}, f32[9,128]{1,0:T(8,128)S(1)}, u32[]{:S(2)}, u32[]{:S(2)}) collective-permute-start(f32[9,128]{1,0:T(8,128)S(1)} %get-tuple-element.139), channel_id=1, source_target_pairs={{0,1},{1,2},{2,3},{3,4},{4,5},{5,6},{6,7},{7,8},{8,9},{9,10},{10,1... | collective-permute-start | bytes 13832 | tf_op jit(solution)/shard_map/ppermute | solution.py:53
  279.9 4.2 %psum.188 = f32[]{:T(128)} all-reduce(f32[]{:T(128)} %fusion.70), channel_id=1, replica_groups=mesh['grp'=2,'reg_0'=4,'reg_1'=4,'reg_2'=4] {'grp'}, use_global_device_ids=true, to_apply=%region_47.48 | all-reduce | flops 1 | bytes 8 | tf_op jit(solution)/shard_map/psum | solution.py:58
  284.1 23.3 %psum.189 = f32[]{:T(128)} all-reduce(f32[]{:T(128)} %psum.188), channel_id=1, replica_groups=mesh['grp'=2,'reg_0'=4,'reg_1'=4,'reg_2'=4] {'reg_0'}, use_global_device_ids=true, to_apply=%region_48.49 | all-reduce | flops 1 | bytes 8 | tf_op jit(solution)/shard_map/psum | solution.py:58
  307.4 6.6 %psum.190 = f32[]{:T(128)} all-reduce(f32[]{:T(128)} %psum.189), channel_id=1, replica_groups=mesh['grp'=2,'reg_0'=4,'reg_1'=4,'reg_2'=4] {'reg_1'}, use_global_device_ids=true, to_apply=%region_49.50 | all-reduce | flops 1 | bytes 8 | tf_op jit(solution)/shard_map/psum | solution.py:58
  314.0 6.6 %psum.191 = f32[]{:T(128)} all-reduce(f32[]{:T(128)} %psum.190), channel_id=1, replica_groups=mesh['grp'=2,'reg_0'=4,'reg_1'=4,'reg_2'=4] {'reg_2'}, use_global_device_ids=true, to_apply=%region_50.51 | all-reduce | flops 1 | bytes 8 | tf_op jit(solution)/shard_map/psum | solution.py:58
  322.0 7.3 %all_gather.15 = f32[9,256]{1,0:T(8,128)S(1)} all-gather(f32[9,128]{1,0:T(8,128)S(1)} %multiply_add_fusion), channel_id=1, replica_groups=mesh['grp'=2,'reg_0'=4,'reg_1'=4,'reg_2'=4] {'grp'}, dimensions={1}, use_global_device_ids=true | all-gather | bytes 13824 | tf_op jit(solution)/shard_map/all_gather | solution.py:145
  (147 shorter events, 75.7 us)
Async XLA Ops:
  0.6 2.8 copy-start.4
  0.6 2.7 copy-start
  1.7 3.8 %copy-start.1 = (bf16[18,2048]{1,0:T(8,128)(2,1)S(1)}, bf16[18,2048]{1,0:T(8,128)(2,1)}, u32[]{:S(2)}) copy-start(bf16[18,2048]{1,0:T(8,128)(2,1)} %param.5) | copy-start | bytes 221188
  7.0 0.7 copy-start.3
  15.5 5.4 %collective-permute-start = (f32[90,128]{1,0:T(8,128)S(1)}, f32[90,128]{1,0:T(8,128)S(1)}, u32[]{:S(2)}, u32[]{:S(2)}) collective-permute-start(f32[90,128]{1,0:T(8,128)S(1)} %get-tuple-element.112), channel_id=1, source_target_pairs={{1,0},{2,1},{3,2},{4,3},{5,4},{6,5},{7,6},{8,7},{9,8},{10,9},{11,1... | collective-permute-start | bytes 138248 | tf_op jit(solution)/shard_map/ppermute | solution.py:53
  16.8 5.2 %collective-permute-start.1 = (f32[90,128]{1,0:T(8,128)S(1)}, f32[90,128]{1,0:T(8,128)S(1)}, u32[]{:S(2)}, u32[]{:S(2)}) collective-permute-start(f32[90,128]{1,0:T(8,128)S(1)} %get-tuple-element.113), channel_id=1, source_target_pairs={{0,1},{1,2},{2,3},{3,4},{4,5},{5,6},{6,7},{7,8},{8,9},{9,10},{10,1... | collective-permute-start | bytes 138248 | tf_op jit(solution)/shard_map/ppermute | solution.py:53
  25.3 5.4 %collective-permute-start.2 = (f32[9,256]{1,0:T(8,128)S(1)}, f32[9,256]{1,0:T(8,128)S(1)}, u32[]{:S(2)}, u32[]{:S(2)}) collective-permute-start(f32[9,256]{1,0:T(8,128)S(1)} %all_gather.12), channel_id=1, source_target_pairs={{0,1},{1,2},{2,3},{3,4},{4,5},{5,6},{6,7},{7,8},{8,9},{9,10},{10,1... | collective-permute-start | bytes 27656 | tf_op jit(solution)/shard_map/ppermute | solution.py:24
  29.3 4.5 %collective-permute-start.3 = (f32[9,256]{1,0:T(8,128)S(1)}, f32[9,256]{1,0:T(8,128)S(1)}, u32[]{:S(2)}, u32[]{:S(2)}) collective-permute-start(f32[9,256]{1,0:T(8,128)S(1)} %all_gather.12), channel_id=1, source_target_pairs={{1,0},{2,1},{3,2},{4,3},{5,4},{6,5},{7,6},{8,7},{9,8},{10,9},{11,1... | collective-permute-start | bytes 27656 | tf_op jit(solution)/shard_map/ppermute | solution.py:25
  46.1 5.9 %collective-permute-start.4 = (f32[9,128]{1,0:T(8,128)S(1)}, f32[9,128]{1,0:T(8,128)S(1)}, u32[]{:S(2)}, u32[]{:S(2)}) collective-permute-start(f32[9,128]{1,0:T(8,128)S(1)} %get-tuple-element.142), channel_id=1, source_target_pairs={{1,0},{2,1},{3,2},{4,3},{5,4},{6,5},{7,6},{8,7},{9,8},{10,9},{11,1... | collective-permute-start | bytes 13832 | tf_op jit(solution)/shard_map/ppermute | solution.py:53
  47.4 5.3 %collective-permute-start.5 = (f32[9,128]{1,0:T(8,128)S(1)}, f32[9,128]{1,0:T(8,128)S(1)}, u32[]{:S(2)}, u32[]{:S(2)}) collective-permute-start(f32[9,128]{1,0:T(8,128)S(1)} %get-tuple-element.143), channel_id=1, source_target_pairs={{0,1},{1,2},{2,3},{3,4},{4,5},{5,6},{6,7},{7,8},{8,9},{9,10},{10,1... | collective-permute-start | bytes 13832 | tf_op jit(solution)/shard_map/ppermute | solution.py:53
  145.9 3.2 collective-permute-start.6
  147.5 4.5 %collective-permute-start.7 = (f32[9,256]{1,0:T(8,128)S(1)}, f32[9,256]{1,0:T(8,128)S(1)}, u32[]{:S(2)}, u32[]{:S(2)}) collective-permute-start(f32[9,256]{1,0:T(8,128)S(1)} %all_gather.13), channel_id=1, source_target_pairs={{1,0},{2,1},{3,2},{4,3},{5,4},{6,5},{7,6},{8,7},{9,8},{10,9},{11,1... | collective-permute-start | bytes 27656 | tf_op jit(solution)/shard_map/ppermute | solution.py:25
  164.4 5.3 %collective-permute-start.8 = (f32[9,128]{1,0:T(8,128)S(1)}, f32[9,128]{1,0:T(8,128)S(1)}, u32[]{:S(2)}, u32[]{:S(2)}) collective-permute-start(f32[9,128]{1,0:T(8,128)S(1)} %get-tuple-element.140), channel_id=1, source_target_pairs={{1,0},{2,1},{3,2},{4,3},{5,4},{6,5},{7,6},{8,7},{9,8},{10,9},{11,1... | collective-permute-start | bytes 13832 | tf_op jit(solution)/shard_map/ppermute | solution.py:53
  165.7 4.8 %collective-permute-start.9 = (f32[9,128]{1,0:T(8,128)S(1)}, f32[9,128]{1,0:T(8,128)S(1)}, u32[]{:S(2)}, u32[]{:S(2)}) collective-permute-start(f32[9,128]{1,0:T(8,128)S(1)} %get-tuple-element.141), channel_id=1, source_target_pairs={{0,1},{1,2},{2,3},{3,4},{4,5},{5,6},{6,7},{7,8},{8,9},{9,10},{10,1... | collective-permute-start | bytes 13832 | tf_op jit(solution)/shard_map/ppermute | solution.py:53
  254.7 3.2 collective-permute-start.10
  256.3 4.5 %collective-permute-start.11 = (f32[9,256]{1,0:T(8,128)S(1)}, f32[9,256]{1,0:T(8,128)S(1)}, u32[]{:S(2)}, u32[]{:S(2)}) collective-permute-start(f32[9,256]{1,0:T(8,128)S(1)} %all_gather.14), channel_id=1, source_target_pairs={{1,0},{2,1},{3,2},{4,3},{5,4},{6,5},{7,6},{8,7},{9,8},{10,9},{11,1... | collective-permute-start | bytes 27656 | tf_op jit(solution)/shard_map/ppermute | solution.py:25
  273.2 5.3 %collective-permute-start.12 = (f32[9,128]{1,0:T(8,128)S(1)}, f32[9,128]{1,0:T(8,128)S(1)}, u32[]{:S(2)}, u32[]{:S(2)}) collective-permute-start(f32[9,128]{1,0:T(8,128)S(1)} %get-tuple-element.138), channel_id=1, source_target_pairs={{1,0},{2,1},{3,2},{4,3},{5,4},{6,5},{7,6},{8,7},{9,8},{10,9},{11,1... | collective-permute-start | bytes 13832 | tf_op jit(solution)/shard_map/ppermute | solution.py:53
  274.5 4.8 %collective-permute-start.13 = (f32[9,128]{1,0:T(8,128)S(1)}, f32[9,128]{1,0:T(8,128)S(1)}, u32[]{:S(2)}, u32[]{:S(2)}) collective-permute-start(f32[9,128]{1,0:T(8,128)S(1)} %get-tuple-element.139), channel_id=1, source_target_pairs={{0,1},{1,2},{2,3},{3,4},{4,5},{5,6},{6,7},{7,8},{8,9},{9,10},{10,1... | collective-permute-start | bytes 13832 | tf_op jit(solution)/shard_map/ppermute | solution.py:53
  321.9 19.3 %copy-start.2 = (f32[9,128]{1,0:T(8,128)}, f32[9,128]{1,0:T(8,128)S(1)}, u32[]{:S(2)}) copy-start(f32[9,128]{1,0:T(8,128)S(1)} %multiply_add_fusion) | copy-start | bytes 13828
  329.3 4.9 %collective-permute-start.14 = (f32[9,256]{1,0:T(8,128)S(1)}, f32[9,256]{1,0:T(8,128)S(1)}, u32[]{:S(2)}, u32[]{:S(2)}) collective-permute-start(f32[9,256]{1,0:T(8,128)S(1)} %all_gather.15), channel_id=1, source_target_pairs={{0,1},{1,2},{2,3},{3,4},{4,5},{5,6},{6,7},{7,8},{8,9},{9,10},{10,1... | collective-permute-start | bytes 27656 | tf_op jit(solution)/shard_map/ppermute | solution.py:24
  332.9 4.5 %collective-permute-start.15 = (f32[9,256]{1,0:T(8,128)S(1)}, f32[9,256]{1,0:T(8,128)S(1)}, u32[]{:S(2)}, u32[]{:S(2)}) collective-permute-start(f32[9,256]{1,0:T(8,128)S(1)} %all_gather.15), channel_id=1, source_target_pairs={{1,0},{2,1},{3,2},{4,3},{5,4},{6,5},{7,6},{8,7},{9,8},{10,9},{11,1... | collective-permute-start | bytes 27656 | tf_op jit(solution)/shard_map/ppermute | solution.py:25
where the time goes:
time: 346 us; the launch traced here: 342 us
  blocking collectives  241 us (70%)
  starting transfers between devices  38.3 us (11%)
  matrix products  30.1 us (9%)
  waiting for transfers between devices  15.4 us (4%)
  between operations  8.08 us (2%)
  other arithmetic  7.05 us (2%)
    psum x20, blocking collectives, one_axis_at_a_time(): x = lax.psum(x, axis)  195 us
    all_gather x4, blocking collectives, spread(): both_groups = lax.all_gather(field, 'grp', axis=1, tiled=True)  25.3 us
    ppermute x8, starting transfers between devices, from_behind(): lax.ppermute(value, axis, [(source, source + steps) for source in range(i...  21.7 us
    all_to_all x4, blocking collectives, sum_at_owner(): tiles = lax.all_to_all(in_blocks(x, dim, peers), axis, 0, 0, tiled=True)  20.5 us
    dot_general x8, matrix products, pick_from(): lax.dot_general(field, onehot, (((1,), (1,)), ((), ())), preferred_elemen...  15.8 us
    dot_general x10, matrix products, sum_into(): jnp.dot(terms, onehot, preferred_element_type=jnp.float32, precision=lax....  14.3 us
    ppermute x4, waiting for transfers between devices, padded(): after = lax.ppermute(initial, axis, down)  12 us
    ppermute x4, starting transfers between devices, padded(): before = lax.ppermute(last, axis, up)  10.8 us
  transfers between devices with their start and end apart: 16, of which 8 were waited for; matrix products, arithmetic and copies ran while one was open for 0% of the time, Pallas kernels for 0%

commit v1 on v0

v1 whole, which is shorter than its diff:
```python
import functools

import jax
import jax.numpy as jnp
from jax import lax
from jax.experimental import pallas as pl
from jax.experimental.pallas import tpu as pltpu
from jax.sharding import Mesh
from jax.sharding import PartitionSpec as P

C_DEV = 128
P_DEV = 256
OBS = 2048
DAMPING = 4.0
WIDE = 2 * C_DEV
REG = ("reg_0", "reg_1", "reg_2")
GRP_REG = ("grp", "reg_0", "reg_1", "reg_2")
F32 = jnp.float32
BF16 = jnp.bfloat16
VMEM = pl.BlockSpec(memory_space=pltpu.VMEM)
SMEM = pl.BlockSpec(memory_space=pltpu.SMEM)


def three_parts(x):
    high = x.astype(BF16)
    rest = x - high.astype(F32)
    middle = rest.astype(BF16)
    low = (rest - middle.astype(F32)).astype(BF16)
    return high, middle, low


def stacked(x):
    high, middle, low = three_parts(x)
    parts = [high.astype(F32), middle.astype(F32), low.astype(F32)]
    return jnp.concatenate(parts, 0).astype(BF16)


def folded(x):
    rows = x.shape[0] // 3
    return x[:rows] + x[rows : 2 * rows] + x[2 * rows :]


def pick(field, onehot):
    return lax.dot_general(
        field, onehot, (((1,), (0,)), ((), ())), preferred_element_type=F32
    )


def put(terms, onehot):
    return lax.dot_general(
        terms, onehot, (((1,), (1,)), ((), ())), preferred_element_type=F32
    )


def onehot_of(index):
    ids = lax.broadcasted_iota(jnp.int32, (WIDE, index.shape[1]), 0)
    return jnp.where(ids == index, 1.0, 0.0).astype(BF16)


def total(x):
    return jnp.sum(jnp.sum(x, 0, keepdims=True), 1, keepdims=True)


def per_lane(x):
    row = jnp.sum(x, 0, keepdims=True)
    return functools.reduce(
        lambda a, b: a + b, [row[:, k : k + 128] for k in range(0, row.shape[1], 128)]
    )


def solve_points(vinv, g):
    a, b, c, d, e, f = [vinv[k : k + 1] for k in range(6)]
    x, y, z = [g[k : k + 1] for k in range(3)]
    rows = [a * x + b * y + c * z, b * x + d * y + e * z, c * x + e * y + f * z]
    return rows + [jnp.zeros((8 - 3, g.shape[1]), F32)]


def point_part(u, p, hot_p, vinv):
    g = folded(put(stacked(p[0] * u[0] + p[1] * u[1]), hot_p))
    s = jnp.concatenate(solve_points(vinv, g), 0)
    back = folded(pick(stacked(s), hot_p))
    return g, s, [jnp.sum(p[i] * back, 0, keepdims=True) for i in range(2)]


def first_kernel(cam, pnt, res, index, part, jx, px, vinv_out, gres_out):
    low, block, slot = index[0:1, :], index[1:2, :], index[2:3, :]
    hot_p = onehot_of(slot)
    camf = cam[...].astype(F32)
    pf = pnt[...].astype(F32)
    zero5 = jnp.zeros((5, OBS), F32)
    zero7 = jnp.zeros((7, OBS), F32)
    for i in range(2):
        jx[i, 0:8, :] = camf[9 * i : 9 * i + 8]
        jx[i, 8:16, :] = jnp.concatenate([camf[9 * i + 8 : 9 * i + 9], zero7], 0)
        px[i] = jnp.concatenate([pf[3 * i : 3 * i + 3], zero5], 0)
    p = [px[0], px[1]]
    a = [jx[0, 0:8, :], jx[1, 0:8, :]]
    last = [jx[0, 8:9, :], jx[1, 8:9, :]]
    r = [res[0:1, :], res[1:2, :]]
    row = lax.broadcasted_iota(jnp.int32, (8, OBS), 0)
    squares = p[0] * p[0] + p[1] * p[1]
    turned = [
        jnp.where(row == 2, jnp.broadcast_to(x[0:1], x.shape), pltpu.roll(x, 7, 0)) for x in p
    ]
    products = p[0] * turned[0] + p[1] * turned[1]
    right = p[0] * r[0] + p[1] * r[1]
    sums = folded(put(stacked(jnp.concatenate([squares, products, right], 0)), hot_p))
    v00, v11, v22 = [sums[k : k + 1] + DAMPING for k in range(3)]
    v01, v12, v02 = [sums[8 + k : 9 + k] for k in range(3)]
    g = sums[16:24]
    c00 = v11 * v22 - v12 * v12
    c01 = v02 * v12 - v01 * v22
    c02 = v01 * v12 - v02 * v11
    c11 = v00 * v22 - v02 * v02
    c12 = v01 * v02 - v00 * v12
    c22 = v00 * v11 - v01 * v01
    scale = 1.0 / (v00 * c00 + v01 * c01 + v02 * c02)
    cofactors = jnp.concatenate(
        [c00, c01, c02, c11, c12, c22, jnp.zeros((2, P_DEV), F32)], 0
    )
    vinv = cofactors * scale
    vinv_out[...] = vinv
    gres_out[...] = g
    s = jnp.concatenate(solve_points(vinv, g), 0)
    back = folded(pick(stacked(s), hot_p))
    rem = [r[i] - jnp.sum(p[i] * back, 0, keepdims=True) for i in range(2)]
    tiles = []
    for d in range(5):
        other = [x if d == 0 else pltpu.roll(x, d, 0) for x in a]
        tiles.append(a[0] * other[0] + a[1] * other[1])
    tiles.append(a[0] * last[0] + a[1] * last[1])
    tiles.append(a[0] * rem[0] + a[1] * rem[1])
    corner = last[0] * last[0] + last[1] * last[1]
    end = last[0] * rem[0] + last[1] * rem[1]
    tiles.append(jnp.where(row == 0, corner, jnp.where(row == 1, end, 0.0)))
    terms = stacked(jnp.concatenate(tiles, 0))
    hot_c = onehot_of(low)
    for k in range(3):
        mask = jnp.where(block == k, 1.0, 0.0).astype(BF16)
        part[k] = folded(put(terms * mask, hot_c))


def factor_kernel(mid, mid_other, got, got_other, factor, v, scal):
    sums = (mid[...] + mid_other[...]) + (got[...] + got_other[...])

    def entry(i, j):
        if i == 8 and j == 8:
            k = 56
        elif i == 8:
            k = 40 + j
        elif i - j <= 4:
            k = 8 * (i - j) + i
        else:
            k = 8 * (8 - (i - j)) + j
        x = sums[k : k + 1]
        return x + DAMPING if i == j else x

    b = [-sums[48 + k : 49 + k] for k in range(8)] + [-sums[57:58]]
    low = [[None] * 9 for _ in range(9)]
    work = [[entry(i, j) if j <= i else None for j in range(9)] for i in range(9)]
    inv = []
    for k in range(9):
        inv.append(1.0 / jnp.sqrt(work[k][k]))
        for i in range(k + 1, 9):
            low[i][k] = work[i][k] * inv[k]
        for i in range(k + 1, 9):
            for j in range(k + 1, i + 1):
                work[i][j] = work[i][j] - low[i][k] * low[j][k]
    rows = [low[i][j] for i in range(9) for j in range(i)] + inv
    rows.append(jnp.zeros((3, WIDE), F32))
    factor[...] = jnp.concatenate(rows, 0)
    x = solve_camera(low, inv, b)
    v[...] = jnp.concatenate(x + [jnp.zeros((7, WIDE), F32)], 0)
    dots = functools.reduce(lambda p, q: p + q, [b[k] * x[k] for k in range(9)])
    scal[...] = jnp.broadcast_to(0.5 * per_lane(dots), (8, 128))


def solve_camera(low, inv, b):
    y = list(b)
    for k in range(9):
        y[k] = y[k] * inv[k]
        for i in range(k + 1, 9):
            y[i] = y[i] - low[i][k] * y[k]
    for k in range(8, -1, -1):
        y[k] = y[k] * inv[k]
        for i in range(k):
            y[i] = y[i] - low[k][i] * y[k]
    return y


def solve_kernel(mid, mid_other, got, got_other, factor, v):
    sums = (mid[...] + mid_other[...]) + (got[...] + got_other[...])
    low = [[None] * 9 for _ in range(9)]
    at = 0
    for i in range(9):
        for j in range(i):
            low[i][j] = factor[at : at + 1, :]
            at += 1
    inv = [factor[at + k : at + k + 1, :] for k in range(9)]
    x = solve_camera(low, inv, [sums[k : k + 1] for k in range(9)])
    v[...] = jnp.concatenate(x + [jnp.zeros((7, WIDE), F32)], 0)


def apply_body(grp, v, got, got_other, index, jx, px, vinv):
    low, block, slot = index[0:1, :], index[1:2, :], index[2:3, :]
    hot_c = onehot_of(low)
    hot_p = onehot_of(slot)
    first = grp[0] == 0
    here = v[...]
    up = jnp.where(first, got[...], got_other[...])
    down = jnp.where(first, got_other[...], got[...])
    fields = jnp.concatenate([stacked(x) for x in (down, here, up)], 0)
    picked = pick(fields, hot_c)
    blocks = [folded(picked[48 * k : 48 * k + 48]) for k in range(3)]
    field = jnp.where(block == 0, blocks[0], jnp.where(block == 1, blocks[1], blocks[2]))
    u = [jnp.sum(jx[i] * field, 0, keepdims=True) for i in range(2)]
    p = [px[0], px[1]]
    g, s, ps = point_part(u, p, hot_p, vinv[...])
    return block, hot_c, u, g, s, ps


def apply_kernel(
    grp, v, got, got_other, index, jx, px, vinv, v_old, s_old, rem_old,
    part, g_out, s_out, rem_out, scal,
):
    block, hot_c, u, g, s, ps = apply_body(grp, v, got, got_other, index, jx, px, vinv)
    rem = [u[i] - ps[i] for i in range(2)]
    g_out[...] = g
    s_out[...] = s
    rem_out[...] = jnp.concatenate(rem + [jnp.zeros((6, OBS), F32)], 0)
    terms = stacked(jx[0] * ps[0] + jx[1] * ps[1])
    lhs = jnp.concatenate(
        [terms * jnp.where(block == k, 1.0, 0.0).astype(BF16) for k in range(3)], 0
    )
    out = put(lhs, hot_c)
    for k in range(3):
        part[k] = folded(out[48 * k : 48 * k + 48])
    scal[...] = scalars(v[...], v_old[...], u, rem, rem_old, g, s, s_old[...])


def scalars(v, v_old, u, rem, rem_old, g, s, s_old):
    half = 0.5 * DAMPING
    rows = [
        half * per_lane(v * v_old) + per_lane(u[0] * rem_old[0:1, :] + u[1] * rem_old[1:2, :]),
        half * per_lane(v * v) + per_lane(u[0] * rem[0] + u[1] * rem[1]),
        per_lane(g * s_old),
        per_lane(g * s),
        jnp.zeros((4, 128), F32),
    ]
    return jnp.concatenate(rows, 0)


def last_apply_kernel(
    grp, v, got, got_other, index, jx, px, vinv, v_old, s_old, rem_old, scal0, scal1, scal2,
    g_out, send,
):
    block, hot_c, u, g, s, ps = apply_body(grp, v, got, got_other, index, jx, px, vinv)
    rem = [u[i] - ps[i] for i in range(2)]
    g_out[...] = g
    scal3 = scalars(v[...], v_old[...], u, rem, rem_old, g, s, s_old[...])
    rows = jnp.concatenate([scal0[...], scal1[...], scal2[...], scal3], 0)
    ones = jnp.ones((128, 128), BF16)
    high, middle, low = three_parts(rows)
    send[...] = put(ones, high) + put(ones, middle) + put(ones, low)


def final_kernel(grp, back, v0, v1, v2, g0, g1, g2, gres, vinv, cam, pnt):
    sums = jnp.sum(back[...], 0, keepdims=True)

    def value(k):
        return sums[:, k : k + 1]

    m = [value(0), value(11), value(18), value(19), value(26)]
    s = [value(9), value(16), value(17), value(24), value(25)]

    def form(h, x):
        out = None
        for i in range(3):
            for j in range(3):
                term = x[i] * x[j] * h[i + j]
                out = term if out is None else out + term
        return out

    def ratio(x, y):
        return jnp.where(y > 0, x / jnp.where(y > 0, y, 1.0), 0.0)

    one, zero = jnp.ones((1, 1), F32), jnp.zeros((1, 1), F32)
    y = [zero, zero, zero]
    z = [one, zero, zero]
    d = list(z)
    current = m[0]
    for turn in range(3):
        step = ratio(current, form(s, d))
        y = [y[k] + step * d[k] for k in range(3)]
        if turn < 2:
            image = [d[0], d[1] - d[0], d[2] - d[1]]
            z = [z[k] - step * image[k] for k in range(3)]
            following = form(m, z)
            beta = ratio(following, current)
            d = [z[k] + beta * d[k] for k in range(3)]
            current = following
    x = y[0] * v0[...] + y[1] * v1[...] + y[2] * v2[...]
    cam[...] = jnp.where(grp[0] == 0, x[0:9, 0:C_DEV], x[0:9, C_DEV:WIDE])
    g = gres[...] + (y[0] * g0[...] + y[1] * g1[...] + y[2] * g2[...])
    rows = solve_points(vinv[...], g)
    for k in range(3):
        pnt[k : k + 1, :] = -rows[k]


def shape(*dims, dtype=F32):
    return jax.ShapeDtypeStruct(dims, dtype)


def call(kernel, outs, *args, scalar=False):
    specs = [VMEM] * len(args)
    if scalar:
        specs[0] = SMEM
    many = isinstance(outs, (tuple, list))
    return pl.pallas_call(
        kernel,
        out_shape=outs,
        in_specs=specs,
        out_specs=[VMEM] * len(outs) if many else VMEM,
        name=kernel.__name__,
    )(*args)


def local(regions, cam_jacobian, point_jacobian, residuals, obs_camera, obs_point):
    region = lax.axis_index(REG)
    group = lax.axis_index("grp")
    grp = group.reshape(1).astype(jnp.int32)
    owners = obs_camera // C_DEV
    low = owners // regions * C_DEV + obs_camera % C_DEV
    block = owners % regions - region + 1
    index = jnp.stack([low, block, obs_point] + [jnp.zeros_like(low)] * 5)

    partner = [(g * regions + r, (1 - g) * regions + r) for g in range(2) for r in range(regions)]
    up = [(r, regions + r + 1) for r in range(regions - 1)]
    cross = up + [(b, a) for a, b in up]

    def other(x):
        return lax.ppermute(x, GRP_REG, partner)

    def across(x):
        return lax.ppermute(x, GRP_REG, cross)

    def to_owner(part):
        theirs = other(part)
        outgoing = jnp.where(group == 0, part[2] + theirs[2], part[0] + theirs[0])
        got = across(outgoing)
        return part[1], theirs[1], got, other(got)

    def spread(v):
        got = across(v)
        return got, other(got)

    rows = 64
    part, jx, px, vinv, gres = call(
        first_kernel,
        [shape(3, rows, WIDE), shape(2, 16, OBS), shape(2, 8, OBS), shape(8, P_DEV), shape(8, P_DEV)],
        cam_jacobian, point_jacobian, residuals, index,
    )
    factor, v0, scal0 = call(
        factor_kernel, [shape(48, WIDE), shape(16, WIDE), shape(8, 128)], *to_owner(part)
    )
    outs = [shape(3, 16, WIDE), shape(8, P_DEV), shape(8, P_DEV), shape(8, OBS), shape(8, 128)]
    common = (index, jx, px, vinv)
    part, g0, s0, rem0, scal1 = call(
        apply_kernel, outs, grp, v0, *spread(v0), *common, v0, gres, residuals, scalar=True
    )
    v1 = call(solve_kernel, shape(16, WIDE), *to_owner(part), factor)
    part, g1, s1, rem1, scal2 = call(
        apply_kernel, outs, grp, v1, *spread(v1), *common, v0, s0, rem0, scalar=True
    )
    v2 = call(solve_kernel, shape(16, WIDE), *to_owner(part), factor)
    g2, send = call(
        last_apply_kernel,
        [shape(8, P_DEV), shape(128, 32)],
        grp, v2, *spread(v2), *common, v1, s1, rem1, scal0, scal1, scal2, scalar=True,
    )
    back = lax.all_to_all(send, GRP_REG, 0, 0, tiled=True)
    cam, pnt = call(
        final_kernel,
        [shape(9, C_DEV), shape(3, P_DEV)],
        grp, back, v0, v1, v2, g0, g1, g2, gres, vinv, scalar=True,
    )
    return cam, pnt


def solution(mesh):
    torus = Mesh(
        mesh.devices.reshape(mesh.shape["grp"], 4, 4, 4), ("grp", "reg_0", "reg_1", "reg_2")
    )
    return jax.shard_map(
        functools.partial(local, mesh.shape["reg"]),
        mesh=torus,
        in_specs=(P(None, GRP_REG), P(None, GRP_REG), P(None, GRP_REG), P(GRP_REG), P(GRP_REG)),
        out_specs=(P(None, GRP_REG), P(None, GRP_REG)),
        check_vma=False,
    )
```

time: 346 us -> 122 us (0.35)
  blocking collectives: 241 us -> 39.9 us
  matrix products: 30.1 us -> 0 us
  Pallas kernels: 0 us -> 21.3 us
  between operations: 8.08 us -> 0.84 us
  waiting for transfers between devices: 15.4 us -> 8.59 us
    psum x20 -> x0, blocking collectives: 195 us -> none  [one_axis_at_a_time(): x = lax.psum(x, axis)]
    dot_general x18 -> x0, matrix products: 30.1 us -> none  [the longest x8 15.8 us: pick_from(): lax.dot_general(field, onehot, (((1,), (1,)), ((), ())), preferred_elemen...]
    all_gather x4 -> x0, blocking collectives: 25.3 us -> none  [spread(): both_groups = lax.all_gather(field, 'grp', axis=1, tiled=True)]
    pallas_call x0 -> x8, Pallas kernels: none -> 21.3 us  [call(): pl.pallas_call(kernel, out_shape=outs, in_specs=specs, out_specs=[VMEM] *...]
    all_to_all x4 -> x1, blocking collectives: 20.5 us -> 39.9 us  [local(): back = lax.all_to_all(send, GRP_REG, 0, 0, tiled=True)]
    ppermute x16 -> x15, waiting for transfers between devices: 15.4 us -> 8.59 us  [the longest x9 8.57 us: other(): return lax.ppermute(x, GRP_REG, partner)]
    reduce_sum x28 -> x0, other arithmetic: 5.41 us -> none  [the longest x3 1.82 us: local(): curvature = one_axis_at_a_time(jnp.sum(direction * product), GRP_REG)]
    unnamed x10 -> x28, local copies, waits for them, and re-layouts: 0.61 us -> 5.02 us
  transfers between devices with their start and end apart: 16 -> 15, of which waited for: 8 -> 9; matrix products, arithmetic and copies ran while one was open for 0% -> 0% of each run, Pallas kernels for 0% -> 0%
where the time goes in v1:
time: 122 us; the launch traced here: 121 us
  starting transfers between devices  40.5 us (33%)
  blocking collectives  39.9 us (33%)
  Pallas kernels  21.3 us (17%)
  waiting for transfers between devices  8.59 us (7%)
  local copies, waits for them, and re-layouts  5.71 us (5%)
  other arithmetic  4.34 us (4%)
    all_to_all x1, blocking collectives, local(): back = lax.all_to_all(send, GRP_REG, 0, 0, tiled=True)  39.9 us
    ppermute x9, starting transfers between devices, other(): return lax.ppermute(x, GRP_REG, partner)  36.6 us
    pallas_call x8, Pallas kernels, call(): pl.pallas_call(kernel, out_shape=outs, in_specs=specs, out_specs=[VMEM] *...  21.3 us
    ppermute x9, waiting for transfers between devices, other(): return lax.ppermute(x, GRP_REG, partner)  8.57 us
    unnamed x28, local copies, waits for them, and re-layouts  5.02 us
    select_n x3, other arithmetic, to_owner(): outgoing = jnp.where(group == 0, part[2] + theirs[2], part[0] + theirs[0])  4.31 us
    ppermute x6, starting transfers between devices, across(): return lax.ppermute(x, GRP_REG, cross)  3.9 us
  transfers between devices with their start and end apart: 15, of which 9 were waited for; matrix products, arithmetic and copies ran while one was open for 0% of the time, Pallas kernels for 0%

profile of v1, /device:TPU:1, one launch (start us, length us, event | category | flops | bytes accessed | tf_op | source)
XLA Modules:
  0.0 121.2 jit_solution(1857331282556290425)
XLA Ops:
  0.6 0.7 copy-done.12
  1.4 0.7 copy-done.13
  2.1 0.7 stack.19.index
  2.8 3.8 %first_kernel.1 = (f32[3,64,256]{2,1,0:T(8,128)}, f32[2,16,2048]{2,1,0:T(8,128)}, f32[2,8,2048]{2,1,0:T(8,128)}, f32[8,256]{1,0:T(8,128)}, f32[8,256]{1,0:T(8,128)}) custom-call(bf16[18,2048]{1,0:T(8,128)(2,1)} %cam.1, bf16[6,2048]{1,0:T(8,128)(2,1)} %pnt.1, f32[2,2048]{1,0:T(2,128)} %rem_old.1, s32[8,2048]{1,0:T(8,128)} %stack.19.index), custom_call_target="tpu_custom_call" | custom-call | tf_op jit(solution)/shard_map/first_kernel/pallas_call | solution.py:319
  6.6 1.4 %collective-permute-start = (f32[3,64,256]{2,1,0:T(8,128)}, f32[3,64,256]{2,1,0:T(8,128)S(1)}, u32[]{:S(2)}, u32[]{:S(2)}) collective-permute-start(f32[3,64,256]{2,1,0:T(8,128)} %get-tuple-element.22), channel_id=1, source_target_pairs={{0,64},{1,65},{2,66},{3,67},{4,68},{5,69},{6,70},{7,71},{8,72},{9,... | collective-permute-start | bytes 589832 | tf_op jit(solution)/shard_map/ppermute | solution.py:342
  7.9 1.3 %collective-permute-done = f32[3,64,256]{2,1,0:T(8,128)S(1)} collective-permute-done((f32[3,64,256]{2,1,0:T(8,128)}, f32[3,64,256]{2,1,0:T(8,128)S(1)}, u32[]{:S(2)}, u32[]{:S(2)}) %collective-permute-start) | collective-permute-done | bytes 196640 | tf_op jit(solution)/shard_map/ppermute | solution.py:342
  9.2 1.6 %fusion.1 = (f32[64,256]{1,0:T(8,128)S(1)}, f32[64,256]{1,0:T(8,128)}, f32[64,256]{1,0:T(8,128)}) fusion(f32[3,64,256]{2,1,0:T(8,128)S(1)} %collective-permute-done, f32[3,64,256]{2,1,0:T(8,128)} %get-tuple-element.22, pred[]{:T(512)S(6)} %eq.8), kind=kLoop, calls=%fused_computation.2 | loop fusion | flops 49152 | bytes 589825 | tf_op jit(solution)/shard_map/jit(_where)/select_n | solution.py:349
  10.8 0.7 collective-permute-start.1
  11.5 5.3 %collective-permute-start.2 = (f32[64,256]{1,0:T(8,128)S(1)}, f32[64,256]{1,0:T(8,128)S(1)}, u32[]{:S(2)}, u32[]{:S(2)}) collective-permute-start(f32[64,256]{1,0:T(8,128)S(1)} %collective-permute-done.1.got), channel_id=1, source_target_pairs={{0,64},{1,65},{2,66},{3,67},{4,68},{5,69},{6,70},{7,71},{8,72},{9,... | collective-permute-start | bytes 196616 | tf_op jit(solution)/shard_map/ppermute | solution.py:342
  16.7 0.9 collective-permute-done.2.got_other
  18.3 1.8 %factor_kernel.1 = (f32[48,256]{1,0:T(8,128)}, f32[16,256]{1,0:T(8,128)}, f32[8,128]{1,0:T(8,128)}) custom-call(f32[64,256]{1,0:T(8,128)} %get-tuple-element.43.mid, f32[64,256]{1,0:T(8,128)} %get-tuple-element.44.mid_other, f32[64,256]{1,0:T(8,128)} %copy-done, f32[64,256]{1,0:T(8,128)} %copy-done.1), custom_call_target="tpu_custom_call" | custom-call | tf_op jit(solution)/shard_map/factor_kernel/pallas_call | solution.py:319
  20.8 4.9 %collective-permute-start.4 = (f32[16,256]{1,0:T(8,128)S(1)}, f32[16,256]{1,0:T(8,128)S(1)}, u32[]{:S(2)}, u32[]{:S(2)}) collective-permute-start(f32[16,256]{1,0:T(8,128)S(1)} %collective-permute-done.3.got), channel_id=1, source_target_pairs={{0,64},{1,65},{2,66},{3,67},{4,68},{5,69},{6,70},{7,71},{8,72},{9,... | collective-permute-start | bytes 49160 | tf_op jit(solution)/shard_map/ppermute | solution.py:342
  25.7 0.8 collective-permute-done.4.got_other
  27.2 3.6 %apply_kernel.2 = (f32[3,16,256]{2,1,0:T(8,128)}, f32[8,256]{1,0:T(8,128)}, f32[8,256]{1,0:T(8,128)}, f32[8,2048]{1,0:T(8,128)}, f32[8,128]{1,0:T(8,128)}) custom-call(s32[1]{0:T(128)} %bitcast.grp, f32[16,256]{1,0:T(8,128)} %get-tuple-element.23.v.v_old.v0, f32[16,256]{1,0:T(8,128)} %copy-done.4, f32[16,256]{1,0:T(8,128)} %copy-done.7, ...), custom_call_target="tpu_custom_call" | custom-call | tf_op jit(solution)/shard_map/apply_kernel/pallas_call | solution.py:319
  31.1 1.1 collective-permute-done.5
  32.2 1.4 %fusion.5 = (f32[16,256]{1,0:T(8,128)S(1)}, f32[16,256]{1,0:T(8,128)}, f32[16,256]{1,0:T(8,128)}) fusion(f32[3,16,256]{2,1,0:T(8,128)S(1)} %collective-permute-done.5, f32[3,16,256]{2,1,0:T(8,128)} %get-tuple-element.28, pred[]{:T(512)S(6)} %eq.8), kind=kLoop, calls=%fused_computation.13 | loop fusion | flops 12288 | bytes 147457 | tf_op jit(solution)/shard_map/jit(_where)/select_n | solution.py:349
  34.2 4.7 %collective-permute-start.7 = (f32[16,256]{1,0:T(8,128)S(1)}, f32[16,256]{1,0:T(8,128)S(1)}, u32[]{:S(2)}, u32[]{:S(2)}) collective-permute-start(f32[16,256]{1,0:T(8,128)S(1)} %collective-permute-done.6.got), channel_id=1, source_target_pairs={{0,64},{1,65},{2,66},{3,67},{4,68},{5,69},{6,70},{7,71},{8,72},{9,... | collective-permute-start | bytes 49160 | tf_op jit(solution)/shard_map/ppermute | solution.py:342
  39.0 0.8 collective-permute-done.7.got_other
  40.4 1.6 %solve_kernel.2.v.v_old.v1 = f32[16,256]{1,0:T(8,128)} custom-call(f32[16,256]{1,0:T(8,128)} %get-tuple-element.49.mid, f32[16,256]{1,0:T(8,128)} %get-tuple-element.50.mid_other, f32[16,256]{1,0:T(8,128)} %copy-done.9, f32[16,256]{1,0:T(8,128)} %copy-done.11, f32[48,256]{1,0:T(8,128)} %get-tuple-element.29.factor), custom_call_target="tpu_custom_call" | custom-call | tf_op jit(solution)/shard_map/solve_kernel/pallas_call | solution.py:319
  42.7 5.7 %collective-permute-start.9 = (f32[16,256]{1,0:T(8,128)S(1)}, f32[16,256]{1,0:T(8,128)S(1)}, u32[]{:S(2)}, u32[]{:S(2)}) collective-permute-start(f32[16,256]{1,0:T(8,128)S(1)} %collective-permute-done.8.got), channel_id=1, source_target_pairs={{0,64},{1,65},{2,66},{3,67},{4,68},{5,69},{6,70},{7,71},{8,72},{9,... | collective-permute-start | bytes 49160 | tf_op jit(solution)/shard_map/ppermute | solution.py:342
  48.4 0.8 collective-permute-done.9.got_other
  49.8 3.6 %apply_kernel.3 = (f32[3,16,256]{2,1,0:T(8,128)}, f32[8,256]{1,0:T(8,128)}, f32[8,256]{1,0:T(8,128)}, f32[8,2048]{1,0:T(8,128)}, f32[8,128]{1,0:T(8,128)}) custom-call(s32[1]{0:T(128)} %bitcast.grp, f32[16,256]{1,0:T(8,128)} %solve_kernel.2.v.v_old.v1, f32[16,256]{1,0:T(8,128)} %copy-done.3, f32[16,256]{1,0:T(8,128)} %copy-done.6, s32[8,2048]{1,0:T(8,128)} %stack.19.index, ...), custom_call_target="tpu_custom_call" | custom-call | tf_op jit(solution)/shard_map/apply_kernel/pallas_call | solution.py:319
  53.8 1.1 collective-permute-done.10
  54.9 1.4 %fusion.3 = (f32[16,256]{1,0:T(8,128)S(1)}, f32[16,256]{1,0:T(8,128)}, f32[16,256]{1,0:T(8,128)}) fusion(f32[3,16,256]{2,1,0:T(8,128)S(1)} %collective-permute-done.10, f32[3,16,256]{2,1,0:T(8,128)} %get-tuple-element.32, pred[]{:T(512)S(6)} %eq.8), kind=kLoop, calls=%fused_computation.8 | loop fusion | flops 12288 | bytes 147457 | tf_op jit(solution)/shard_map/jit(_where)/select_n | solution.py:349
  56.9 6.8 %collective-permute-start.12 = (f32[16,256]{1,0:T(8,128)S(1)}, f32[16,256]{1,0:T(8,128)S(1)}, u32[]{:S(2)}, u32[]{:S(2)}) collective-permute-start(f32[16,256]{1,0:T(8,128)S(1)} %collective-permute-done.11.got), channel_id=1, source_target_pairs={{0,64},{1,65},{2,66},{3,67},{4,68},{5,69},{6,70},{7,71},{8,72},{9,... | collective-permute-start | bytes 49160 | tf_op jit(solution)/shard_map/ppermute | solution.py:342
  63.7 0.8 collective-permute-done.12.got_other
  65.2 1.6 %solve_kernel.3.v.v2 = f32[16,256]{1,0:T(8,128)} custom-call(f32[16,256]{1,0:T(8,128)} %get-tuple-element.46.mid, f32[16,256]{1,0:T(8,128)} %get-tuple-element.47.mid_other, f32[16,256]{1,0:T(8,128)} %copy-done.8, f32[16,256]{1,0:T(8,128)} %copy-done.10, f32[48,256]{1,0:T(8,128)} %get-tuple-element.29.factor), custom_call_target="tpu_custom_call" | custom-call | tf_op jit(solution)/shard_map/solve_kernel/pallas_call | solution.py:319
  67.5 7.0 %collective-permute-start.14 = (f32[16,256]{1,0:T(8,128)S(1)}, f32[16,256]{1,0:T(8,128)S(1)}, u32[]{:S(2)}, u32[]{:S(2)}) collective-permute-start(f32[16,256]{1,0:T(8,128)S(1)} %collective-permute-done.13.got), channel_id=1, source_target_pairs={{0,64},{1,65},{2,66},{3,67},{4,68},{5,69},{6,70},{7,71},{8,72},{9,... | collective-permute-start | bytes 49160 | tf_op jit(solution)/shard_map/ppermute | solution.py:342
  74.5 0.8 collective-permute-done.14.got_other
  76.0 3.2 %last_apply_kernel.1 = (f32[8,256]{1,0:T(8,128)}, f32[128,32]{1,0:T(8,128)}) custom-call(s32[1]{0:T(128)} %bitcast.grp, f32[16,256]{1,0:T(8,128)} %solve_kernel.3.v.v2, f32[16,256]{1,0:T(8,128)} %copy-done.2, f32[16,256]{1,0:T(8,128)} %copy-done.5, s32[8,2048]{1,0:T(8,128)} %stack.19.index, f32[2,16,2048]{2,1,0:T(8,128)} %get-tuple-element.24.jx, ...), custom_call_target="tpu_custom_call" | custom-call | tf_op jit(solution)/shard_map/last_apply_kernel/pallas_call | solution.py:319
  79.1 39.9 %all_to_all.11 = f32[128,1,32]{2,1,0:T(1,128)} all-to-all(f32[128,1,32]{2,1,0:T(1,128)} %bitcast.27), channel_id=1, replica_groups=mesh['grp'=2,'reg_0'=4,'reg_1'=4,'reg_2'=4] {'grp','reg_0','reg_1','reg_2'}, dimensions={0} | all-to-all | bytes 32768 | tf_op jit(solution)/shard_map/all_to_all | solution.py:381
  119.1 2.1 %final_kernel.1 = (f32[9,128]{1,0:T(8,128)}, f32[3,256]{1,0:T(4,128)}) custom-call(s32[1]{0:T(128)} %bitcast.grp, f32[128,32]{1,0:T(8,128)} %bitcast.26, f32[16,256]{1,0:T(8,128)} %get-tuple-element.23.v.v_old.v0, f32[16,256]{1,0:T(8,128)} %solve_kernel.2.v.v_old.v1, f32[16,256]{1,0:T(8,128)} %solve_kernel.3.v.v2, f32[8,256]{1,0:T(8,128)} %get-tuple-element.39.g0, ...), custom_call_target="tpu_custom_call" | custom-call | tf_op jit(solution)/shard_map/final_kernel/pallas_call | solution.py:319
  (42 shorter events, 7.7 us)
Async XLA Ops:
  0.6 0.7 copy-start.12
  1.4 0.7 copy-start.13
  6.6 2.7 %collective-permute-start = (f32[3,64,256]{2,1,0:T(8,128)}, f32[3,64,256]{2,1,0:T(8,128)S(1)}, u32[]{:S(2)}, u32[]{:S(2)}) collective-permute-start(f32[3,64,256]{2,1,0:T(8,128)} %get-tuple-element.22), channel_id=1, source_target_pairs={{0,64},{1,65},{2,66},{3,67},{4,68},{5,69},{6,70},{7,71},{8,72},{9,... | collective-permute-start | bytes 589832 | tf_op jit(solution)/shard_map/ppermute | solution.py:342
  10.8 0.7 collective-permute-start.1
  11.5 6.2 %copy-start = (f32[64,256]{1,0:T(8,128)}, f32[64,256]{1,0:T(8,128)S(1)}, u32[]{:S(2)}) copy-start(f32[64,256]{1,0:T(8,128)S(1)} %collective-permute-done.1.got) | copy-start | bytes 196612
  11.5 6.2 %collective-permute-start.2 = (f32[64,256]{1,0:T(8,128)S(1)}, f32[64,256]{1,0:T(8,128)S(1)}, u32[]{:S(2)}, u32[]{:S(2)}) collective-permute-start(f32[64,256]{1,0:T(8,128)S(1)} %collective-permute-done.1.got), channel_id=1, source_target_pairs={{0,64},{1,65},{2,66},{3,67},{4,68},{5,69},{6,70},{7,71},{8,72},{9,... | collective-permute-start | bytes 196616 | tf_op jit(solution)/shard_map/ppermute | solution.py:342
  17.6 0.6 copy-start.1
  20.1 0.7 collective-permute-start.3
  20.8 5.8 %copy-start.4 = (f32[16,256]{1,0:T(8,128)}, f32[16,256]{1,0:T(8,128)S(1)}, u32[]{:S(2)}) copy-start(f32[16,256]{1,0:T(8,128)S(1)} %collective-permute-done.3.got) | copy-start | bytes 49156
  20.8 5.8 %collective-permute-start.4 = (f32[16,256]{1,0:T(8,128)S(1)}, f32[16,256]{1,0:T(8,128)S(1)}, u32[]{:S(2)}, u32[]{:S(2)}) collective-permute-start(f32[16,256]{1,0:T(8,128)S(1)} %collective-permute-done.3.got), channel_id=1, source_target_pairs={{0,64},{1,65},{2,66},{3,67},{4,68},{5,69},{6,70},{7,71},{8,72},{9,... | collective-permute-start | bytes 49160 | tf_op jit(solution)/shard_map/ppermute | solution.py:342
  26.6 0.6 copy-start.7
  30.7 1.4 %collective-permute-start.5 = (f32[3,16,256]{2,1,0:T(8,128)}, f32[3,16,256]{2,1,0:T(8,128)S(1)}, u32[]{:S(2)}, u32[]{:S(2)}) collective-permute-start(f32[3,16,256]{2,1,0:T(8,128)} %get-tuple-element.28), channel_id=1, source_target_pairs={{0,64},{1,65},{2,66},{3,67},{4,68},{5,69},{6,70},{7,71},{8,72},{9,... | collective-permute-start | bytes 147464 | tf_op jit(solution)/shard_map/ppermute | solution.py:342
  33.6 0.7 collective-permute-start.6
  34.2 5.6 %copy-start.9 = (f32[16,256]{1,0:T(8,128)}, f32[16,256]{1,0:T(8,128)S(1)}, u32[]{:S(2)}) copy-start(f32[16,256]{1,0:T(8,128)S(1)} %collective-permute-done.6.got) | copy-start | bytes 49156
  34.2 5.6 %collective-permute-start.7 = (f32[16,256]{1,0:T(8,128)S(1)}, f32[16,256]{1,0:T(8,128)S(1)}, u32[]{:S(2)}, u32[]{:S(2)}) collective-permute-start(f32[16,256]{1,0:T(8,128)S(1)} %collective-permute-done.6.got), channel_id=1, source_target_pairs={{0,64},{1,65},{2,66},{3,67},{4,68},{5,69},{6,70},{7,71},{8,72},{9,... | collective-permute-start | bytes 49160 | tf_op jit(solution)/shard_map/ppermute | solution.py:342
  39.8 0.6 copy-start.11
  42.0 0.7 collective-permute-start.8
  42.7 6.6 %copy-start.3 = (f32[16,256]{1,0:T(8,128)}, f32[16,256]{1,0:T(8,128)S(1)}, u32[]{:S(2)}) copy-start(f32[16,256]{1,0:T(8,128)S(1)} %collective-permute-done.8.got) | copy-start | bytes 49156
  42.7 6.6 %collective-permute-start.9 = (f32[16,256]{1,0:T(8,128)S(1)}, f32[16,256]{1,0:T(8,128)S(1)}, u32[]{:S(2)}, u32[]{:S(2)}) collective-permute-start(f32[16,256]{1,0:T(8,128)S(1)} %collective-permute-done.8.got), channel_id=1, source_target_pairs={{0,64},{1,65},{2,66},{3,67},{4,68},{5,69},{6,70},{7,71},{8,72},{9,... | collective-permute-start | bytes 49160 | tf_op jit(solution)/shard_map/ppermute | solution.py:342
  49.2 0.6 copy-start.6
  53.4 1.4 %collective-permute-start.10 = (f32[3,16,256]{2,1,0:T(8,128)}, f32[3,16,256]{2,1,0:T(8,128)S(1)}, u32[]{:S(2)}, u32[]{:S(2)}) collective-permute-start(f32[3,16,256]{2,1,0:T(8,128)} %get-tuple-element.32), channel_id=1, source_target_pairs={{0,64},{1,65},{2,66},{3,67},{4,68},{5,69},{6,70},{7,71},{8,72},{9,... | collective-permute-start | bytes 147464 | tf_op jit(solution)/shard_map/ppermute | solution.py:342
  56.2 0.7 collective-permute-start.11
  56.9 7.7 %copy-start.8 = (f32[16,256]{1,0:T(8,128)}, f32[16,256]{1,0:T(8,128)S(1)}, u32[]{:S(2)}) copy-start(f32[16,256]{1,0:T(8,128)S(1)} %collective-permute-done.11.got) | copy-start | bytes 49156
  56.9 7.7 %collective-permute-start.12 = (f32[16,256]{1,0:T(8,128)S(1)}, f32[16,256]{1,0:T(8,128)S(1)}, u32[]{:S(2)}, u32[]{:S(2)}) collective-permute-start(f32[16,256]{1,0:T(8,128)S(1)} %collective-permute-done.11.got), channel_id=1, source_target_pairs={{0,64},{1,65},{2,66},{3,67},{4,68},{5,69},{6,70},{7,71},{8,72},{9,... | collective-permute-start | bytes 49160 | tf_op jit(solution)/shard_map/ppermute | solution.py:342
  64.6 0.6 copy-start.10
  66.8 0.7 collective-permute-start.13
  67.5 7.9 %copy-start.2 = (f32[16,256]{1,0:T(8,128)}, f32[16,256]{1,0:T(8,128)S(1)}, u32[]{:S(2)}) copy-start(f32[16,256]{1,0:T(8,128)S(1)} %collective-permute-done.13.got) | copy-start | bytes 49156
  67.5 7.9 %collective-permute-start.14 = (f32[16,256]{1,0:T(8,128)S(1)}, f32[16,256]{1,0:T(8,128)S(1)}, u32[]{:S(2)}, u32[]{:S(2)}) collective-permute-start(f32[16,256]{1,0:T(8,128)S(1)} %collective-permute-done.13.got), channel_id=1, source_target_pairs={{0,64},{1,65},{2,66},{3,67},{4,68},{5,69},{6,70},{7,71},{8,72},{9,... | collective-permute-start | bytes 49160 | tf_op jit(solution)/shard_map/ppermute | solution.py:342
  75.4 0.6 copy-start.5

commit v2 on v1

v2 whole, which is shorter than its diff:
```python
import functools

import jax
import jax.numpy as jnp
from jax import lax
from jax.experimental import pallas as pl
from jax.experimental.pallas import tpu as pltpu
from jax.sharding import Mesh
from jax.sharding import PartitionSpec as P

C_DEV = 128
P_DEV = 256
OBS = 2048
DAMPING = 4.0
WIDE = 2 * C_DEV
REG = ("reg_0", "reg_1", "reg_2")
GRP_REG = ("grp", "reg_0", "reg_1", "reg_2")
F32 = jnp.float32
BF16 = jnp.bfloat16
VMEM = pl.BlockSpec(memory_space=pltpu.VMEM)
SMEM = pl.BlockSpec(memory_space=pltpu.SMEM)
ROWS = 56
VMEM_LIMIT = 32 * 1024 * 1024


def three_parts(x):
    high = x.astype(BF16)
    rest = x - high.astype(F32)
    middle = rest.astype(BF16)
    low = (rest - middle.astype(F32)).astype(BF16)
    return high, middle, low


def stacked(x):
    high, middle, low = three_parts(x)
    parts = [high.astype(F32), middle.astype(F32), low.astype(F32)]
    return jnp.concatenate(parts, 0).astype(BF16)


def folded(x):
    rows = x.shape[0] // 3
    return x[:rows] + x[rows : 2 * rows] + x[2 * rows :]


def pick(field, onehot):
    return lax.dot_general(
        field, onehot, (((1,), (0,)), ((), ())), preferred_element_type=F32
    )


def put(terms, onehot):
    return lax.dot_general(
        terms, onehot, (((1,), (1,)), ((), ())), preferred_element_type=F32
    )


def onehot_of(index):
    ids = lax.broadcasted_iota(jnp.int32, (WIDE, index.shape[1]), 0)
    return jnp.where(ids == index, 1.0, 0.0).astype(BF16)


def total(x):
    return jnp.sum(jnp.sum(x, 0, keepdims=True), 1, keepdims=True)


def per_lane(x):
    row = jnp.sum(x, 0, keepdims=True)
    return functools.reduce(
        lambda a, b: a + b, [row[:, k : k + 128] for k in range(0, row.shape[1], 128)]
    )


def solve_points(vinv, g):
    a, b, c, d, e, f = [vinv[k : k + 1] for k in range(6)]
    x, y, z = [g[k : k + 1] for k in range(3)]
    rows = [a * x + b * y + c * z, b * x + d * y + e * z, c * x + e * y + f * z]
    return rows + [jnp.zeros((8 - 3, g.shape[1]), F32)]


def point_part(u, p, hot_p, vinv):
    g = folded(put(stacked(p[0] * u[0] + p[1] * u[1]), hot_p))
    s = jnp.concatenate(solve_points(vinv, g), 0)
    back = folded(pick(stacked(s), hot_p))
    return g, s, [jnp.sum(p[i] * back, 0, keepdims=True) for i in range(2)]


def position(where, regions):
    device = where[0]
    region = device & (regions - 1)
    return device >> (regions.bit_length() - 1), region, region & 1


def indices(regions, region, camera, slot):
    owners = camera[...] >> (C_DEV.bit_length() - 1)
    low = ((owners >> (regions.bit_length() - 1)) * C_DEV) | (camera[...] & (C_DEV - 1))
    return low, (owners & (regions - 1)) - region + 1, slot[...]


def split_frames(group, odd, blocks, keep, send):
    even = odd == 0
    zero = jnp.zeros_like(blocks[0])
    frames = [
        jnp.where(even, blocks[0], zero),
        jnp.where(even, blocks[1], blocks[0]),
        jnp.where(even, blocks[2], blocks[1]),
        jnp.where(even, zero, blocks[2]),
    ]
    first = group == 0
    for k in range(2):
        keep[k] = jnp.where(first, frames[2 + k], frames[k])
        send[k] = jnp.where(first, frames[k], frames[2 + k])


def to_tiles(tiles, group, here, there):
    first = group == 0
    rows = here.shape[1]
    for k in range(2):
        mine, other = here[k], there[k]
        lower = jnp.where(first, other, mine)
        upper = jnp.where(first, mine, other)
        for h in range(2):
            lanes = slice(128 * h, 128 * h + 128)
            tiles[pl.ds(2 * k + h, rows, stride=8), :] = lower[:, lanes]
            tiles[pl.ds(4 + 2 * k + h, rows, stride=8), :] = upper[:, lanes]


def tile(tiles, k):
    return tiles[8 * k : 8 * k + 8, :]


def first_kernel(
    regions, where, cam, pnt, res, camera, points, keep, send, jx, px, vinv_out, gres_out
):
    group, region, odd = position(where, regions)
    low, block, slot = indices(regions, region, camera, points)
    hot_p = onehot_of(slot)
    camf = cam[...].astype(F32)
    pf = pnt[...].astype(F32)
    zero5 = jnp.zeros((5, OBS), F32)
    zero7 = jnp.zeros((7, OBS), F32)
    for i in range(2):
        jx[i, 0:8, :] = camf[9 * i : 9 * i + 8]
        jx[i, 8:16, :] = jnp.concatenate([camf[9 * i + 8 : 9 * i + 9], zero7], 0)
        px[i] = jnp.concatenate([pf[3 * i : 3 * i + 3], zero5], 0)
    p = [px[0], px[1]]
    a = [jx[0, 0:8, :], jx[1, 0:8, :]]
    last = [jx[0, 8:9, :], jx[1, 8:9, :]]
    r = [res[0:1, :], res[1:2, :]]
    row = lax.broadcasted_iota(jnp.int32, (8, OBS), 0)
    squares = p[0] * p[0] + p[1] * p[1]
    turned = [
        jnp.where(row == 2, jnp.broadcast_to(x[0:1], x.shape), pltpu.roll(x, 7, 0)) for x in p
    ]
    products = p[0] * turned[0] + p[1] * turned[1]
    right = p[0] * r[0] + p[1] * r[1]
    sums = folded(put(stacked(jnp.concatenate([squares, products, right], 0)), hot_p))
    v00, v11, v22 = [sums[k : k + 1] + DAMPING for k in range(3)]
    v01, v12, v02 = [sums[8 + k : 9 + k] for k in range(3)]
    g = sums[16:24]
    c00 = v11 * v22 - v12 * v12
    c01 = v02 * v12 - v01 * v22
    c02 = v01 * v12 - v02 * v11
    c11 = v00 * v22 - v02 * v02
    c12 = v01 * v02 - v00 * v12
    c22 = v00 * v11 - v01 * v01
    scale = 1.0 / (v00 * c00 + v01 * c01 + v02 * c02)
    cofactors = jnp.concatenate(
        [c00, c01, c02, c11, c12, c22, jnp.zeros((2, P_DEV), F32)], 0
    )
    vinv = cofactors * scale
    vinv_out[...] = vinv
    gres_out[...] = g
    s = jnp.concatenate(solve_points(vinv, g), 0)
    back = folded(pick(stacked(s), hot_p))
    rem = [r[i] - jnp.sum(p[i] * back, 0, keepdims=True) for i in range(2)]
    rolled = []
    for d in range(5):
        other = [x if d == 0 else pltpu.roll(x, d, 0) for x in a]
        rolled.append(a[0] * other[0] + a[1] * other[1])
    corner = last[0] * last[0] + last[1] * last[1]
    end = last[0] * rem[0] + last[1] * rem[1]
    rolled[4] = jnp.where(row < 4, rolled[4], jnp.where(row == 4, corner, end))
    edge = a[0] * last[0] + a[1] * last[1]
    gradient = a[0] * rem[0] + a[1] * rem[1]
    terms = stacked(jnp.concatenate(rolled + [edge, gradient], 0))
    hot_c = onehot_of(low)
    blocks = []
    for k in range(3):
        mask = jnp.where(block == k, 1.0, 0.0).astype(BF16)
        blocks.append(folded(put(terms * mask, hot_c)))
    split_frames(group, odd, blocks, keep, send)


def solve_camera(low, inv, b):
    y = list(b)
    for k in range(9):
        y[k] = y[k] * inv[k]
        for i in range(k + 1, 9):
            y[i] = y[i] - low[i][k] * y[k]
    for k in range(8, -1, -1):
        y[k] = y[k] * inv[k]
        for i in range(k):
            y[i] = y[i] - low[k][i] * y[k]
    return y


def factor_camera(tiles, factor):
    def entry(i, j):
        if i == 8:
            k = 36 if j == 8 else 40 + j
        elif i - j < 4:
            k = 8 * (i - j) + i
        elif i - j == 4:
            k = 32 + j
        else:
            k = 8 * (8 - (i - j)) + j
        x = tile(tiles, k)
        return x + DAMPING if i == j else x

    low = [[None] * 9 for _ in range(9)]
    work = [[entry(i, j) if j <= i else None for j in range(9)] for i in range(9)]
    inv = []
    for k in range(9):
        inv.append(1.0 / jnp.sqrt(work[k][k]))
        for i in range(k + 1, 9):
            low[i][k] = work[i][k] * inv[k]
        for i in range(k + 1, 9):
            for j in range(k + 1, i + 1):
                work[i][j] = work[i][j] - low[i][k] * low[j][k]
    flat = [low[i][j] for i in range(9) for j in range(i)] + inv
    for k, x in enumerate(flat):
        factor[8 * k : 8 * k + 8, :] = x
    return low, inv


def read_factor(factor):
    low = [[None] * 9 for _ in range(9)]
    at = 0
    for i in range(9):
        for j in range(i):
            low[i][j] = tile(factor, at)
            at += 1
    return low, [tile(factor, at + k) for k in range(9)]


def apply_body(group, odd, x, field, low, block, slot, jx, px, vinv):
    hot_c = onehot_of(low)
    hot_p = onehot_of(slot)
    for k in range(9):
        field[8 * k : 8 * k + 8, :] = x[k]
    for k in range(9, 16):
        field[8 * k : 8 * k + 8, :] = jnp.zeros((8, 128), F32)
    frames = [
        jnp.concatenate([field[pl.ds(2 * f + h, 16, stride=8), :] for h in range(2)], 1)
        for f in range(4)
    ]
    seen = [jnp.where(odd == 0, frames[k], frames[k + 1]) for k in range(3)]
    v = jnp.where(group == 0, seen[1][:, 0:128], seen[1][:, 128:256])
    picked = pick(jnp.concatenate([stacked(f) for f in seen], 0), hot_c)
    blocks = [folded(picked[48 * k : 48 * k + 48]) for k in range(3)]
    values = jnp.where(block == 0, blocks[0], jnp.where(block == 1, blocks[1], blocks[2]))
    u = [jnp.sum(jx[i] * values, 0, keepdims=True) for i in range(2)]
    p = [px[0], px[1]]
    g, s, ps = point_part(u, p, hot_p, vinv[...])
    return hot_c, v, u, g, s, ps


def finish(group, odd, hot_c, block, jx, ps, keep, send):
    terms = stacked(jx[0] * ps[0] + jx[1] * ps[1])
    lhs = jnp.concatenate(
        [terms * jnp.where(block == k, 1.0, 0.0).astype(BF16) for k in range(3)], 0
    )
    out = put(lhs, hot_c)
    split_frames(
        group, odd, [folded(out[48 * k : 48 * k + 48]) for k in range(3)], keep, send
    )


def scalar_rows(pairs):
    rows = [functools.reduce(lambda a, b: a + b, [per_lane(x) for x in pair]) for pair in pairs]
    return jnp.concatenate(rows + [jnp.zeros((8 - len(rows), 128), F32)], 0)


def scalars(v, v_old, u, rem, rem_old, g, s, s_old):
    return scalar_rows(
        [
            (DAMPING * v * v_old, u[0] * rem_old[0:1, :] + u[1] * rem_old[1:2, :]),
            (DAMPING * v * v, u[0] * rem[0] + u[1] * rem[1]),
            (g * s_old,),
            (g * s,),
        ]
    )


def start_kernel(
    regions, where, here, there, camera, points, jx, px, vinv,
    keep, send, factor, v_out, g_out, s_out, rem_out, scal, tiles, field,
):
    group, region, odd = position(where, regions)
    low, block, slot = indices(regions, region, camera, points)
    to_tiles(tiles, group, here, there)
    lower, inv = factor_camera(tiles, factor)
    b = [-tile(tiles, 48 + k) for k in range(8)] + [-tile(tiles, 37)]
    x = solve_camera(lower, inv, b)
    dots = functools.reduce(lambda p, q: p + q, [b[k] * x[k] for k in range(9)])
    own = lax.broadcasted_iota(jnp.int32, (8, 128), 0) == 2 * (1 + odd) + group
    hot_c, v, u, g, s, ps = apply_body(
        group, odd, x, field, low, block, slot, jx, px, vinv
    )
    rem = [u[i] - ps[i] for i in range(2)]
    v_out[...], g_out[...], s_out[...] = v, g, s
    rem_out[...] = jnp.concatenate(rem + [jnp.zeros((6, OBS), F32)], 0)
    finish(group, odd, hot_c, block, jx, ps, keep, send)
    scal[...] = scalar_rows(
        [
            (jnp.where(own, dots, 0.0),),
            (DAMPING * v * v, u[0] * rem[0] + u[1] * rem[1]),
            (g * s,),
        ]
    )


def next_kernel(
    regions, where, here, there, factor, camera, points, jx, px, vinv, v_old, s_old, rem_old,
    keep, send, v_out, g_out, s_out, rem_out, scal, tiles, field,
):
    group, region, odd = position(where, regions)
    low, block, slot = indices(regions, region, camera, points)
    to_tiles(tiles, group, here, there)
    x = solve_camera(*read_factor(factor), [tile(tiles, k) for k in range(9)])
    hot_c, v, u, g, s, ps = apply_body(
        group, odd, x, field, low, block, slot, jx, px, vinv
    )
    rem = [u[i] - ps[i] for i in range(2)]
    v_out[...], g_out[...], s_out[...] = v, g, s
    rem_out[...] = jnp.concatenate(rem + [jnp.zeros((6, OBS), F32)], 0)
    finish(group, odd, hot_c, block, jx, ps, keep, send)
    scal[...] = scalars(v, v_old[...], u, rem, rem_old, g, s, s_old[...])


def last_kernel(
    regions, where, here, there, factor, camera, points, jx, px, vinv, v_old, s_old, rem_old,
    scal0, scal1, v_out, g_out, sums, tiles, field,
):
    group, region, odd = position(where, regions)
    low, block, slot = indices(regions, region, camera, points)
    to_tiles(tiles, group, here, there)
    x = solve_camera(*read_factor(factor), [tile(tiles, k) for k in range(9)])
    hot_c, v, u, g, s, ps = apply_body(
        group, odd, x, field, low, block, slot, jx, px, vinv
    )
    rem = [u[i] - ps[i] for i in range(2)]
    v_out[...], g_out[...] = v, g
    scal2 = scalars(v, v_old[...], u, rem, rem_old, g, s, s_old[...])
    rows = jnp.concatenate([scal0[...], scal1[...], scal2, jnp.zeros((8, 128), F32)], 0)
    ones = jnp.ones((128, 128), BF16)
    high, middle, low_part = three_parts(rows)
    sums[...] = put(ones, high) + put(ones, middle) + put(ones, low_part)


def final_kernel(back, v0, v1, v2, g0, g1, g2, gres, vinv, cam, pnt):
    sums = jnp.sum(back[...], 0, keepdims=True)

    def value(k):
        return sums[:, k : k + 1]

    m = [value(k) for k in (0, 2, 10, 11, 18)]
    s = [value(k) for k in (1, 8, 9, 16, 17)]

    def form(h, x):
        terms = [x[i] * x[j] * h[i + j] for i in range(3) for j in range(3)]
        return functools.reduce(lambda p, q: p + q, terms)

    def ratio(x, y):
        return jnp.where(y > 0, x / jnp.where(y > 0, y, 1.0), 0.0)

    one, zero = jnp.ones((1, 1), F32), jnp.zeros((1, 1), F32)
    y = [zero, zero, zero]
    z = [one, zero, zero]
    d = list(z)
    current = m[0]
    for turn in range(3):
        step = ratio(current, form(s, d))
        y = [y[k] + step * d[k] for k in range(3)]
        if turn < 2:
            image = [d[0], d[1] - d[0], d[2] - d[1]]
            z = [z[k] - step * image[k] for k in range(3)]
            following = form(m, z)
            beta = ratio(following, current)
            d = [z[k] + beta * d[k] for k in range(3)]
            current = following
    x = y[0] * v0[...] + y[1] * v1[...] + y[2] * v2[...]
    cam[...] = x[0:9]
    g = gres[...] + (y[0] * g0[...] + y[1] * g1[...] + y[2] * g2[...])
    rows = solve_points(vinv[...], g)
    for k in range(3):
        pnt[k : k + 1, :] = -rows[k]


def shape(*dims, dtype=F32):
    return jax.ShapeDtypeStruct(dims, dtype)


def call(kernel, outs, *args, scalar=False, scratch=(), regions=None):
    specs = [VMEM] * len(args)
    if scalar:
        specs[0] = SMEM
    return pl.pallas_call(
        kernel if regions is None else functools.partial(kernel, regions),
        out_shape=outs,
        in_specs=specs,
        out_specs=[VMEM] * len(outs),
        scratch_shapes=scratch,
        compiler_params=pltpu.CompilerParams(vmem_limit_bytes=VMEM_LIMIT),
        name=kernel.__name__,
    )(*args)


def local(regions, cam_jacobian, point_jacobian, residuals, obs_camera, obs_point):
    where = (lax.axis_index("grp") * regions + lax.axis_index(REG)).reshape(1)
    camera, points = obs_camera.reshape(1, OBS), obs_point.reshape(1, OBS)

    def both_ways(pairs):
        return pairs + [(b, a) for a, b in pairs]

    cores = both_ways([(r, regions + r) for r in range(regions)])
    pair = both_ways(
        [(g * regions + r, g * regions + r + 1) for g in range(2) for r in range(0, regions, 2)]
    )
    next_pair = both_ways(
        [(r + i, regions + r + 3 - i) for r in range(0, regions - 2, 2) for i in range(2)]
    )

    def swap(x, pairs):
        return lax.ppermute(x, GRP_REG, pairs)

    def totals(keep, send):
        half = keep + swap(send, cores)
        half = half + swap(half, pair)
        half = half + swap(half, next_pair)
        return half, swap(half, cores)

    def halves(rows):
        return [shape(2, rows, WIDE)] * 2

    run = functools.partial(call, scalar=True, regions=regions)
    field = pltpu.VMEM((128, 128), F32)
    per_point = shape(8, P_DEV)
    rest = [shape(16, 128), per_point, per_point, shape(8, OBS), shape(8, 128)]

    keep, send, jx, px, vinv, gres = run(
        first_kernel,
        halves(ROWS) + [shape(2, 16, OBS), shape(2, 8, OBS), per_point, per_point],
        where, cam_jacobian, point_jacobian, residuals, camera, points,
    )
    common = (camera, points, jx, px, vinv)
    keep, send, factor, v0, g0, s0, rem0, scal0 = run(
        start_kernel,
        halves(16) + [shape(45 * 8, 128)] + rest,
        where, *totals(keep, send), *common,
        scratch=[pltpu.VMEM((8 * ROWS, 128), F32), field],
    )
    keep, send, v1, g1, s1, rem1, scal1 = run(
        next_kernel,
        halves(16) + rest,
        where, *totals(keep, send), factor, *common, v0, s0, rem0,
        scratch=[field, field],
    )
    v2, g2, sums = run(
        last_kernel,
        [shape(16, 128), per_point, shape(128, 32)],
        where, *totals(keep, send), factor, *common, v1, s1, rem1, scal0, scal1,
        scratch=[field, field],
    )
    back = lax.all_to_all(sums, GRP_REG, 0, 0, tiled=True)
    return call(
        final_kernel,
        [shape(9, C_DEV), shape(3, P_DEV)],
        back, v0, v1, v2, g0, g1, g2, gres, vinv,
    )


def solution(mesh):
    torus = Mesh(
        mesh.devices.reshape(mesh.shape["grp"], 4, 4, 4), ("grp", "reg_0", "reg_1", "reg_2")
    )
    return jax.shard_map(
        functools.partial(local, mesh.shape["reg"]),
        mesh=torus,
        in_specs=(P(None, GRP_REG), P(None, GRP_REG), P(None, GRP_REG), P(GRP_REG), P(GRP_REG)),
        out_specs=(P(None, GRP_REG), P(None, GRP_REG)),
        check_vma=False,
    )
```

time: 122 us -> 82.6 us (0.68)
  Pallas kernels: 21.3 us -> 8.75 us
  blocking collectives: 39.9 us -> 27.6 us
  starting transfers between devices: 40.5 us -> 29 us
  waiting for transfers between devices: 8.59 us -> 13.6 us
  other arithmetic: 4.34 us -> 0.1 us
  local copies, waits for them, and re-layouts: 5.71 us -> 2.35 us
    pallas_call x8 -> x5, Pallas kernels: 21.3 us -> 8.75 us  [call(): pl.pallas_call(kernel if regions is None else functools.partial(kernel, r...]
    all_to_all x1, blocking collectives: 39.9 us -> 27.6 us  [local(): back = lax.all_to_all(sums, GRP_REG, 0, 0, tiled=True)]
    ppermute x15 -> x12, starting transfers between devices: 40.5 us -> 29 us  [swap(): return lax.ppermute(x, GRP_REG, pairs)]
    ppermute x15 -> x12, waiting for transfers between devices: 8.59 us -> 13.6 us  [swap(): return lax.ppermute(x, GRP_REG, pairs)]
    select_n x3 -> x0, other arithmetic: 4.31 us -> none  [to_owner(): outgoing = jnp.where(group == 0, part[2] + theirs[2], part[0] + theirs[0])]
    unnamed x28 -> x10, local copies, waits for them, and re-layouts: 5.02 us -> 2.35 us
  transfers between devices with their start and end apart: 15 -> 12, of which waited for: 9 -> 9; matrix products, arithmetic and copies ran while one was open for 0% -> 0% of each run, Pallas kernels for 0% -> 0%
where the time goes in v2:
time: 82.6 us; the launch traced here: 82.2 us
  starting transfers between devices  29 us (35%)
  blocking collectives  27.6 us (33%)
  waiting for transfers between devices  13.6 us (16%)
  Pallas kernels  8.75 us (11%)
  local copies, waits for them, and re-layouts  2.35 us (3%)
    ppermute x12, starting transfers between devices, swap(): return lax.ppermute(x, GRP_REG, pairs)  29 us
    all_to_all x1, blocking collectives, local(): back = lax.all_to_all(sums, GRP_REG, 0, 0, tiled=True)  27.6 us
    ppermute x12, waiting for transfers between devices, swap(): return lax.ppermute(x, GRP_REG, pairs)  13.6 us
    pallas_call x5, Pallas kernels, call(): pl.pallas_call(kernel if regions is None else functools.partial(kernel, r...  8.75 us
    unnamed x10, local copies, waits for them, and re-layouts  2.35 us
  transfers between devices with their start and end apart: 12, of which 9 were waited for; matrix products, arithmetic and copies ran while one was open for 0% of the time, Pallas kernels for 0%

profile of v2, /device:TPU:1, one launch (start us, length us, event | category | flops | bytes accessed | tf_op | source)
XLA Modules:
  0.0 82.2 jit_solution(12327632379360506971)
XLA Ops:
  0.7 0.7 copy-done.4
  1.4 0.0 copy-done
  1.4 0.9 %copy-done.2 = bf16[18,2048]{1,0:T(8,128)(2,1)S(1)} copy-done((bf16[18,2048]{1,0:T(8,128)(2,1)S(1)}, bf16[18,2048]{1,0:T(8,128)(2,1)}, u32[]{:S(2)}) %copy-start.2) | copy-done | bytes 73752
  2.3 0.8 copy-done.3
  3.0 2.2 %first_kernel.1 = (f32[2,56,256]{2,1,0:T(8,128)S(1)}, f32[2,56,256]{2,1,0:T(8,128)S(1)}, f32[2,16,2048]{2,1,0:T(8,128)S(1)}, f32[2,8,2048]{2,1,0:T(8,128)S(1)}, ...) custom-call(s32[1]{0:T(128)} %bitcast.where, bf16[18,2048]{1,0:T(8,128)(2,1)S(1)} %copy-done.2, bf16[6,2048]{1,0:T(8,128)(2,1)S(1)} %copy-done.3, ...), custom_call_target="tpu_custom_call" | custom-call | tf_op jit(solution)/shard_map/first_kernel/pallas_call | solution.py:408
  5.2 1.5 %collective-permute-start = (f32[2,56,256]{2,1,0:T(8,128)S(1)}, f32[2,56,256]{2,1,0:T(8,128)S(1)}, u32[]{:S(2)}, u32[]{:S(2)}) collective-permute-start(f32[2,56,256]{2,1,0:T(8,128)S(1)} %get-tuple-element.27), channel_id=1, source_target_pairs={{0,64},{1,65},{2,66},{3,67},{4,68},{5,69},{6,70},{7,71},{8,72},{9,... | collective-permute-start | bytes 344072 | tf_op jit(solution)/shard_map/ppermute | solution.py:435
  6.7 1.0 %collective-permute-done = f32[2,56,256]{2,1,0:T(8,128)S(1)} collective-permute-done((f32[2,56,256]{2,1,0:T(8,128)S(1)}, f32[2,56,256]{2,1,0:T(8,128)S(1)}, u32[]{:S(2)}, u32[]{:S(2)}) %collective-permute-start) | collective-permute-done | bytes 114720 | tf_op jit(solution)/shard_map/ppermute | solution.py:435
  7.7 1.5 %collective-permute-start.1 = (f32[2,56,256]{2,1,0:T(8,128)S(1)}, f32[2,56,256]{2,1,0:T(8,128)S(1)}, u32[]{:S(2)}, u32[]{:S(2)}) collective-permute-start(f32[2,56,256]{2,1,0:T(8,128)S(1)} %add.39), channel_id=1, source_target_pairs={{0,1},{2,3},{4,5},{6,7},{8,9},{10,11},{12,13},{14,15},{16,17},{18,... | collective-permute-start | bytes 344072 | tf_op jit(solution)/shard_map/ppermute | solution.py:435
  9.2 2.9 %collective-permute-done.1 = f32[2,56,256]{2,1,0:T(8,128)S(1)} collective-permute-done((f32[2,56,256]{2,1,0:T(8,128)S(1)}, f32[2,56,256]{2,1,0:T(8,128)S(1)}, u32[]{:S(2)}, u32[]{:S(2)}) %collective-permute-start.1) | collective-permute-done | bytes 114720 | tf_op jit(solution)/shard_map/ppermute | solution.py:435
  12.1 0.7 collective-permute-start.2
  12.8 7.9 %collective-permute-start.3 = (f32[2,56,256]{2,1,0:T(8,128)S(1)}, f32[2,56,256]{2,1,0:T(8,128)S(1)}, u32[]{:S(2)}, u32[]{:S(2)}) collective-permute-start(f32[2,56,256]{2,1,0:T(8,128)S(1)} %add.41.here), channel_id=1, source_target_pairs={{0,64},{1,65},{2,66},{3,67},{4,68},{5,69},{6,70},{7,71},{8,72},{9,... | collective-permute-start | bytes 344072 | tf_op jit(solution)/shard_map/ppermute | solution.py:435
  20.8 1.0 %collective-permute-done.3.there = f32[2,56,256]{2,1,0:T(8,128)S(1)} collective-permute-done((f32[2,56,256]{2,1,0:T(8,128)S(1)}, f32[2,56,256]{2,1,0:T(8,128)S(1)}, u32[]{:S(2)}, u32[]{:S(2)}) %collective-permute-start.3) | collective-permute-done | bytes 114720 | tf_op jit(solution)/shard_map/ppermute | solution.py:435
  21.7 2.0 %start_kernel.1 = (f32[2,16,256]{2,1,0:T(8,128)S(1)}, f32[2,16,256]{2,1,0:T(8,128)S(1)}, f32[360,128]{1,0:T(8,128)S(1)}, f32[16,128]{1,0:T(8,128)S(1)}, f32[8,25...) custom-call(s32[1]{0:T(128)} %bitcast.where, f32[2,56,256]{2,1,0:T(8,128)S(1)} %add.41.here, ...), custom_call_target="tpu_custom_call" | custom-call | tf_op jit(solution)/shard_map/start_kernel/pallas_call | solution.py:408
  23.7 0.4 collective-permute-start.4
  24.2 0.9 %collective-permute-done.4 = f32[2,16,256]{2,1,0:T(8,128)S(1)} collective-permute-done((f32[2,16,256]{2,1,0:T(8,128)S(1)}, f32[2,16,256]{2,1,0:T(8,128)S(1)}, u32[]{:S(2)}, u32[]{:S(2)}) %collective-permute-start.4) | collective-permute-done | bytes 32800 | tf_op jit(solution)/shard_map/ppermute | solution.py:435
  25.0 0.2 collective-permute-start.5
  25.2 2.6 %collective-permute-done.5 = f32[2,16,256]{2,1,0:T(8,128)S(1)} collective-permute-done((f32[2,16,256]{2,1,0:T(8,128)S(1)}, f32[2,16,256]{2,1,0:T(8,128)S(1)}, u32[]{:S(2)}, u32[]{:S(2)}) %collective-permute-start.5) | collective-permute-done | bytes 32800 | tf_op jit(solution)/shard_map/ppermute | solution.py:435
  27.8 0.7 collective-permute-start.6
  28.5 0.0 collective-permute-done.6
  28.5 7.3 %collective-permute-start.7 = (f32[2,16,256]{2,1,0:T(8,128)S(1)}, f32[2,16,256]{2,1,0:T(8,128)S(1)}, u32[]{:S(2)}, u32[]{:S(2)}) collective-permute-start(f32[2,16,256]{2,1,0:T(8,128)S(1)} %add.44.here), channel_id=1, source_target_pairs={{0,64},{1,65},{2,66},{3,67},{4,68},{5,69},{6,70},{7,71},{8,72},{9,... | collective-permute-start | bytes 98312 | tf_op jit(solution)/shard_map/ppermute | solution.py:435
  35.7 0.9 %collective-permute-done.7.there = f32[2,16,256]{2,1,0:T(8,128)S(1)} collective-permute-done((f32[2,16,256]{2,1,0:T(8,128)S(1)}, f32[2,16,256]{2,1,0:T(8,128)S(1)}, u32[]{:S(2)}, u32[]{:S(2)}) %collective-permute-start.7) | collective-permute-done | bytes 32800 | tf_op jit(solution)/shard_map/ppermute | solution.py:435
  36.6 1.9 %next_kernel.1 = (f32[2,16,256]{2,1,0:T(8,128)S(1)}, f32[2,16,256]{2,1,0:T(8,128)S(1)}, f32[16,128]{1,0:T(8,128)S(1)}, f32[8,256]{1,0:T(8,128)S(1)}, f32[8,256]{...) custom-call(s32[1]{0:T(128)} %bitcast.where, f32[2,16,256]{2,1,0:T(8,128)S(1)} %add.44.here, ...), custom_call_target="tpu_custom_call" | custom-call | tf_op jit(solution)/shard_map/next_kernel/pallas_call | solution.py:408
  38.5 0.4 collective-permute-start.8
  39.0 0.9 %collective-permute-done.8 = f32[2,16,256]{2,1,0:T(8,128)S(1)} collective-permute-done((f32[2,16,256]{2,1,0:T(8,128)S(1)}, f32[2,16,256]{2,1,0:T(8,128)S(1)}, u32[]{:S(2)}, u32[]{:S(2)}) %collective-permute-start.8) | collective-permute-done | bytes 32800 | tf_op jit(solution)/shard_map/ppermute | solution.py:435
  39.8 2.8 %collective-permute-done.9 = f32[2,16,256]{2,1,0:T(8,128)S(1)} collective-permute-done((f32[2,16,256]{2,1,0:T(8,128)S(1)}, f32[2,16,256]{2,1,0:T(8,128)S(1)}, u32[]{:S(2)}, u32[]{:S(2)}) %collective-permute-start.9) | collective-permute-done | bytes 32800 | tf_op jit(solution)/shard_map/ppermute | solution.py:435
  42.6 0.7 collective-permute-start.10
  43.3 0.0 collective-permute-done.10
  43.3 7.8 %collective-permute-start.11 = (f32[2,16,256]{2,1,0:T(8,128)S(1)}, f32[2,16,256]{2,1,0:T(8,128)S(1)}, u32[]{:S(2)}, u32[]{:S(2)}) collective-permute-start(f32[2,16,256]{2,1,0:T(8,128)S(1)} %add.47.here), channel_id=1, source_target_pairs={{0,64},{1,65},{2,66},{3,67},{4,68},{5,69},{6,70},{7,71},{8,72},{9,... | collective-permute-start | bytes 98312 | tf_op jit(solution)/shard_map/ppermute | solution.py:435
  51.1 0.9 %collective-permute-done.11.there = f32[2,16,256]{2,1,0:T(8,128)S(1)} collective-permute-done((f32[2,16,256]{2,1,0:T(8,128)S(1)}, f32[2,16,256]{2,1,0:T(8,128)S(1)}, u32[]{:S(2)}, u32[]{:S(2)}) %collective-permute-start.11) | collective-permute-done | bytes 32800 | tf_op jit(solution)/shard_map/ppermute | solution.py:435
  52.0 1.5 %last_kernel.1 = (f32[16,128]{1,0:T(8,128)S(1)}, f32[8,256]{1,0:T(8,128)S(1)}, f32[128,32]{1,0:T(8,128)S(1)}) custom-call(s32[1]{0:T(128)} %bitcast.where, f32[2,16,256]{2,1,0:T(8,128)S(1)} %add.47.here, f32[2,16,256]{2,1,0:T(8,128)S(1)} %collective-permute-done.11.there, f32[360,128]{1,0:T(8,128)S(1)} %get-tuple-element.33.factor, s32[1,2048]{1,0:T(1,128)S(1)} %bitcast.11, ...), custom_call_target="tpu_custom_call" | custom-call | tf_op jit(solution)/shard_map/last_kernel/pallas_call | solution.py:408
  53.5 27.6 %all_to_all.11 = f32[128,1,32]{2,1,0:T(1,128)S(1)} all-to-all(f32[128,1,32]{2,1,0:T(1,128)S(1)} %bitcast.16), channel_id=1, replica_groups=mesh['grp'=2,'reg_0'=4,'reg_1'=4,'reg_2'=4] {'grp','reg_0','reg_1','reg_2'}, dimensions={0} | all-to-all | bytes 32768 | tf_op jit(solution)/shard_map/all_to_all | solution.py:475
  81.0 1.2 %final_kernel.1 = (f32[9,128]{1,0:T(8,128)}, f32[3,256]{1,0:T(4,128)}) custom-call(f32[128,32]{1,0:T(8,128)S(1)} %bitcast.7, f32[16,128]{1,0:T(8,128)S(1)} %get-tuple-element.34.v_old.v0, f32[16,128]{1,0:T(8,128)S(1)} %get-tuple-element.39.v_old.v1, f32[16,128]{1,0:T(8,128)S(1)} %get-tuple-element.45.v2, f32[8,256]{1,0:T(8,128)S(1)} %get-tuple-element.46.g0, ...), custom_call_target="tpu_custom_call" | custom-call | tf_op jit(solution)/shard_map/final_kernel/pallas_call | solution.py:408
  (17 shorter events, 0.1 us)
Async XLA Ops:
  0.6 0.7 copy-start.4
  0.6 0.7 copy-start.1
  0.7 0.7 copy-start
  1.4 0.9 %copy-start.2 = (bf16[18,2048]{1,0:T(8,128)(2,1)S(1)}, bf16[18,2048]{1,0:T(8,128)(2,1)}, u32[]{:S(2)}) copy-start(bf16[18,2048]{1,0:T(8,128)(2,1)} %cam.1) | copy-start | bytes 221188
  2.3 0.8 copy-start.3
  5.2 2.4 %collective-permute-start = (f32[2,56,256]{2,1,0:T(8,128)S(1)}, f32[2,56,256]{2,1,0:T(8,128)S(1)}, u32[]{:S(2)}, u32[]{:S(2)}) collective-permute-start(f32[2,56,256]{2,1,0:T(8,128)S(1)} %get-tuple-element.27), channel_id=1, source_target_pairs={{0,64},{1,65},{2,66},{3,67},{4,68},{5,69},{6,70},{7,71},{8,72},{9,... | collective-permute-start | bytes 344072 | tf_op jit(solution)/shard_map/ppermute | solution.py:435
  7.7 4.4 %collective-permute-start.1 = (f32[2,56,256]{2,1,0:T(8,128)S(1)}, f32[2,56,256]{2,1,0:T(8,128)S(1)}, u32[]{:S(2)}, u32[]{:S(2)}) collective-permute-start(f32[2,56,256]{2,1,0:T(8,128)S(1)} %add.39), channel_id=1, source_target_pairs={{0,1},{2,3},{4,5},{6,7},{8,9},{10,11},{12,13},{14,15},{16,17},{18,... | collective-permute-start | bytes 344072 | tf_op jit(solution)/shard_map/ppermute | solution.py:435
  12.1 0.7 collective-permute-start.2
  12.8 8.9 %collective-permute-start.3 = (f32[2,56,256]{2,1,0:T(8,128)S(1)}, f32[2,56,256]{2,1,0:T(8,128)S(1)}, u32[]{:S(2)}, u32[]{:S(2)}) collective-permute-start(f32[2,56,256]{2,1,0:T(8,128)S(1)} %add.41.here), channel_id=1, source_target_pairs={{0,64},{1,65},{2,66},{3,67},{4,68},{5,69},{6,70},{7,71},{8,72},{9,... | collective-permute-start | bytes 344072 | tf_op jit(solution)/shard_map/ppermute | solution.py:435
  23.7 1.3 %collective-permute-start.4 = (f32[2,16,256]{2,1,0:T(8,128)S(1)}, f32[2,16,256]{2,1,0:T(8,128)S(1)}, u32[]{:S(2)}, u32[]{:S(2)}) collective-permute-start(f32[2,16,256]{2,1,0:T(8,128)S(1)} %get-tuple-element.32), channel_id=1, source_target_pairs={{0,64},{1,65},{2,66},{3,67},{4,68},{5,69},{6,70},{7,71},{8,72},{9,... | collective-permute-start | bytes 98312 | tf_op jit(solution)/shard_map/ppermute | solution.py:435
  25.0 2.8 %collective-permute-start.5 = (f32[2,16,256]{2,1,0:T(8,128)S(1)}, f32[2,16,256]{2,1,0:T(8,128)S(1)}, u32[]{:S(2)}, u32[]{:S(2)}) collective-permute-start(f32[2,16,256]{2,1,0:T(8,128)S(1)} %add.42), channel_id=1, source_target_pairs={{0,1},{2,3},{4,5},{6,7},{8,9},{10,11},{12,13},{14,15},{16,17},{18,... | collective-permute-start | bytes 98312 | tf_op jit(solution)/shard_map/ppermute | solution.py:435
  27.8 0.7 collective-permute-start.6
  28.5 8.1 %collective-permute-start.7 = (f32[2,16,256]{2,1,0:T(8,128)S(1)}, f32[2,16,256]{2,1,0:T(8,128)S(1)}, u32[]{:S(2)}, u32[]{:S(2)}) collective-permute-start(f32[2,16,256]{2,1,0:T(8,128)S(1)} %add.44.here), channel_id=1, source_target_pairs={{0,64},{1,65},{2,66},{3,67},{4,68},{5,69},{6,70},{7,71},{8,72},{9,... | collective-permute-start | bytes 98312 | tf_op jit(solution)/shard_map/ppermute | solution.py:435
  38.5 1.3 %collective-permute-start.8 = (f32[2,16,256]{2,1,0:T(8,128)S(1)}, f32[2,16,256]{2,1,0:T(8,128)S(1)}, u32[]{:S(2)}, u32[]{:S(2)}) collective-permute-start(f32[2,16,256]{2,1,0:T(8,128)S(1)} %get-tuple-element.38), channel_id=1, source_target_pairs={{0,64},{1,65},{2,66},{3,67},{4,68},{5,69},{6,70},{7,71},{8,72},{9,... | collective-permute-start | bytes 98312 | tf_op jit(solution)/shard_map/ppermute | solution.py:435
  39.8 2.8 %collective-permute-start.9 = (f32[2,16,256]{2,1,0:T(8,128)S(1)}, f32[2,16,256]{2,1,0:T(8,128)S(1)}, u32[]{:S(2)}, u32[]{:S(2)}) collective-permute-start(f32[2,16,256]{2,1,0:T(8,128)S(1)} %add.45), channel_id=1, source_target_pairs={{0,1},{2,3},{4,5},{6,7},{8,9},{10,11},{12,13},{14,15},{16,17},{18,... | collective-permute-start | bytes 98312 | tf_op jit(solution)/shard_map/ppermute | solution.py:435
  42.6 0.7 collective-permute-start.10
  43.3 8.7 %collective-permute-start.11 = (f32[2,16,256]{2,1,0:T(8,128)S(1)}, f32[2,16,256]{2,1,0:T(8,128)S(1)}, u32[]{:S(2)}, u32[]{:S(2)}) collective-permute-start(f32[2,16,256]{2,1,0:T(8,128)S(1)} %add.47.here), channel_id=1, source_target_pairs={{0,64},{1,65},{2,66},{3,67},{4,68},{5,69},{6,70},{7,71},{8,72},{9,... | collective-permute-start | bytes 98312 | tf_op jit(solution)/shard_map/ppermute | solution.py:435

commit v3 on v2

--- a/solution.py
+++ b/solution.py
@@ -18,6 +18,7 @@
 F32 = jnp.float32
 BF16 = jnp.bfloat16
 VMEM = pl.BlockSpec(memory_space=pltpu.VMEM)
+HBM = pl.BlockSpec(memory_space=pltpu.HBM)
 SMEM = pl.BlockSpec(memory_space=pltpu.SMEM)
 ROWS = 56
 VMEM_LIMIT = 32 * 1024 * 1024
@@ -90,10 +91,10 @@
     return device >> (regions.bit_length() - 1), region, region & 1
 
 
-def indices(regions, region, camera, slot):
-    owners = camera[...] >> (C_DEV.bit_length() - 1)
-    low = ((owners >> (regions.bit_length() - 1)) * C_DEV) | (camera[...] & (C_DEV - 1))
-    return low, (owners & (regions - 1)) - region + 1, slot[...]
+def indices(regions, region, camera):
+    owners = camera >> (C_DEV.bit_length() - 1)
+    low = ((owners >> (regions.bit_length() - 1)) * C_DEV) | (camera & (C_DEV - 1))
+    return low, (owners & (regions - 1)) - region + 1
 
 
 def split_frames(group, odd, blocks, keep, send):
@@ -105,14 +106,14 @@
         jnp.where(even, blocks[2], blocks[1]),
         jnp.where(even, zero, blocks[2]),
     ]
-    first = group == 0
+    first = group == odd
     for k in range(2):
         keep[k] = jnp.where(first, frames[2 + k], frames[k])
         send[k] = jnp.where(first, frames[k], frames[2 + k])
 
 
-def to_tiles(tiles, group, here, there):
-    first = group == 0
+def to_tiles(tiles, group, odd, here, there):
+    first = group == odd
     rows = here.shape[1]
     for k in range(2):
         mine, other = here[k], there[k]
@@ -129,11 +130,21 @@
 
 
 def first_kernel(
-    regions, where, cam, pnt, res, camera, points, keep, send, jx, px, vinv_out, gres_out
+    regions, where, cam_hbm, pnt_hbm, res_hbm, camera_hbm, points_hbm,
+    keep, send, jx, px, vinv_out, gres_out, index, res, cam, pnt, camera, points, sems,
 ):
+    pairs = [(points_hbm, points), (pnt_hbm, pnt), (res_hbm, res), (camera_hbm, camera), (cam_hbm, cam)]
+    copies = [pltpu.make_async_copy(a, b, sems.at[k]) for k, (a, b) in enumerate(pairs)]
+    for copy in copies:
+        copy.start()
     group, region, odd = position(where, regions)
-    low, block, slot = indices(regions, region, camera, points)
+    copies[0].wait()
+    slot = points[...]
     hot_p = onehot_of(slot)
+    for copy in copies[1:]:
+        copy.wait()
+    low, block = indices(regions, region, camera[...])
+    index[...] = jnp.concatenate([low, block, slot] + [jnp.zeros_like(low)] * 5, 0)
     camf = cam[...].astype(F32)
     pf = pnt[...].astype(F32)
     zero5 = jnp.zeros((5, OBS), F32)
@@ -293,12 +304,12 @@
 
 
 def start_kernel(
-    regions, where, here, there, camera, points, jx, px, vinv,
+    regions, where, here, there, index, jx, px, vinv,
     keep, send, factor, v_out, g_out, s_out, rem_out, scal, tiles, field,
 ):
     group, region, odd = position(where, regions)
-    low, block, slot = indices(regions, region, camera, points)
-    to_tiles(tiles, group, here, there)
+    low, block, slot = index[0:1, :], index[1:2, :], index[2:3, :]
+    to_tiles(tiles, group, odd, here, there)
     lower, inv = factor_camera(tiles, factor)
     b = [-tile(tiles, 48 + k) for k in range(8)] + [-tile(tiles, 37)]
     x = solve_camera(lower, inv, b)
@@ -321,12 +332,12 @@
 
 
 def next_kernel(
-    regions, where, here, there, factor, camera, points, jx, px, vinv, v_old, s_old, rem_old,
+    regions, where, here, there, factor, index, jx, px, vinv, v_old, s_old, rem_old,
     keep, send, v_out, g_out, s_out, rem_out, scal, tiles, field,
 ):
     group, region, odd = position(where, regions)
-    low, block, slot = indices(regions, region, camera, points)
-    to_tiles(tiles, group, here, there)
+    low, block, slot = index[0:1, :], index[1:2, :], index[2:3, :]
+    to_tiles(tiles, group, odd, here, there)
     x = solve_camera(*read_factor(factor), [tile(tiles, k) for k in range(9)])
     hot_c, v, u, g, s, ps = apply_body(
         group, odd, x, field, low, block, slot, jx, px, vinv
@@ -339,12 +350,12 @@
 
 
 def last_kernel(
-    regions, where, here, there, factor, camera, points, jx, px, vinv, v_old, s_old, rem_old,
+    regions, where, here, there, factor, index, jx, px, vinv, v_old, s_old, rem_old,
     scal0, scal1, v_out, g_out, sums, tiles, field,
 ):
     group, region, odd = position(where, regions)
-    low, block, slot = indices(regions, region, camera, points)
-    to_tiles(tiles, group, here, there)
+    low, block, slot = index[0:1, :], index[1:2, :], index[2:3, :]
+    to_tiles(tiles, group, odd, here, there)
     x = solve_camera(*read_factor(factor), [tile(tiles, k) for k in range(9)])
     hot_c, v, u, g, s, ps = apply_body(
         group, odd, x, field, low, block, slot, jx, px, vinv
@@ -401,8 +412,8 @@
     return jax.ShapeDtypeStruct(dims, dtype)
 
 
-def call(kernel, outs, *args, scalar=False, scratch=(), regions=None):
-    specs = [VMEM] * len(args)
+def call(kernel, outs, *args, scalar=False, scratch=(), regions=None, inputs=VMEM):
+    specs = [inputs] * len(args)
     if scalar:
         specs[0] = SMEM
     return pl.pallas_call(
@@ -423,13 +434,25 @@
     def both_ways(pairs):
         return pairs + [(b, a) for a, b in pairs]
 
+    def device(left, region):
+        return ((region & 1) ^ left) * regions + region
+
     cores = both_ways([(r, regions + r) for r in range(regions)])
     pair = both_ways(
-        [(g * regions + r, g * regions + r + 1) for g in range(2) for r in range(0, regions, 2)]
-    )
+        [(device(h, r), device(h, r + 1)) for h in range(2) for r in range(0, regions, 2)]
+    )
+    ends = [(device(1, 0), device(1, 1)), (device(0, regions - 2), device(0, regions - 1))]
     next_pair = both_ways(
-        [(r + i, regions + r + 3 - i) for r in range(0, regions - 2, 2) for i in range(2)]
-    )
+        [
+            (device(0, r + i), device(1, r + 3 - i))
+            for r in range(0, regions - 2, 2)
+            for i in range(2)
+        ]
+        + ends
+    )
+    group, region = lax.axis_index("grp"), lax.axis_index(REG)
+    right = group == region % 2
+    alone = jnp.where(right, region >= regions - 2, region < 2)
 
     def swap(x, pairs):
         return lax.ppermute(x, GRP_REG, pairs)
@@ -437,7 +460,8 @@
     def totals(keep, send):
         half = keep + swap(send, cores)
         half = half + swap(half, pair)
-        half = half + swap(half, next_pair)
+        got = swap(half, next_pair)
+        half = half + jnp.where(alone, 0.0, got)
         return half, swap(half, cores)
 
     def halves(rows):
@@ -448,12 +472,20 @@
     per_point = shape(8, P_DEV)
     rest = [shape(16, 128), per_point, per_point, shape(8, OBS), shape(8, 128)]
 
-    keep, send, jx, px, vinv, gres = run(
+    keep, send, jx, px, vinv, gres, index = run(
         first_kernel,
-        halves(ROWS) + [shape(2, 16, OBS), shape(2, 8, OBS), per_point, per_point],
+        halves(ROWS)
+        + [shape(2, 16, OBS), shape(2, 8, OBS), per_point, per_point]
+        + [shape(8, OBS, dtype=jnp.int32)],
         where, cam_jacobian, point_jacobian, residuals, camera, points,
-    )
-    common = (camera, points, jx, px, vinv)
+        scratch=[
+            pltpu.VMEM((2, OBS), F32), pltpu.VMEM((18, OBS), BF16), pltpu.VMEM((6, OBS), BF16),
+            pltpu.VMEM((1, OBS), jnp.int32), pltpu.VMEM((1, OBS), jnp.int32),
+            pltpu.SemaphoreType.DMA((5,)),
+        ],
+        inputs=HBM,
+    )
+    common = (index, jx, px, vinv)
     keep, send, factor, v0, g0, s0, rem0, scal0 = run(
         start_kernel,
         halves(16) + [shape(45 * 8, 128)] + rest,

time: 82.6 us -> 75.8 us (0.918)
  starting transfers between devices: 29 us -> 13.8 us
  waiting for transfers between devices: 13.6 us -> 24.7 us
  blocking collectives: 27.6 us -> 23.3 us
  local copies, waits for them, and re-layouts: 2.35 us -> 3.74 us
    ppermute x12, starting transfers between devices: 29 us -> 13.8 us  [swap(): return lax.ppermute(x, GRP_REG, pairs)]
    ppermute x12, waiting for transfers between devices: 13.6 us -> 24.7 us  [swap(): return lax.ppermute(x, GRP_REG, pairs)]
    all_to_all x1, blocking collectives: 27.6 us -> 23.3 us  [local(): back = lax.all_to_all(sums, GRP_REG, 0, 0, tiled=True)]
    unnamed x10, local copies, waits for them, and re-layouts: 2.35 us -> 3.74 us
  transfers between devices with their start and end apart: 12 -> 12, of which waited for: 9 -> 12; matrix products, arithmetic and copies ran while one was open for 0% -> 0% of each run, Pallas kernels for 0% -> 0%
where the time goes in v3:
time: 75.8 us; the launch traced here: 75.5 us
  waiting for transfers between devices  24.7 us (33%)
  blocking collectives  23.3 us (31%)
  starting transfers between devices  13.8 us (18%)
  Pallas kernels  9.18 us (12%)
  local copies, waits for them, and re-layouts  3.74 us (5%)
    ppermute x12, waiting for transfers between devices, swap(): return lax.ppermute(x, GRP_REG, pairs)  24.7 us
    all_to_all x1, blocking collectives, local(): back = lax.all_to_all(sums, GRP_REG, 0, 0, tiled=True)  23.3 us
    ppermute x12, starting transfers between devices, swap(): return lax.ppermute(x, GRP_REG, pairs)  13.8 us
    pallas_call x5, Pallas kernels, call(): pl.pallas_call(kernel if regions is None else functools.partial(kernel, r...  9.18 us
    unnamed x10, local copies, waits for them, and re-layouts  3.74 us
  transfers between devices with their start and end apart: 12, of which 12 were waited for; matrix products, arithmetic and copies ran while one was open for 0% of the time, Pallas kernels for 0%

profile of v3, /device:TPU:1, one launch (start us, length us, event | category | flops | bytes accessed | tf_op | source)
XLA Modules:
  0.0 75.5 jit_solution(16349286725468779585)
XLA Ops:
  0.7 0.7 copy-done.1
  1.4 0.9 %copy-done = bf16[18,2048]{1,0:T(8,128)(2,1)S(1)} copy-done((bf16[18,2048]{1,0:T(8,128)(2,1)S(1)}, bf16[18,2048]{1,0:T(8,128)(2,1)}, u32[]{:S(2)}) %copy-start) | copy-done | bytes 73752
  2.3 0.7 copy-done.2
  3.0 0.7 copy-done.3
  3.7 0.7 copy-done.4
  4.4 2.7 %first_kernel.1 = (f32[2,56,256]{2,1,0:T(8,128)S(1)}, f32[2,56,256]{2,1,0:T(8,128)S(1)}, f32[2,16,2048]{2,1,0:T(8,128)S(1)}, f32[2,8,2048]{2,1,0:T(8,128)S(1)}, ...) custom-call(s32[1]{0:T(128)} %bitcast.where, bf16[18,2048]{1,0:T(8,128)(2,1)S(1)} %copy-done, ...), custom_call_target="tpu_custom_call" | custom-call | tf_op jit(solution)/shard_map/first_kernel/pallas_call | solution.py:419
  7.1 1.5 %collective-permute-start = (f32[2,56,256]{2,1,0:T(8,128)S(1)}, f32[2,56,256]{2,1,0:T(8,128)S(1)}, u32[]{:S(2)}, u32[]{:S(2)}) collective-permute-start(f32[2,56,256]{2,1,0:T(8,128)S(1)} %get-tuple-element.28), channel_id=1, source_target_pairs={{0,64},{1,65},{2,66},{3,67},{4,68},{5,69},{6,70},{7,71},{8,72},{9,... | collective-permute-start | bytes 344072 | tf_op jit(solution)/shard_map/ppermute | solution.py:458
  8.6 1.0 %collective-permute-done = f32[2,56,256]{2,1,0:T(8,128)S(1)} collective-permute-done((f32[2,56,256]{2,1,0:T(8,128)S(1)}, f32[2,56,256]{2,1,0:T(8,128)S(1)}, u32[]{:S(2)}, u32[]{:S(2)}) %collective-permute-start) | collective-permute-done | bytes 114720 | tf_op jit(solution)/shard_map/ppermute | solution.py:458
  9.6 1.7 %collective-permute-start.1 = (f32[2,56,256]{2,1,0:T(8,128)S(1)}, f32[2,56,256]{2,1,0:T(8,128)S(1)}, u32[]{:S(2)}, u32[]{:S(2)}) collective-permute-start(f32[2,56,256]{2,1,0:T(8,128)S(1)} %add.45), channel_id=1, source_target_pairs={{0,65},{2,67},{4,69},{6,71},{8,73},{10,75},{12,77},{14,79},{16,81}... | collective-permute-start | bytes 344072 | tf_op jit(solution)/shard_map/ppermute | solution.py:458
  11.3 3.5 %collective-permute-done.1 = f32[2,56,256]{2,1,0:T(8,128)S(1)} collective-permute-done((f32[2,56,256]{2,1,0:T(8,128)S(1)}, f32[2,56,256]{2,1,0:T(8,128)S(1)}, u32[]{:S(2)}, u32[]{:S(2)}) %collective-permute-start.1) | collective-permute-done | bytes 114720 | tf_op jit(solution)/shard_map/ppermute | solution.py:458
  14.8 1.7 %collective-permute-start.2 = (f32[2,56,256]{2,1,0:T(8,128)S(1)}, f32[2,56,256]{2,1,0:T(8,128)S(1)}, u32[]{:S(2)}, u32[]{:S(2)}) collective-permute-start(f32[2,56,256]{2,1,0:T(8,128)S(1)} %add.46), channel_id=1, source_target_pairs={{0,3},{65,66},{2,5},{67,68},{4,7},{69,70},{6,9},{71,72},{8,11},{73... | collective-permute-start | bytes 344072 | tf_op jit(solution)/shard_map/ppermute | solution.py:458
  16.5 2.6 %collective-permute-done.2 = f32[2,56,256]{2,1,0:T(8,128)S(1)} collective-permute-done((f32[2,56,256]{2,1,0:T(8,128)S(1)}, f32[2,56,256]{2,1,0:T(8,128)S(1)}, u32[]{:S(2)}, u32[]{:S(2)}) %collective-permute-start.2) | collective-permute-done | bytes 114720 | tf_op jit(solution)/shard_map/ppermute | solution.py:458
  19.1 2.9 %collective-permute-start.3 = (f32[2,56,256]{2,1,0:T(8,128)S(1)}, f32[2,56,256]{2,1,0:T(8,128)S(1)}, u32[]{:S(2)}, u32[]{:S(2)}) collective-permute-start(f32[2,56,256]{2,1,0:T(8,128)S(1)} %select_add_fusion.here), channel_id=1, source_target_pairs={{0,64},{1,65},{2,66},{3,67},{4,68},{5,69},{6,70},{7,71},{8,72},{9,... | collective-permute-start | bytes 344072 | tf_op jit(solution)/shard_map/ppermute | solution.py:458
  22.0 1.0 %collective-permute-done.3.there = f32[2,56,256]{2,1,0:T(8,128)S(1)} collective-permute-done((f32[2,56,256]{2,1,0:T(8,128)S(1)}, f32[2,56,256]{2,1,0:T(8,128)S(1)}, u32[]{:S(2)}, u32[]{:S(2)}) %collective-permute-start.3) | collective-permute-done | bytes 114720 | tf_op jit(solution)/shard_map/ppermute | solution.py:458
  23.0 2.0 %start_kernel.1 = (f32[2,16,256]{2,1,0:T(8,128)S(1)}, f32[2,16,256]{2,1,0:T(8,128)S(1)}, f32[360,128]{1,0:T(8,128)S(1)}, f32[16,128]{1,0:T(8,128)S(1)}, f32[8,25...) custom-call(s32[1]{0:T(128)} %bitcast.where, ...), custom_call_target="tpu_custom_call" | custom-call | tf_op jit(solution)/shard_map/start_kernel/pallas_call | solution.py:419
  24.9 0.4 collective-permute-start.4
  25.4 0.9 %collective-permute-done.4 = f32[2,16,256]{2,1,0:T(8,128)S(1)} collective-permute-done((f32[2,16,256]{2,1,0:T(8,128)S(1)}, f32[2,16,256]{2,1,0:T(8,128)S(1)}, u32[]{:S(2)}, u32[]{:S(2)}) %collective-permute-start.4) | collective-permute-done | bytes 32800 | tf_op jit(solution)/shard_map/ppermute | solution.py:458
  26.3 3.3 %collective-permute-done.5 = f32[2,16,256]{2,1,0:T(8,128)S(1)} collective-permute-done((f32[2,16,256]{2,1,0:T(8,128)S(1)}, f32[2,16,256]{2,1,0:T(8,128)S(1)}, u32[]{:S(2)}, u32[]{:S(2)}) %collective-permute-start.5) | collective-permute-done | bytes 32800 | tf_op jit(solution)/shard_map/ppermute | solution.py:458
  29.6 3.3 %collective-permute-done.6 = f32[2,16,256]{2,1,0:T(8,128)S(1)} collective-permute-done((f32[2,16,256]{2,1,0:T(8,128)S(1)}, f32[2,16,256]{2,1,0:T(8,128)S(1)}, u32[]{:S(2)}, u32[]{:S(2)}) %collective-permute-start.6) | collective-permute-done | bytes 32800 | tf_op jit(solution)/shard_map/ppermute | solution.py:458
  32.9 2.6 %collective-permute-start.7 = (f32[2,16,256]{2,1,0:T(8,128)S(1)}, f32[2,16,256]{2,1,0:T(8,128)S(1)}, u32[]{:S(2)}, u32[]{:S(2)}) collective-permute-start(f32[2,16,256]{2,1,0:T(8,128)S(1)} %select_add_fusion.2.here), channel_id=1, source_target_pairs={{0,64},{1,65},{2,66},{3,67},{4,68},{5,69},{6,70},{7,71},{8,72},{9,... | collective-permute-start | bytes 98312 | tf_op jit(solution)/shard_map/ppermute | solution.py:458
  35.5 0.9 %collective-permute-done.7.there = f32[2,16,256]{2,1,0:T(8,128)S(1)} collective-permute-done((f32[2,16,256]{2,1,0:T(8,128)S(1)}, f32[2,16,256]{2,1,0:T(8,128)S(1)}, u32[]{:S(2)}, u32[]{:S(2)}) %collective-permute-start.7) | collective-permute-done | bytes 32800 | tf_op jit(solution)/shard_map/ppermute | solution.py:458
  36.4 1.9 %next_kernel.1 = (f32[2,16,256]{2,1,0:T(8,128)S(1)}, f32[2,16,256]{2,1,0:T(8,128)S(1)}, f32[16,128]{1,0:T(8,128)S(1)}, f32[8,256]{1,0:T(8,128)S(1)}, f32[8,256]{...) custom-call(s32[1]{0:T(128)} %bitcast.where, f32[2,16,256]{2,1,0:T(8,128)S(1)} %select_add_fusion.2.here, ...), custom_call_target="tpu_custom_call" | custom-call | tf_op jit(solution)/shard_map/next_kernel/pallas_call | solution.py:419
  38.3 0.4 collective-permute-start.8
  38.7 0.9 %collective-permute-done.8 = f32[2,16,256]{2,1,0:T(8,128)S(1)} collective-permute-done((f32[2,16,256]{2,1,0:T(8,128)S(1)}, f32[2,16,256]{2,1,0:T(8,128)S(1)}, u32[]{:S(2)}, u32[]{:S(2)}) %collective-permute-start.8) | collective-permute-done | bytes 32800 | tf_op jit(solution)/shard_map/ppermute | solution.py:458
  39.6 0.0 collective-permute-start.9
  39.6 3.3 %collective-permute-done.9 = f32[2,16,256]{2,1,0:T(8,128)S(1)} collective-permute-done((f32[2,16,256]{2,1,0:T(8,128)S(1)}, f32[2,16,256]{2,1,0:T(8,128)S(1)}, u32[]{:S(2)}, u32[]{:S(2)}) %collective-permute-start.9) | collective-permute-done | bytes 32800 | tf_op jit(solution)/shard_map/ppermute | solution.py:458
  42.9 3.3 %collective-permute-done.10 = f32[2,16,256]{2,1,0:T(8,128)S(1)} collective-permute-done((f32[2,16,256]{2,1,0:T(8,128)S(1)}, f32[2,16,256]{2,1,0:T(8,128)S(1)}, u32[]{:S(2)}, u32[]{:S(2)}) %collective-permute-start.10) | collective-permute-done | bytes 32800 | tf_op jit(solution)/shard_map/ppermute | solution.py:458
  46.3 2.5 %collective-permute-start.11 = (f32[2,16,256]{2,1,0:T(8,128)S(1)}, f32[2,16,256]{2,1,0:T(8,128)S(1)}, u32[]{:S(2)}, u32[]{:S(2)}) collective-permute-start(f32[2,16,256]{2,1,0:T(8,128)S(1)} %select_add_fusion.1.here), channel_id=1, source_target_pairs={{0,64},{1,65},{2,66},{3,67},{4,68},{5,69},{6,70},{7,71},{8,72},{9,... | collective-permute-start | bytes 98312 | tf_op jit(solution)/shard_map/ppermute | solution.py:458
  48.8 0.9 %collective-permute-done.11.there = f32[2,16,256]{2,1,0:T(8,128)S(1)} collective-permute-done((f32[2,16,256]{2,1,0:T(8,128)S(1)}, f32[2,16,256]{2,1,0:T(8,128)S(1)}, u32[]{:S(2)}, u32[]{:S(2)}) %collective-permute-start.11) | collective-permute-done | bytes 32800 | tf_op jit(solution)/shard_map/ppermute | solution.py:458
  49.6 1.5 %last_kernel.1 = (f32[16,128]{1,0:T(8,128)S(1)}, f32[8,256]{1,0:T(8,128)S(1)}, f32[128,32]{1,0:T(8,128)S(1)}) custom-call(s32[1]{0:T(128)} %bitcast.where, f32[2,16,256]{2,1,0:T(8,128)S(1)} %select_add_fusion.1.here, f32[2,16,256]{2,1,0:T(8,128)S(1)} %collective-permute-done.11.there, f32[360,128]{1,0:T(8,128)S(1)} %get-tuple-element.35.factor, ...), custom_call_target="tpu_custom_call" | custom-call | tf_op jit(solution)/shard_map/last_kernel/pallas_call | solution.py:419
  51.1 23.3 %all_to_all.11 = f32[128,1,32]{2,1,0:T(1,128)S(1)} all-to-all(f32[128,1,32]{2,1,0:T(1,128)S(1)} %bitcast.8), channel_id=1, replica_groups=mesh['grp'=2,'reg_0'=4,'reg_1'=4,'reg_2'=4] {'grp','reg_0','reg_1','reg_2'}, dimensions={0} | all-to-all | bytes 32768 | tf_op jit(solution)/shard_map/all_to_all | solution.py:507
  74.3 1.2 %final_kernel.1 = (f32[9,128]{1,0:T(8,128)}, f32[3,256]{1,0:T(4,128)}) custom-call(f32[128,32]{1,0:T(8,128)S(1)} %bitcast.7, f32[16,128]{1,0:T(8,128)S(1)} %get-tuple-element.36.v_old.v0, f32[16,128]{1,0:T(8,128)S(1)} %get-tuple-element.41.v_old.v1, f32[16,128]{1,0:T(8,128)S(1)} %get-tuple-element.47.v2, f32[8,256]{1,0:T(8,128)S(1)} %get-tuple-element.48.g0, ...), custom_call_target="tpu_custom_call" | custom-call | tf_op jit(solution)/shard_map/final_kernel/pallas_call | solution.py:419
  (17 shorter events, 0.1 us)
Async XLA Ops:
  0.6 0.8 %copy-start.1 = (bf16[6,2048]{1,0:T(8,128)(2,1)S(1)}, bf16[6,2048]{1,0:T(8,128)(2,1)}, u32[]{:S(2)}) copy-start(bf16[6,2048]{1,0:T(8,128)(2,1)} %pnt_hbm.1) | copy-start | bytes 73732
  1.4 0.9 %copy-start = (bf16[18,2048]{1,0:T(8,128)(2,1)S(1)}, bf16[18,2048]{1,0:T(8,128)(2,1)}, u32[]{:S(2)}) copy-start(bf16[18,2048]{1,0:T(8,128)(2,1)} %cam_hbm.1) | copy-start | bytes 221188
  2.3 0.7 copy-start.2
  3.0 0.7 copy-start.3
  3.7 0.7 copy-start.4
  7.1 2.4 %collective-permute-start = (f32[2,56,256]{2,1,0:T(8,128)S(1)}, f32[2,56,256]{2,1,0:T(8,128)S(1)}, u32[]{:S(2)}, u32[]{:S(2)}) collective-permute-start(f32[2,56,256]{2,1,0:T(8,128)S(1)} %get-tuple-element.28), channel_id=1, source_target_pairs={{0,64},{1,65},{2,66},{3,67},{4,68},{5,69},{6,70},{7,71},{8,72},{9,... | collective-permute-start | bytes 344072 | tf_op jit(solution)/shard_map/ppermute | solution.py:458
  9.6 5.2 %collective-permute-start.1 = (f32[2,56,256]{2,1,0:T(8,128)S(1)}, f32[2,56,256]{2,1,0:T(8,128)S(1)}, u32[]{:S(2)}, u32[]{:S(2)}) collective-permute-start(f32[2,56,256]{2,1,0:T(8,128)S(1)} %add.45), channel_id=1, source_target_pairs={{0,65},{2,67},{4,69},{6,71},{8,73},{10,75},{12,77},{14,79},{16,81}... | collective-permute-start | bytes 344072 | tf_op jit(solution)/shard_map/ppermute | solution.py:458
  14.8 4.3 %collective-permute-start.2 = (f32[2,56,256]{2,1,0:T(8,128)S(1)}, f32[2,56,256]{2,1,0:T(8,128)S(1)}, u32[]{:S(2)}, u32[]{:S(2)}) collective-permute-start(f32[2,56,256]{2,1,0:T(8,128)S(1)} %add.46), channel_id=1, source_target_pairs={{0,3},{65,66},{2,5},{67,68},{4,7},{69,70},{6,9},{71,72},{8,11},{73... | collective-permute-start | bytes 344072 | tf_op jit(solution)/shard_map/ppermute | solution.py:458
  19.1 3.9 %collective-permute-start.3 = (f32[2,56,256]{2,1,0:T(8,128)S(1)}, f32[2,56,256]{2,1,0:T(8,128)S(1)}, u32[]{:S(2)}, u32[]{:S(2)}) collective-permute-start(f32[2,56,256]{2,1,0:T(8,128)S(1)} %select_add_fusion.here), channel_id=1, source_target_pairs={{0,64},{1,65},{2,66},{3,67},{4,68},{5,69},{6,70},{7,71},{8,72},{9,... | collective-permute-start | bytes 344072 | tf_op jit(solution)/shard_map/ppermute | solution.py:458
  24.9 1.3 %collective-permute-start.4 = (f32[2,16,256]{2,1,0:T(8,128)S(1)}, f32[2,16,256]{2,1,0:T(8,128)S(1)}, u32[]{:S(2)}, u32[]{:S(2)}) collective-permute-start(f32[2,16,256]{2,1,0:T(8,128)S(1)} %get-tuple-element.34), channel_id=1, source_target_pairs={{0,64},{1,65},{2,66},{3,67},{4,68},{5,69},{6,70},{7,71},{8,72},{9,... | collective-permute-start | bytes 98312 | tf_op jit(solution)/shard_map/ppermute | solution.py:458
  26.2 3.3 %collective-permute-start.5 = (f32[2,16,256]{2,1,0:T(8,128)S(1)}, f32[2,16,256]{2,1,0:T(8,128)S(1)}, u32[]{:S(2)}, u32[]{:S(2)}) collective-permute-start(f32[2,16,256]{2,1,0:T(8,128)S(1)} %add.49), channel_id=1, source_target_pairs={{0,65},{2,67},{4,69},{6,71},{8,73},{10,75},{12,77},{14,79},{16,81}... | collective-permute-start | bytes 98312 | tf_op jit(solution)/shard_map/ppermute | solution.py:458
  29.6 3.3 %collective-permute-start.6 = (f32[2,16,256]{2,1,0:T(8,128)S(1)}, f32[2,16,256]{2,1,0:T(8,128)S(1)}, u32[]{:S(2)}, u32[]{:S(2)}) collective-permute-start(f32[2,16,256]{2,1,0:T(8,128)S(1)} %add.50), channel_id=1, source_target_pairs={{0,3},{65,66},{2,5},{67,68},{4,7},{69,70},{6,9},{71,72},{8,11},{73... | collective-permute-start | bytes 98312 | tf_op jit(solution)/shard_map/ppermute | solution.py:458
  32.9 3.4 %collective-permute-start.7 = (f32[2,16,256]{2,1,0:T(8,128)S(1)}, f32[2,16,256]{2,1,0:T(8,128)S(1)}, u32[]{:S(2)}, u32[]{:S(2)}) collective-permute-start(f32[2,16,256]{2,1,0:T(8,128)S(1)} %select_add_fusion.2.here), channel_id=1, source_target_pairs={{0,64},{1,65},{2,66},{3,67},{4,68},{5,69},{6,70},{7,71},{8,72},{9,... | collective-permute-start | bytes 98312 | tf_op jit(solution)/shard_map/ppermute | solution.py:458
  38.3 1.3 %collective-permute-start.8 = (f32[2,16,256]{2,1,0:T(8,128)S(1)}, f32[2,16,256]{2,1,0:T(8,128)S(1)}, u32[]{:S(2)}, u32[]{:S(2)}) collective-permute-start(f32[2,16,256]{2,1,0:T(8,128)S(1)} %get-tuple-element.40), channel_id=1, source_target_pairs={{0,64},{1,65},{2,66},{3,67},{4,68},{5,69},{6,70},{7,71},{8,72},{9,... | collective-permute-start | bytes 98312 | tf_op jit(solution)/shard_map/ppermute | solution.py:458
  39.6 3.3 %collective-permute-start.9 = (f32[2,16,256]{2,1,0:T(8,128)S(1)}, f32[2,16,256]{2,1,0:T(8,128)S(1)}, u32[]{:S(2)}, u32[]{:S(2)}) collective-permute-start(f32[2,16,256]{2,1,0:T(8,128)S(1)} %add.52), channel_id=1, source_target_pairs={{0,65},{2,67},{4,69},{6,71},{8,73},{10,75},{12,77},{14,79},{16,81}... | collective-permute-start | bytes 98312 | tf_op jit(solution)/shard_map/ppermute | solution.py:458
  42.9 3.3 %collective-permute-start.10 = (f32[2,16,256]{2,1,0:T(8,128)S(1)}, f32[2,16,256]{2,1,0:T(8,128)S(1)}, u32[]{:S(2)}, u32[]{:S(2)}) collective-permute-start(f32[2,16,256]{2,1,0:T(8,128)S(1)} %add.53), channel_id=1, source_target_pairs={{0,3},{65,66},{2,5},{67,68},{4,7},{69,70},{6,9},{71,72},{8,11},{73... | collective-permute-start | bytes 98312 | tf_op jit(solution)/shard_map/ppermute | solution.py:458
  46.3 3.3 %collective-permute-start.11 = (f32[2,16,256]{2,1,0:T(8,128)S(1)}, f32[2,16,256]{2,1,0:T(8,128)S(1)}, u32[]{:S(2)}, u32[]{:S(2)}) collective-permute-start(f32[2,16,256]{2,1,0:T(8,128)S(1)} %select_add_fusion.1.here), channel_id=1, source_target_pairs={{0,64},{1,65},{2,66},{3,67},{4,68},{5,69},{6,70},{7,71},{8,72},{9,... | collective-permute-start | bytes 98312 | tf_op jit(solution)/shard_map/ppermute | solution.py:458

commit v4 on v3

--- a/solution.py
+++ b/solution.py
@@ -429,7 +429,9 @@
 
 def local(regions, cam_jacobian, point_jacobian, residuals, obs_camera, obs_point):
     where = (lax.axis_index("grp") * regions + lax.axis_index(REG)).reshape(1)
-    camera, points = obs_camera.reshape(1, OBS), obs_point.reshape(1, OBS)
+    arrays = (cam_jacobian, point_jacobian, residuals)
+    arrays += (obs_camera.reshape(1, OBS), obs_point.reshape(1, OBS))
+    arrays = [pltpu.with_memory_space_constraint(x, pltpu.HBM) for x in arrays]
 
     def both_ways(pairs):
         return pairs + [(b, a) for a, b in pairs]
@@ -477,7 +479,7 @@
         halves(ROWS)
         + [shape(2, 16, OBS), shape(2, 8, OBS), per_point, per_point]
         + [shape(8, OBS, dtype=jnp.int32)],
-        where, cam_jacobian, point_jacobian, residuals, camera, points,
+        where, *arrays,
         scratch=[
             pltpu.VMEM((2, OBS), F32), pltpu.VMEM((18, OBS), BF16), pltpu.VMEM((6, OBS), BF16),
             pltpu.VMEM((1, OBS), jnp.int32), pltpu.VMEM((1, OBS), jnp.int32),

time: 75.8 us -> 72.4 us (0.955)
  local copies, waits for them, and re-layouts: 3.74 us -> 0 us
    unnamed x10 -> x0, local copies, waits for them, and re-layouts: 3.74 us -> none
where the time goes in v4:
time: 72.4 us; the launch traced here: 72.3 us
  waiting for transfers between devices  24.7 us (34%)
  blocking collectives  23.3 us (32%)
  starting transfers between devices  13.7 us (19%)
  Pallas kernels  9.71 us (13%)
    ppermute x12, waiting for transfers between devices, swap(): return lax.ppermute(x, GRP_REG, pairs)  24.7 us
    all_to_all x1, blocking collectives, local(): back = lax.all_to_all(sums, GRP_REG, 0, 0, tiled=True)  23.3 us
    ppermute x12, starting transfers between devices, swap(): return lax.ppermute(x, GRP_REG, pairs)  13.7 us
    pallas_call x5, Pallas kernels, call(): pl.pallas_call(kernel if regions is None else functools.partial(kernel, r...  9.71 us
  transfers between devices with their start and end apart: 12, of which 12 were waited for; matrix products, arithmetic and copies ran while one was open for 0% of the time, Pallas kernels for 0%

profile of v4, /device:TPU:1, one launch (start us, length us, event | category | flops | bytes accessed | tf_op | source)
XLA Modules:
  0.0 72.3 jit_solution(10372548827080076418)
XLA Ops:
  0.6 3.2 %first_kernel.1 = (f32[2,56,256]{2,1,0:T(8,128)S(1)}, f32[2,56,256]{2,1,0:T(8,128)S(1)}, f32[2,16,2048]{2,1,0:T(8,128)S(1)}, f32[2,8,2048]{2,1,0:T(8,128)S(1)}, ...) custom-call(s32[1]{0:T(128)} %bitcast.where, bf16[18,2048]{1,0:T(8,128)(2,1)} %cam_hbm.1, ...), custom_call_target="tpu_custom_call" | custom-call | tf_op jit(solution)/shard_map/first_kernel/pallas_call | solution.py:419
  3.9 1.5 %collective-permute-start = (f32[2,56,256]{2,1,0:T(8,128)S(1)}, f32[2,56,256]{2,1,0:T(8,128)S(1)}, u32[]{:S(2)}, u32[]{:S(2)}) collective-permute-start(f32[2,56,256]{2,1,0:T(8,128)S(1)} %get-tuple-element.28), channel_id=1, source_target_pairs={{0,64},{1,65},{2,66},{3,67},{4,68},{5,69},{6,70},{7,71},{8,72},{9,... | collective-permute-start | bytes 344072 | tf_op jit(solution)/shard_map/ppermute | solution.py:460
  5.3 1.0 %collective-permute-done = f32[2,56,256]{2,1,0:T(8,128)S(1)} collective-permute-done((f32[2,56,256]{2,1,0:T(8,128)S(1)}, f32[2,56,256]{2,1,0:T(8,128)S(1)}, u32[]{:S(2)}, u32[]{:S(2)}) %collective-permute-start) | collective-permute-done | bytes 114720 | tf_op jit(solution)/shard_map/ppermute | solution.py:460
  6.3 1.7 %collective-permute-start.1 = (f32[2,56,256]{2,1,0:T(8,128)S(1)}, f32[2,56,256]{2,1,0:T(8,128)S(1)}, u32[]{:S(2)}, u32[]{:S(2)}) collective-permute-start(f32[2,56,256]{2,1,0:T(8,128)S(1)} %add.45), channel_id=1, source_target_pairs={{0,65},{2,67},{4,69},{6,71},{8,73},{10,75},{12,77},{14,79},{16,81}... | collective-permute-start | bytes 344072 | tf_op jit(solution)/shard_map/ppermute | solution.py:460
  8.1 3.5 %collective-permute-done.1 = f32[2,56,256]{2,1,0:T(8,128)S(1)} collective-permute-done((f32[2,56,256]{2,1,0:T(8,128)S(1)}, f32[2,56,256]{2,1,0:T(8,128)S(1)}, u32[]{:S(2)}, u32[]{:S(2)}) %collective-permute-start.1) | collective-permute-done | bytes 114720 | tf_op jit(solution)/shard_map/ppermute | solution.py:460
  11.5 1.7 %collective-permute-start.2 = (f32[2,56,256]{2,1,0:T(8,128)S(1)}, f32[2,56,256]{2,1,0:T(8,128)S(1)}, u32[]{:S(2)}, u32[]{:S(2)}) collective-permute-start(f32[2,56,256]{2,1,0:T(8,128)S(1)} %add.46), channel_id=1, source_target_pairs={{0,3},{65,66},{2,5},{67,68},{4,7},{69,70},{6,9},{71,72},{8,11},{73... | collective-permute-start | bytes 344072 | tf_op jit(solution)/shard_map/ppermute | solution.py:460
  13.3 2.6 %collective-permute-done.2 = f32[2,56,256]{2,1,0:T(8,128)S(1)} collective-permute-done((f32[2,56,256]{2,1,0:T(8,128)S(1)}, f32[2,56,256]{2,1,0:T(8,128)S(1)}, u32[]{:S(2)}, u32[]{:S(2)}) %collective-permute-start.2) | collective-permute-done | bytes 114720 | tf_op jit(solution)/shard_map/ppermute | solution.py:460
  15.9 2.9 %collective-permute-start.3 = (f32[2,56,256]{2,1,0:T(8,128)S(1)}, f32[2,56,256]{2,1,0:T(8,128)S(1)}, u32[]{:S(2)}, u32[]{:S(2)}) collective-permute-start(f32[2,56,256]{2,1,0:T(8,128)S(1)} %select_add_fusion.here), channel_id=1, source_target_pairs={{0,64},{1,65},{2,66},{3,67},{4,68},{5,69},{6,70},{7,71},{8,72},{9,... | collective-permute-start | bytes 344072 | tf_op jit(solution)/shard_map/ppermute | solution.py:460
  18.8 1.0 %collective-permute-done.3.there = f32[2,56,256]{2,1,0:T(8,128)S(1)} collective-permute-done((f32[2,56,256]{2,1,0:T(8,128)S(1)}, f32[2,56,256]{2,1,0:T(8,128)S(1)}, u32[]{:S(2)}, u32[]{:S(2)}) %collective-permute-start.3) | collective-permute-done | bytes 114720 | tf_op jit(solution)/shard_map/ppermute | solution.py:460
  19.7 2.0 %start_kernel.1 = (f32[2,16,256]{2,1,0:T(8,128)S(1)}, f32[2,16,256]{2,1,0:T(8,128)S(1)}, f32[360,128]{1,0:T(8,128)S(1)}, f32[16,128]{1,0:T(8,128)S(1)}, f32[8,25...) custom-call(s32[1]{0:T(128)} %bitcast.where, ...), custom_call_target="tpu_custom_call" | custom-call | tf_op jit(solution)/shard_map/start_kernel/pallas_call | solution.py:419
  21.7 0.4 collective-permute-start.4
  22.2 0.9 %collective-permute-done.4 = f32[2,16,256]{2,1,0:T(8,128)S(1)} collective-permute-done((f32[2,16,256]{2,1,0:T(8,128)S(1)}, f32[2,16,256]{2,1,0:T(8,128)S(1)}, u32[]{:S(2)}, u32[]{:S(2)}) %collective-permute-start.4) | collective-permute-done | bytes 32800 | tf_op jit(solution)/shard_map/ppermute | solution.py:460
  23.0 0.0 collective-permute-start.5
  23.0 3.3 %collective-permute-done.5 = f32[2,16,256]{2,1,0:T(8,128)S(1)} collective-permute-done((f32[2,16,256]{2,1,0:T(8,128)S(1)}, f32[2,16,256]{2,1,0:T(8,128)S(1)}, u32[]{:S(2)}, u32[]{:S(2)}) %collective-permute-start.5) | collective-permute-done | bytes 32800 | tf_op jit(solution)/shard_map/ppermute | solution.py:460
  26.4 0.0 collective-permute-start.6
  26.4 3.3 %collective-permute-done.6 = f32[2,16,256]{2,1,0:T(8,128)S(1)} collective-permute-done((f32[2,16,256]{2,1,0:T(8,128)S(1)}, f32[2,16,256]{2,1,0:T(8,128)S(1)}, u32[]{:S(2)}, u32[]{:S(2)}) %collective-permute-start.6) | collective-permute-done | bytes 32800 | tf_op jit(solution)/shard_map/ppermute | solution.py:460
  29.7 2.6 %collective-permute-start.7 = (f32[2,16,256]{2,1,0:T(8,128)S(1)}, f32[2,16,256]{2,1,0:T(8,128)S(1)}, u32[]{:S(2)}, u32[]{:S(2)}) collective-permute-start(f32[2,16,256]{2,1,0:T(8,128)S(1)} %select_add_fusion.2.here), channel_id=1, source_target_pairs={{0,64},{1,65},{2,66},{3,67},{4,68},{5,69},{6,70},{7,71},{8,72},{9,... | collective-permute-start | bytes 98312 | tf_op jit(solution)/shard_map/ppermute | solution.py:460
  32.3 0.9 %collective-permute-done.7.there = f32[2,16,256]{2,1,0:T(8,128)S(1)} collective-permute-done((f32[2,16,256]{2,1,0:T(8,128)S(1)}, f32[2,16,256]{2,1,0:T(8,128)S(1)}, u32[]{:S(2)}, u32[]{:S(2)}) %collective-permute-start.7) | collective-permute-done | bytes 32800 | tf_op jit(solution)/shard_map/ppermute | solution.py:460
  33.1 1.9 %next_kernel.1 = (f32[2,16,256]{2,1,0:T(8,128)S(1)}, f32[2,16,256]{2,1,0:T(8,128)S(1)}, f32[16,128]{1,0:T(8,128)S(1)}, f32[8,256]{1,0:T(8,128)S(1)}, f32[8,256]{...) custom-call(s32[1]{0:T(128)} %bitcast.where, f32[2,16,256]{2,1,0:T(8,128)S(1)} %select_add_fusion.2.here, ...), custom_call_target="tpu_custom_call" | custom-call | tf_op jit(solution)/shard_map/next_kernel/pallas_call | solution.py:419
  35.0 0.4 collective-permute-start.8
  35.5 0.9 %collective-permute-done.8 = f32[2,16,256]{2,1,0:T(8,128)S(1)} collective-permute-done((f32[2,16,256]{2,1,0:T(8,128)S(1)}, f32[2,16,256]{2,1,0:T(8,128)S(1)}, u32[]{:S(2)}, u32[]{:S(2)}) %collective-permute-start.8) | collective-permute-done | bytes 32800 | tf_op jit(solution)/shard_map/ppermute | solution.py:460
  36.3 0.0 collective-permute-start.9
  36.3 3.3 %collective-permute-done.9 = f32[2,16,256]{2,1,0:T(8,128)S(1)} collective-permute-done((f32[2,16,256]{2,1,0:T(8,128)S(1)}, f32[2,16,256]{2,1,0:T(8,128)S(1)}, u32[]{:S(2)}, u32[]{:S(2)}) %collective-permute-start.9) | collective-permute-done | bytes 32800 | tf_op jit(solution)/shard_map/ppermute | solution.py:460
  39.7 0.0 collective-permute-start.10
  39.7 3.3 %collective-permute-done.10 = f32[2,16,256]{2,1,0:T(8,128)S(1)} collective-permute-done((f32[2,16,256]{2,1,0:T(8,128)S(1)}, f32[2,16,256]{2,1,0:T(8,128)S(1)}, u32[]{:S(2)}, u32[]{:S(2)}) %collective-permute-start.10) | collective-permute-done | bytes 32800 | tf_op jit(solution)/shard_map/ppermute | solution.py:460
  43.0 2.5 %collective-permute-start.11 = (f32[2,16,256]{2,1,0:T(8,128)S(1)}, f32[2,16,256]{2,1,0:T(8,128)S(1)}, u32[]{:S(2)}, u32[]{:S(2)}) collective-permute-start(f32[2,16,256]{2,1,0:T(8,128)S(1)} %select_add_fusion.1.here), channel_id=1, source_target_pairs={{0,64},{1,65},{2,66},{3,67},{4,68},{5,69},{6,70},{7,71},{8,72},{9,... | collective-permute-start | bytes 98312 | tf_op jit(solution)/shard_map/ppermute | solution.py:460
  45.5 0.9 %collective-permute-done.11.there = f32[2,16,256]{2,1,0:T(8,128)S(1)} collective-permute-done((f32[2,16,256]{2,1,0:T(8,128)S(1)}, f32[2,16,256]{2,1,0:T(8,128)S(1)}, u32[]{:S(2)}, u32[]{:S(2)}) %collective-permute-start.11) | collective-permute-done | bytes 32800 | tf_op jit(solution)/shard_map/ppermute | solution.py:460
  46.4 1.5 %last_kernel.1 = (f32[16,128]{1,0:T(8,128)S(1)}, f32[8,256]{1,0:T(8,128)S(1)}, f32[128,32]{1,0:T(8,128)S(1)}) custom-call(s32[1]{0:T(128)} %bitcast.where, f32[2,16,256]{2,1,0:T(8,128)S(1)} %select_add_fusion.1.here, f32[2,16,256]{2,1,0:T(8,128)S(1)} %collective-permute-done.11.there, f32[360,128]{1,0:T(8,128)S(1)} %get-tuple-element.35.factor, ...), custom_call_target="tpu_custom_call" | custom-call | tf_op jit(solution)/shard_map/last_kernel/pallas_call | solution.py:419
  47.8 23.3 %all_to_all.11 = f32[128,1,32]{2,1,0:T(1,128)S(1)} all-to-all(f32[128,1,32]{2,1,0:T(1,128)S(1)} %bitcast.8), channel_id=1, replica_groups=mesh['grp'=2,'reg_0'=4,'reg_1'=4,'reg_2'=4] {'grp','reg_0','reg_1','reg_2'}, dimensions={0} | all-to-all | bytes 32768 | tf_op jit(solution)/shard_map/all_to_all | solution.py:509
  71.1 1.2 %final_kernel.1 = (f32[9,128]{1,0:T(8,128)}, f32[3,256]{1,0:T(4,128)}) custom-call(f32[128,32]{1,0:T(8,128)S(1)} %bitcast.7, f32[16,128]{1,0:T(8,128)S(1)} %get-tuple-element.36.v_old.v0, f32[16,128]{1,0:T(8,128)S(1)} %get-tuple-element.41.v_old.v1, f32[16,128]{1,0:T(8,128)S(1)} %get-tuple-element.47.v2, f32[8,256]{1,0:T(8,128)S(1)} %get-tuple-element.48.g0, ...), custom_call_target="tpu_custom_call" | custom-call | tf_op jit(solution)/shard_map/final_kernel/pallas_call | solution.py:419
  (9 shorter events, 0.1 us)
Async XLA Ops:
  3.9 2.4 %collective-permute-start = (f32[2,56,256]{2,1,0:T(8,128)S(1)}, f32[2,56,256]{2,1,0:T(8,128)S(1)}, u32[]{:S(2)}, u32[]{:S(2)}) collective-permute-start(f32[2,56,256]{2,1,0:T(8,128)S(1)} %get-tuple-element.28), channel_id=1, source_target_pairs={{0,64},{1,65},{2,66},{3,67},{4,68},{5,69},{6,70},{7,71},{8,72},{9,... | collective-permute-start | bytes 344072 | tf_op jit(solution)/shard_map/ppermute | solution.py:460
  6.3 5.2 %collective-permute-start.1 = (f32[2,56,256]{2,1,0:T(8,128)S(1)}, f32[2,56,256]{2,1,0:T(8,128)S(1)}, u32[]{:S(2)}, u32[]{:S(2)}) collective-permute-start(f32[2,56,256]{2,1,0:T(8,128)S(1)} %add.45), channel_id=1, source_target_pairs={{0,65},{2,67},{4,69},{6,71},{8,73},{10,75},{12,77},{14,79},{16,81}... | collective-permute-start | bytes 344072 | tf_op jit(solution)/shard_map/ppermute | solution.py:460
  11.5 4.3 %collective-permute-start.2 = (f32[2,56,256]{2,1,0:T(8,128)S(1)}, f32[2,56,256]{2,1,0:T(8,128)S(1)}, u32[]{:S(2)}, u32[]{:S(2)}) collective-permute-start(f32[2,56,256]{2,1,0:T(8,128)S(1)} %add.46), channel_id=1, source_target_pairs={{0,3},{65,66},{2,5},{67,68},{4,7},{69,70},{6,9},{71,72},{8,11},{73... | collective-permute-start | bytes 344072 | tf_op jit(solution)/shard_map/ppermute | solution.py:460
  15.9 3.9 %collective-permute-start.3 = (f32[2,56,256]{2,1,0:T(8,128)S(1)}, f32[2,56,256]{2,1,0:T(8,128)S(1)}, u32[]{:S(2)}, u32[]{:S(2)}) collective-permute-start(f32[2,56,256]{2,1,0:T(8,128)S(1)} %select_add_fusion.here), channel_id=1, source_target_pairs={{0,64},{1,65},{2,66},{3,67},{4,68},{5,69},{6,70},{7,71},{8,72},{9,... | collective-permute-start | bytes 344072 | tf_op jit(solution)/shard_map/ppermute | solution.py:460
  21.7 1.3 %collective-permute-start.4 = (f32[2,16,256]{2,1,0:T(8,128)S(1)}, f32[2,16,256]{2,1,0:T(8,128)S(1)}, u32[]{:S(2)}, u32[]{:S(2)}) collective-permute-start(f32[2,16,256]{2,1,0:T(8,128)S(1)} %get-tuple-element.34), channel_id=1, source_target_pairs={{0,64},{1,65},{2,66},{3,67},{4,68},{5,69},{6,70},{7,71},{8,72},{9,... | collective-permute-start | bytes 98312 | tf_op jit(solution)/shard_map/ppermute | solution.py:460
  23.0 3.3 %collective-permute-start.5 = (f32[2,16,256]{2,1,0:T(8,128)S(1)}, f32[2,16,256]{2,1,0:T(8,128)S(1)}, u32[]{:S(2)}, u32[]{:S(2)}) collective-permute-start(f32[2,16,256]{2,1,0:T(8,128)S(1)} %add.49), channel_id=1, source_target_pairs={{0,65},{2,67},{4,69},{6,71},{8,73},{10,75},{12,77},{14,79},{16,81}... | collective-permute-start | bytes 98312 | tf_op jit(solution)/shard_map/ppermute | solution.py:460
  26.4 3.3 %collective-permute-start.6 = (f32[2,16,256]{2,1,0:T(8,128)S(1)}, f32[2,16,256]{2,1,0:T(8,128)S(1)}, u32[]{:S(2)}, u32[]{:S(2)}) collective-permute-start(f32[2,16,256]{2,1,0:T(8,128)S(1)} %add.50), channel_id=1, source_target_pairs={{0,3},{65,66},{2,5},{67,68},{4,7},{69,70},{6,9},{71,72},{8,11},{73... | collective-permute-start | bytes 98312 | tf_op jit(solution)/shard_map/ppermute | solution.py:460
  29.7 3.4 %collective-permute-start.7 = (f32[2,16,256]{2,1,0:T(8,128)S(1)}, f32[2,16,256]{2,1,0:T(8,128)S(1)}, u32[]{:S(2)}, u32[]{:S(2)}) collective-permute-start(f32[2,16,256]{2,1,0:T(8,128)S(1)} %select_add_fusion.2.here), channel_id=1, source_target_pairs={{0,64},{1,65},{2,66},{3,67},{4,68},{5,69},{6,70},{7,71},{8,72},{9,... | collective-permute-start | bytes 98312 | tf_op jit(solution)/shard_map/ppermute | solution.py:460
  35.0 1.3 %collective-permute-start.8 = (f32[2,16,256]{2,1,0:T(8,128)S(1)}, f32[2,16,256]{2,1,0:T(8,128)S(1)}, u32[]{:S(2)}, u32[]{:S(2)}) collective-permute-start(f32[2,16,256]{2,1,0:T(8,128)S(1)} %get-tuple-element.40), channel_id=1, source_target_pairs={{0,64},{1,65},{2,66},{3,67},{4,68},{5,69},{6,70},{7,71},{8,72},{9,... | collective-permute-start | bytes 98312 | tf_op jit(solution)/shard_map/ppermute | solution.py:460
  36.3 3.3 %collective-permute-start.9 = (f32[2,16,256]{2,1,0:T(8,128)S(1)}, f32[2,16,256]{2,1,0:T(8,128)S(1)}, u32[]{:S(2)}, u32[]{:S(2)}) collective-permute-start(f32[2,16,256]{2,1,0:T(8,128)S(1)} %add.52), channel_id=1, source_target_pairs={{0,65},{2,67},{4,69},{6,71},{8,73},{10,75},{12,77},{14,79},{16,81}... | collective-permute-start | bytes 98312 | tf_op jit(solution)/shard_map/ppermute | solution.py:460
  39.7 3.3 %collective-permute-start.10 = (f32[2,16,256]{2,1,0:T(8,128)S(1)}, f32[2,16,256]{2,1,0:T(8,128)S(1)}, u32[]{:S(2)}, u32[]{:S(2)}) collective-permute-start(f32[2,16,256]{2,1,0:T(8,128)S(1)} %add.53), channel_id=1, source_target_pairs={{0,3},{65,66},{2,5},{67,68},{4,7},{69,70},{6,9},{71,72},{8,11},{73... | collective-permute-start | bytes 98312 | tf_op jit(solution)/shard_map/ppermute | solution.py:460
  43.0 3.3 %collective-permute-start.11 = (f32[2,16,256]{2,1,0:T(8,128)S(1)}, f32[2,16,256]{2,1,0:T(8,128)S(1)}, u32[]{:S(2)}, u32[]{:S(2)}) collective-permute-start(f32[2,16,256]{2,1,0:T(8,128)S(1)} %select_add_fusion.1.here), channel_id=1, source_target_pairs={{0,64},{1,65},{2,66},{3,67},{4,68},{5,69},{6,70},{7,71},{8,72},{9,... | collective-permute-start | bytes 98312 | tf_op jit(solution)/shard_map/ppermute | solution.py:460

commit v5 on v4

--- a/solution.py
+++ b/solution.py
@@ -51,17 +51,33 @@
 
 def put(terms, onehot):
     return lax.dot_general(
-        terms, onehot, (((1,), (1,)), ((), ())), preferred_element_type=F32
-    )
-
-
-def onehot_of(index):
-    ids = lax.broadcasted_iota(jnp.int32, (WIDE, index.shape[1]), 0)
-    return jnp.where(ids == index, 1.0, 0.0).astype(BF16)
-
-
-def total(x):
-    return jnp.sum(jnp.sum(x, 0, keepdims=True), 1, keepdims=True)
+        terms, onehot[...], (((1,), (1,)), ((), ())), preferred_element_type=F32
+    )
+
+
+def put_few(terms, onehot):
+    half = WIDE // 2
+    parts = [
+        lax.dot_general(
+            terms,
+            onehot[k : k + half, :],
+            (((1,), (1,)), ((), ())),
+            preferred_element_type=F32,
+        )
+        for k in (0, half)
+    ]
+    return jnp.concatenate(parts, 1)
+
+
+def write_onehot(out, index):
+    ids = lax.broadcasted_iota(jnp.int32, (16, index.shape[1]), 0)
+
+    def step(k, carry):
+        start = pl.multiple_of(k * 16, 16)
+        out[pl.ds(start, 16), :] = jnp.where(ids == index - start, 1.0, 0.0).astype(BF16)
+        return carry
+
+    lax.fori_loop(0, WIDE // 16, step, 0)
 
 
 def per_lane(x):
@@ -79,9 +95,9 @@
 
 
 def point_part(u, p, hot_p, vinv):
-    g = folded(put(stacked(p[0] * u[0] + p[1] * u[1]), hot_p))
+    g = folded(put_few(stacked(p[0] * u[0] + p[1] * u[1]), hot_p))
     s = jnp.concatenate(solve_points(vinv, g), 0)
-    back = folded(pick(stacked(s), hot_p))
+    back = folded(pick(stacked(s), hot_p[...]))
     return g, s, [jnp.sum(p[i] * back, 0, keepdims=True) for i in range(2)]
 
 
@@ -131,7 +147,7 @@
 
 def first_kernel(
     regions, where, cam_hbm, pnt_hbm, res_hbm, camera_hbm, points_hbm,
-    keep, send, jx, px, vinv_out, gres_out, index, res, cam, pnt, camera, points, sems,
+    keep, send, jx, px, vinv_out, gres_out, block_out, hot_p, hot_c, res, cam, pnt, camera, points, sems,
 ):
     pairs = [(points_hbm, points), (pnt_hbm, pnt), (res_hbm, res), (camera_hbm, camera), (cam_hbm, cam)]
     copies = [pltpu.make_async_copy(a, b, sems.at[k]) for k, (a, b) in enumerate(pairs)]
@@ -139,12 +155,12 @@
         copy.start()
     group, region, odd = position(where, regions)
     copies[0].wait()
-    slot = points[...]
-    hot_p = onehot_of(slot)
+    write_onehot(hot_p, points[...])
     for copy in copies[1:]:
         copy.wait()
     low, block = indices(regions, region, camera[...])
-    index[...] = jnp.concatenate([low, block, slot] + [jnp.zeros_like(low)] * 5, 0)
+    block_out[...] = block
+    write_onehot(hot_c, low)
     camf = cam[...].astype(F32)
     pf = pnt[...].astype(F32)
     zero5 = jnp.zeros((5, OBS), F32)
@@ -164,7 +180,7 @@
     ]
     products = p[0] * turned[0] + p[1] * turned[1]
     right = p[0] * r[0] + p[1] * r[1]
-    sums = folded(put(stacked(jnp.concatenate([squares, products, right], 0)), hot_p))
+    sums = folded(put_few(stacked(jnp.concatenate([squares, products, right], 0)), hot_p))
     v00, v11, v22 = [sums[k : k + 1] + DAMPING for k in range(3)]
     v01, v12, v02 = [sums[8 + k : 9 + k] for k in range(3)]
     g = sums[16:24]
@@ -182,7 +198,7 @@
     vinv_out[...] = vinv
     gres_out[...] = g
     s = jnp.concatenate(solve_points(vinv, g), 0)
-    back = folded(pick(stacked(s), hot_p))
+    back = folded(pick(stacked(s), hot_p[...]))
     rem = [r[i] - jnp.sum(p[i] * back, 0, keepdims=True) for i in range(2)]
     rolled = []
     for d in range(5):
@@ -194,7 +210,6 @@
     edge = a[0] * last[0] + a[1] * last[1]
     gradient = a[0] * rem[0] + a[1] * rem[1]
     terms = stacked(jnp.concatenate(rolled + [edge, gradient], 0))
-    hot_c = onehot_of(low)
     blocks = []
     for k in range(3):
         mask = jnp.where(block == k, 1.0, 0.0).astype(BF16)
@@ -254,9 +269,7 @@
     return low, [tile(factor, at + k) for k in range(9)]
 
 
-def apply_body(group, odd, x, field, low, block, slot, jx, px, vinv):
-    hot_c = onehot_of(low)
-    hot_p = onehot_of(slot)
+def apply_body(group, odd, x, field, block, hot_p, hot_c, jx, px, vinv):
     for k in range(9):
         field[8 * k : 8 * k + 8, :] = x[k]
     for k in range(9, 16):
@@ -267,13 +280,13 @@
     ]
     seen = [jnp.where(odd == 0, frames[k], frames[k + 1]) for k in range(3)]
     v = jnp.where(group == 0, seen[1][:, 0:128], seen[1][:, 128:256])
-    picked = pick(jnp.concatenate([stacked(f) for f in seen], 0), hot_c)
+    picked = pick(jnp.concatenate([stacked(f) for f in seen], 0), hot_c[...])
     blocks = [folded(picked[48 * k : 48 * k + 48]) for k in range(3)]
     values = jnp.where(block == 0, blocks[0], jnp.where(block == 1, blocks[1], blocks[2]))
     u = [jnp.sum(jx[i] * values, 0, keepdims=True) for i in range(2)]
     p = [px[0], px[1]]
     g, s, ps = point_part(u, p, hot_p, vinv[...])
-    return hot_c, v, u, g, s, ps
+    return v, u, g, s, ps
 
 
 def finish(group, odd, hot_c, block, jx, ps, keep, send):
@@ -304,19 +317,19 @@
 
 
 def start_kernel(
-    regions, where, here, there, index, jx, px, vinv,
+    regions, where, here, there, block_in, hot_p, hot_c, jx, px, vinv,
     keep, send, factor, v_out, g_out, s_out, rem_out, scal, tiles, field,
 ):
     group, region, odd = position(where, regions)
-    low, block, slot = index[0:1, :], index[1:2, :], index[2:3, :]
+    block = block_in[...]
     to_tiles(tiles, group, odd, here, there)
     lower, inv = factor_camera(tiles, factor)
     b = [-tile(tiles, 48 + k) for k in range(8)] + [-tile(tiles, 37)]
     x = solve_camera(lower, inv, b)
     dots = functools.reduce(lambda p, q: p + q, [b[k] * x[k] for k in range(9)])
     own = lax.broadcasted_iota(jnp.int32, (8, 128), 0) == 2 * (1 + odd) + group
-    hot_c, v, u, g, s, ps = apply_body(
-        group, odd, x, field, low, block, slot, jx, px, vinv
+    v, u, g, s, ps = apply_body(
+        group, odd, x, field, block, hot_p, hot_c, jx, px, vinv
     )
     rem = [u[i] - ps[i] for i in range(2)]
     v_out[...], g_out[...], s_out[...] = v, g, s
@@ -332,15 +345,15 @@
 
 
 def next_kernel(
-    regions, where, here, there, factor, index, jx, px, vinv, v_old, s_old, rem_old,
+    regions, where, here, there, factor, block_in, hot_p, hot_c, jx, px, vinv, v_old, s_old, rem_old,
     keep, send, v_out, g_out, s_out, rem_out, scal, tiles, field,
 ):
     group, region, odd = position(where, regions)
-    low, block, slot = index[0:1, :], index[1:2, :], index[2:3, :]
+    block = block_in[...]
     to_tiles(tiles, group, odd, here, there)
     x = solve_camera(*read_factor(factor), [tile(tiles, k) for k in range(9)])
-    hot_c, v, u, g, s, ps = apply_body(
-        group, odd, x, field, low, block, slot, jx, px, vinv
+    v, u, g, s, ps = apply_body(
+        group, odd, x, field, block, hot_p, hot_c, jx, px, vinv
     )
     rem = [u[i] - ps[i] for i in range(2)]
     v_out[...], g_out[...], s_out[...] = v, g, s
@@ -350,15 +363,15 @@
 
 
 def last_kernel(
-    regions, where, here, there, factor, index, jx, px, vinv, v_old, s_old, rem_old,
+    regions, where, here, there, factor, block_in, hot_p, hot_c, jx, px, vinv, v_old, s_old, rem_old,
     scal0, scal1, v_out, g_out, sums, tiles, field,
 ):
     group, region, odd = position(where, regions)
-    low, block, slot = index[0:1, :], index[1:2, :], index[2:3, :]
+    block = block_in[...]
     to_tiles(tiles, group, odd, here, there)
     x = solve_camera(*read_factor(factor), [tile(tiles, k) for k in range(9)])
-    hot_c, v, u, g, s, ps = apply_body(
-        group, odd, x, field, low, block, slot, jx, px, vinv
+    v, u, g, s, ps = apply_body(
+        group, odd, x, field, block, hot_p, hot_c, jx, px, vinv
     )
     rem = [u[i] - ps[i] for i in range(2)]
     v_out[...], g_out[...] = v, g
@@ -366,7 +379,10 @@
     rows = jnp.concatenate([scal0[...], scal1[...], scal2, jnp.zeros((8, 128), F32)], 0)
     ones = jnp.ones((128, 128), BF16)
     high, middle, low_part = three_parts(rows)
-    sums[...] = put(ones, high) + put(ones, middle) + put(ones, low_part)
+    sums[...] = sum(
+        lax.dot_general(ones, x, (((1,), (1,)), ((), ())), preferred_element_type=F32)
+        for x in (high, middle, low_part)
+    )
 
 
 def final_kernel(back, v0, v1, v2, g0, g1, g2, gres, vinv, cam, pnt):
@@ -474,11 +490,12 @@
     per_point = shape(8, P_DEV)
     rest = [shape(16, 128), per_point, per_point, shape(8, OBS), shape(8, 128)]
 
-    keep, send, jx, px, vinv, gres, index = run(
+    keep, send, jx, px, vinv, gres, block, hot_p, hot_c = run(
         first_kernel,
         halves(ROWS)
         + [shape(2, 16, OBS), shape(2, 8, OBS), per_point, per_point]
-        + [shape(8, OBS, dtype=jnp.int32)],
+        + [shape(1, OBS, dtype=jnp.int32)]
+        + [shape(WIDE, OBS, dtype=BF16)] * 2,
         where, *arrays,
         scratch=[
             pltpu.VMEM((2, OBS), F32), pltpu.VMEM((18, OBS), BF16), pltpu.VMEM((6, OBS), BF16),
@@ -487,7 +504,7 @@
         ],
         inputs=HBM,
     )
-    common = (index, jx, px, vinv)
+    common = (block, hot_p, hot_c, jx, px, vinv)
     keep, send, factor, v0, g0, s0, rem0, scal0 = run(
         start_kernel,
         halves(16) + [shape(45 * 8, 128)] + rest,

time: 72.4 us -> 71 us (0.981)
  Pallas kernels: 9.71 us -> 8.33 us
    pallas_call x5, Pallas kernels: 9.71 us -> 8.33 us  [call(): pl.pallas_call(kernel if regions is None else functools.partial(kernel, r...]
where the time goes in v5:
time: 71 us; the launch traced here: 70.9 us
  waiting for transfers between devices  24.7 us (35%)
  blocking collectives  23.2 us (33%)
  starting transfers between devices  13.7 us (19%)
  Pallas kernels  8.33 us (12%)
  between operations  0.72 us (1%)
    ppermute x12, waiting for transfers between devices, swap(): return lax.ppermute(x, GRP_REG, pairs)  24.7 us
    all_to_all x1, blocking collectives, local(): back = lax.all_to_all(sums, GRP_REG, 0, 0, tiled=True)  23.2 us
    ppermute x12, starting transfers between devices, swap(): return lax.ppermute(x, GRP_REG, pairs)  13.7 us
    pallas_call x5, Pallas kernels, call(): pl.pallas_call(kernel if regions is None else functools.partial(kernel, r...  8.33 us
  transfers between devices with their start and end apart: 12, of which 12 were waited for; matrix products, arithmetic and copies ran while one was open for 0% of the time, Pallas kernels for 0%

profile of v5, /device:TPU:1, one launch (start us, length us, event | category | flops | bytes accessed | tf_op | source)
XLA Modules:
  0.0 70.9 jit_solution(17146512365744229309)
XLA Ops:
  0.6 3.1 %first_kernel.1 = (f32[2,56,256]{2,1,0:T(8,128)S(1)}, f32[2,56,256]{2,1,0:T(8,128)S(1)}, f32[2,16,2048]{2,1,0:T(8,128)S(1)}, f32[2,8,2048]{2,1,0:T(8,128)S(1)}, ...) custom-call(s32[1]{0:T(128)} %bitcast.where, ...), custom_call_target="tpu_custom_call" | custom-call | tf_op jit(solution)/shard_map/first_kernel/pallas_call | solution.py:435
  3.7 1.5 %collective-permute-start = (f32[2,56,256]{2,1,0:T(8,128)S(1)}, f32[2,56,256]{2,1,0:T(8,128)S(1)}, u32[]{:S(2)}, u32[]{:S(2)}) collective-permute-start(f32[2,56,256]{2,1,0:T(8,128)S(1)} %get-tuple-element.30), channel_id=1, source_target_pairs={{0,64},{1,65},{2,66},{3,67},{4,68},{5,69},{6,70},{7,71},{8,72},{9,... | collective-permute-start | bytes 344072 | tf_op jit(solution)/shard_map/ppermute | solution.py:476
  5.2 1.0 %collective-permute-done = f32[2,56,256]{2,1,0:T(8,128)S(1)} collective-permute-done((f32[2,56,256]{2,1,0:T(8,128)S(1)}, f32[2,56,256]{2,1,0:T(8,128)S(1)}, u32[]{:S(2)}, u32[]{:S(2)}) %collective-permute-start) | collective-permute-done | bytes 114720 | tf_op jit(solution)/shard_map/ppermute | solution.py:476
  6.1 1.7 %collective-permute-start.1 = (f32[2,56,256]{2,1,0:T(8,128)S(1)}, f32[2,56,256]{2,1,0:T(8,128)S(1)}, u32[]{:S(2)}, u32[]{:S(2)}) collective-permute-start(f32[2,56,256]{2,1,0:T(8,128)S(1)} %add.45), channel_id=1, source_target_pairs={{0,65},{2,67},{4,69},{6,71},{8,73},{10,75},{12,77},{14,79},{16,81}... | collective-permute-start | bytes 344072 | tf_op jit(solution)/shard_map/ppermute | solution.py:476
  7.9 3.5 %collective-permute-done.1 = f32[2,56,256]{2,1,0:T(8,128)S(1)} collective-permute-done((f32[2,56,256]{2,1,0:T(8,128)S(1)}, f32[2,56,256]{2,1,0:T(8,128)S(1)}, u32[]{:S(2)}, u32[]{:S(2)}) %collective-permute-start.1) | collective-permute-done | bytes 114720 | tf_op jit(solution)/shard_map/ppermute | solution.py:476
  11.4 1.7 %collective-permute-start.2 = (f32[2,56,256]{2,1,0:T(8,128)S(1)}, f32[2,56,256]{2,1,0:T(8,128)S(1)}, u32[]{:S(2)}, u32[]{:S(2)}) collective-permute-start(f32[2,56,256]{2,1,0:T(8,128)S(1)} %add.46), channel_id=1, source_target_pairs={{0,3},{65,66},{2,5},{67,68},{4,7},{69,70},{6,9},{71,72},{8,11},{73... | collective-permute-start | bytes 344072 | tf_op jit(solution)/shard_map/ppermute | solution.py:476
  13.1 2.6 %collective-permute-done.2 = f32[2,56,256]{2,1,0:T(8,128)S(1)} collective-permute-done((f32[2,56,256]{2,1,0:T(8,128)S(1)}, f32[2,56,256]{2,1,0:T(8,128)S(1)}, u32[]{:S(2)}, u32[]{:S(2)}) %collective-permute-start.2) | collective-permute-done | bytes 114720 | tf_op jit(solution)/shard_map/ppermute | solution.py:476
  15.7 2.9 %collective-permute-start.3 = (f32[2,56,256]{2,1,0:T(8,128)S(1)}, f32[2,56,256]{2,1,0:T(8,128)S(1)}, u32[]{:S(2)}, u32[]{:S(2)}) collective-permute-start(f32[2,56,256]{2,1,0:T(8,128)S(1)} %select_add_fusion.here), channel_id=1, source_target_pairs={{0,64},{1,65},{2,66},{3,67},{4,68},{5,69},{6,70},{7,71},{8,72},{9,... | collective-permute-start | bytes 344072 | tf_op jit(solution)/shard_map/ppermute | solution.py:476
  18.6 1.0 %collective-permute-done.3.there = f32[2,56,256]{2,1,0:T(8,128)S(1)} collective-permute-done((f32[2,56,256]{2,1,0:T(8,128)S(1)}, f32[2,56,256]{2,1,0:T(8,128)S(1)}, u32[]{:S(2)}, u32[]{:S(2)}) %collective-permute-start.3) | collective-permute-done | bytes 114720 | tf_op jit(solution)/shard_map/ppermute | solution.py:476
  19.6 1.5 %start_kernel.1 = (f32[2,16,256]{2,1,0:T(8,128)S(1)}, f32[2,16,256]{2,1,0:T(8,128)S(1)}, f32[360,128]{1,0:T(8,128)S(1)}, f32[16,128]{1,0:T(8,128)S(1)}, f32[8,25...) custom-call(s32[1]{0:T(128)} %bitcast.where, ...), custom_call_target="tpu_custom_call" | custom-call | tf_op jit(solution)/shard_map/start_kernel/pallas_call | solution.py:435
  21.1 0.4 collective-permute-start.4
  21.5 0.9 %collective-permute-done.4 = f32[2,16,256]{2,1,0:T(8,128)S(1)} collective-permute-done((f32[2,16,256]{2,1,0:T(8,128)S(1)}, f32[2,16,256]{2,1,0:T(8,128)S(1)}, u32[]{:S(2)}, u32[]{:S(2)}) %collective-permute-start.4) | collective-permute-done | bytes 32800 | tf_op jit(solution)/shard_map/ppermute | solution.py:476
  22.4 0.0 collective-permute-start.5
  22.4 3.3 %collective-permute-done.5 = f32[2,16,256]{2,1,0:T(8,128)S(1)} collective-permute-done((f32[2,16,256]{2,1,0:T(8,128)S(1)}, f32[2,16,256]{2,1,0:T(8,128)S(1)}, u32[]{:S(2)}, u32[]{:S(2)}) %collective-permute-start.5) | collective-permute-done | bytes 32800 | tf_op jit(solution)/shard_map/ppermute | solution.py:476
  25.7 0.0 collective-permute-start.6
  25.8 3.3 %collective-permute-done.6 = f32[2,16,256]{2,1,0:T(8,128)S(1)} collective-permute-done((f32[2,16,256]{2,1,0:T(8,128)S(1)}, f32[2,16,256]{2,1,0:T(8,128)S(1)}, u32[]{:S(2)}, u32[]{:S(2)}) %collective-permute-start.6) | collective-permute-done | bytes 32800 | tf_op jit(solution)/shard_map/ppermute | solution.py:476
  29.1 2.6 %collective-permute-start.7 = (f32[2,16,256]{2,1,0:T(8,128)S(1)}, f32[2,16,256]{2,1,0:T(8,128)S(1)}, u32[]{:S(2)}, u32[]{:S(2)}) collective-permute-start(f32[2,16,256]{2,1,0:T(8,128)S(1)} %select_add_fusion.2.here), channel_id=1, source_target_pairs={{0,64},{1,65},{2,66},{3,67},{4,68},{5,69},{6,70},{7,71},{8,72},{9,... | collective-permute-start | bytes 98312 | tf_op jit(solution)/shard_map/ppermute | solution.py:476
  31.7 0.9 %collective-permute-done.7.there = f32[2,16,256]{2,1,0:T(8,128)S(1)} collective-permute-done((f32[2,16,256]{2,1,0:T(8,128)S(1)}, f32[2,16,256]{2,1,0:T(8,128)S(1)}, u32[]{:S(2)}, u32[]{:S(2)}) %collective-permute-start.7) | collective-permute-done | bytes 32800 | tf_op jit(solution)/shard_map/ppermute | solution.py:476
  32.5 1.4 %next_kernel.1 = (f32[2,16,256]{2,1,0:T(8,128)S(1)}, f32[2,16,256]{2,1,0:T(8,128)S(1)}, f32[16,128]{1,0:T(8,128)S(1)}, f32[8,256]{1,0:T(8,128)S(1)}, f32[8,256]{...) custom-call(s32[1]{0:T(128)} %bitcast.where, f32[2,16,256]{2,1,0:T(8,128)S(1)} %select_add_fusion.2.here, ...), custom_call_target="tpu_custom_call" | custom-call | tf_op jit(solution)/shard_map/next_kernel/pallas_call | solution.py:435
  33.9 0.4 collective-permute-start.8
  34.3 0.9 %collective-permute-done.8 = f32[2,16,256]{2,1,0:T(8,128)S(1)} collective-permute-done((f32[2,16,256]{2,1,0:T(8,128)S(1)}, f32[2,16,256]{2,1,0:T(8,128)S(1)}, u32[]{:S(2)}, u32[]{:S(2)}) %collective-permute-start.8) | collective-permute-done | bytes 32800 | tf_op jit(solution)/shard_map/ppermute | solution.py:476
  35.2 0.0 collective-permute-start.9
  35.2 3.3 %collective-permute-done.9 = f32[2,16,256]{2,1,0:T(8,128)S(1)} collective-permute-done((f32[2,16,256]{2,1,0:T(8,128)S(1)}, f32[2,16,256]{2,1,0:T(8,128)S(1)}, u32[]{:S(2)}, u32[]{:S(2)}) %collective-permute-start.9) | collective-permute-done | bytes 32800 | tf_op jit(solution)/shard_map/ppermute | solution.py:476
  38.5 0.0 collective-permute-start.10
  38.6 3.3 %collective-permute-done.10 = f32[2,16,256]{2,1,0:T(8,128)S(1)} collective-permute-done((f32[2,16,256]{2,1,0:T(8,128)S(1)}, f32[2,16,256]{2,1,0:T(8,128)S(1)}, u32[]{:S(2)}, u32[]{:S(2)}) %collective-permute-start.10) | collective-permute-done | bytes 32800 | tf_op jit(solution)/shard_map/ppermute | solution.py:476
  41.9 2.5 %collective-permute-start.11 = (f32[2,16,256]{2,1,0:T(8,128)S(1)}, f32[2,16,256]{2,1,0:T(8,128)S(1)}, u32[]{:S(2)}, u32[]{:S(2)}) collective-permute-start(f32[2,16,256]{2,1,0:T(8,128)S(1)} %select_add_fusion.1.here), channel_id=1, source_target_pairs={{0,64},{1,65},{2,66},{3,67},{4,68},{5,69},{6,70},{7,71},{8,72},{9,... | collective-permute-start | bytes 98312 | tf_op jit(solution)/shard_map/ppermute | solution.py:476
  44.4 0.9 %collective-permute-done.11.there = f32[2,16,256]{2,1,0:T(8,128)S(1)} collective-permute-done((f32[2,16,256]{2,1,0:T(8,128)S(1)}, f32[2,16,256]{2,1,0:T(8,128)S(1)}, u32[]{:S(2)}, u32[]{:S(2)}) %collective-permute-start.11) | collective-permute-done | bytes 32800 | tf_op jit(solution)/shard_map/ppermute | solution.py:476
  45.2 1.2 %last_kernel.1 = (f32[16,128]{1,0:T(8,128)S(1)}, f32[8,256]{1,0:T(8,128)S(1)}, f32[128,32]{1,0:T(8,128)S(1)}) custom-call(s32[1]{0:T(128)} %bitcast.where, f32[2,16,256]{2,1,0:T(8,128)S(1)} %select_add_fusion.1.here, f32[2,16,256]{2,1,0:T(8,128)S(1)} %collective-permute-done.11.there, f32[360,128]{1,0:T(8,128)S(1)} %get-tuple-element.39.factor, ...), custom_call_target="tpu_custom_call" | custom-call | tf_op jit(solution)/shard_map/last_kernel/pallas_call | solution.py:435
  46.5 23.2 %all_to_all.11 = f32[128,1,32]{2,1,0:T(1,128)S(1)} all-to-all(f32[128,1,32]{2,1,0:T(1,128)S(1)} %bitcast.8), channel_id=1, replica_groups=mesh['grp'=2,'reg_0'=4,'reg_1'=4,'reg_2'=4] {'grp','reg_0','reg_1','reg_2'}, dimensions={0} | all-to-all | bytes 32768 | tf_op jit(solution)/shard_map/all_to_all | solution.py:526
  69.7 1.2 %final_kernel.1 = (f32[9,128]{1,0:T(8,128)}, f32[3,256]{1,0:T(4,128)}) custom-call(f32[128,32]{1,0:T(8,128)S(1)} %bitcast.7, f32[16,128]{1,0:T(8,128)S(1)} %get-tuple-element.40.v_old.v0, f32[16,128]{1,0:T(8,128)S(1)} %get-tuple-element.45.v_old.v1, f32[16,128]{1,0:T(8,128)S(1)} %get-tuple-element.51.v2, f32[8,256]{1,0:T(8,128)S(1)} %get-tuple-element.52.g0, ...), custom_call_target="tpu_custom_call" | custom-call | tf_op jit(solution)/shard_map/final_kernel/pallas_call | solution.py:435
  (9 shorter events, 0.1 us)
Async XLA Ops:
  3.7 2.4 %collective-permute-start = (f32[2,56,256]{2,1,0:T(8,128)S(1)}, f32[2,56,256]{2,1,0:T(8,128)S(1)}, u32[]{:S(2)}, u32[]{:S(2)}) collective-permute-start(f32[2,56,256]{2,1,0:T(8,128)S(1)} %get-tuple-element.30), channel_id=1, source_target_pairs={{0,64},{1,65},{2,66},{3,67},{4,68},{5,69},{6,70},{7,71},{8,72},{9,... | collective-permute-start | bytes 344072 | tf_op jit(solution)/shard_map/ppermute | solution.py:476
  6.1 5.2 %collective-permute-start.1 = (f32[2,56,256]{2,1,0:T(8,128)S(1)}, f32[2,56,256]{2,1,0:T(8,128)S(1)}, u32[]{:S(2)}, u32[]{:S(2)}) collective-permute-start(f32[2,56,256]{2,1,0:T(8,128)S(1)} %add.45), channel_id=1, source_target_pairs={{0,65},{2,67},{4,69},{6,71},{8,73},{10,75},{12,77},{14,79},{16,81}... | collective-permute-start | bytes 344072 | tf_op jit(solution)/shard_map/ppermute | solution.py:476
  11.4 4.3 %collective-permute-start.2 = (f32[2,56,256]{2,1,0:T(8,128)S(1)}, f32[2,56,256]{2,1,0:T(8,128)S(1)}, u32[]{:S(2)}, u32[]{:S(2)}) collective-permute-start(f32[2,56,256]{2,1,0:T(8,128)S(1)} %add.46), channel_id=1, source_target_pairs={{0,3},{65,66},{2,5},{67,68},{4,7},{69,70},{6,9},{71,72},{8,11},{73... | collective-permute-start | bytes 344072 | tf_op jit(solution)/shard_map/ppermute | solution.py:476
  15.7 3.9 %collective-permute-start.3 = (f32[2,56,256]{2,1,0:T(8,128)S(1)}, f32[2,56,256]{2,1,0:T(8,128)S(1)}, u32[]{:S(2)}, u32[]{:S(2)}) collective-permute-start(f32[2,56,256]{2,1,0:T(8,128)S(1)} %select_add_fusion.here), channel_id=1, source_target_pairs={{0,64},{1,65},{2,66},{3,67},{4,68},{5,69},{6,70},{7,71},{8,72},{9,... | collective-permute-start | bytes 344072 | tf_op jit(solution)/shard_map/ppermute | solution.py:476
  21.1 1.3 %collective-permute-start.4 = (f32[2,16,256]{2,1,0:T(8,128)S(1)}, f32[2,16,256]{2,1,0:T(8,128)S(1)}, u32[]{:S(2)}, u32[]{:S(2)}) collective-permute-start(f32[2,16,256]{2,1,0:T(8,128)S(1)} %get-tuple-element.38), channel_id=1, source_target_pairs={{0,64},{1,65},{2,66},{3,67},{4,68},{5,69},{6,70},{7,71},{8,72},{9,... | collective-permute-start | bytes 98312 | tf_op jit(solution)/shard_map/ppermute | solution.py:476
  22.4 3.3 %collective-permute-start.5 = (f32[2,16,256]{2,1,0:T(8,128)S(1)}, f32[2,16,256]{2,1,0:T(8,128)S(1)}, u32[]{:S(2)}, u32[]{:S(2)}) collective-permute-start(f32[2,16,256]{2,1,0:T(8,128)S(1)} %add.49), channel_id=1, source_target_pairs={{0,65},{2,67},{4,69},{6,71},{8,73},{10,75},{12,77},{14,79},{16,81}... | collective-permute-start | bytes 98312 | tf_op jit(solution)/shard_map/ppermute | solution.py:476
  25.7 3.3 %collective-permute-start.6 = (f32[2,16,256]{2,1,0:T(8,128)S(1)}, f32[2,16,256]{2,1,0:T(8,128)S(1)}, u32[]{:S(2)}, u32[]{:S(2)}) collective-permute-start(f32[2,16,256]{2,1,0:T(8,128)S(1)} %add.50), channel_id=1, source_target_pairs={{0,3},{65,66},{2,5},{67,68},{4,7},{69,70},{6,9},{71,72},{8,11},{73... | collective-permute-start | bytes 98312 | tf_op jit(solution)/shard_map/ppermute | solution.py:476
  29.1 3.4 %collective-permute-start.7 = (f32[2,16,256]{2,1,0:T(8,128)S(1)}, f32[2,16,256]{2,1,0:T(8,128)S(1)}, u32[]{:S(2)}, u32[]{:S(2)}) collective-permute-start(f32[2,16,256]{2,1,0:T(8,128)S(1)} %select_add_fusion.2.here), channel_id=1, source_target_pairs={{0,64},{1,65},{2,66},{3,67},{4,68},{5,69},{6,70},{7,71},{8,72},{9,... | collective-permute-start | bytes 98312 | tf_op jit(solution)/shard_map/ppermute | solution.py:476
  33.9 1.3 %collective-permute-start.8 = (f32[2,16,256]{2,1,0:T(8,128)S(1)}, f32[2,16,256]{2,1,0:T(8,128)S(1)}, u32[]{:S(2)}, u32[]{:S(2)}) collective-permute-start(f32[2,16,256]{2,1,0:T(8,128)S(1)} %get-tuple-element.44), channel_id=1, source_target_pairs={{0,64},{1,65},{2,66},{3,67},{4,68},{5,69},{6,70},{7,71},{8,72},{9,... | collective-permute-start | bytes 98312 | tf_op jit(solution)/shard_map/ppermute | solution.py:476
  35.2 3.3 %collective-permute-start.9 = (f32[2,16,256]{2,1,0:T(8,128)S(1)}, f32[2,16,256]{2,1,0:T(8,128)S(1)}, u32[]{:S(2)}, u32[]{:S(2)}) collective-permute-start(f32[2,16,256]{2,1,0:T(8,128)S(1)} %add.52), channel_id=1, source_target_pairs={{0,65},{2,67},{4,69},{6,71},{8,73},{10,75},{12,77},{14,79},{16,81}... | collective-permute-start | bytes 98312 | tf_op jit(solution)/shard_map/ppermute | solution.py:476
  38.5 3.3 %collective-permute-start.10 = (f32[2,16,256]{2,1,0:T(8,128)S(1)}, f32[2,16,256]{2,1,0:T(8,128)S(1)}, u32[]{:S(2)}, u32[]{:S(2)}) collective-permute-start(f32[2,16,256]{2,1,0:T(8,128)S(1)} %add.53), channel_id=1, source_target_pairs={{0,3},{65,66},{2,5},{67,68},{4,7},{69,70},{6,9},{71,72},{8,11},{73... | collective-permute-start | bytes 98312 | tf_op jit(solution)/shard_map/ppermute | solution.py:476
  41.9 3.3 %collective-permute-start.11 = (f32[2,16,256]{2,1,0:T(8,128)S(1)}, f32[2,16,256]{2,1,0:T(8,128)S(1)}, u32[]{:S(2)}, u32[]{:S(2)}) collective-permute-start(f32[2,16,256]{2,1,0:T(8,128)S(1)} %select_add_fusion.1.here), channel_id=1, source_target_pairs={{0,64},{1,65},{2,66},{3,67},{4,68},{5,69},{6,70},{7,71},{8,72},{9,... | collective-permute-start | bytes 98312 | tf_op jit(solution)/shard_map/ppermute | solution.py:476

commit v6 on v5

--- a/solution.py
+++ b/solution.py
@@ -70,14 +70,18 @@
 
 
 def write_onehot(out, index):
-    ids = lax.broadcasted_iota(jnp.int32, (16, index.shape[1]), 0)
+    rows = lax.broadcasted_iota(jnp.int32, (16, 128), 0)
+    here = jnp.broadcast_to(index.astype(F32), (16, OBS)).astype(BF16)
+    one, zero = jnp.ones((16, 128), BF16), jnp.zeros((16, 128), BF16)
 
     def step(k, carry):
         start = pl.multiple_of(k * 16, 16)
-        out[pl.ds(start, 16), :] = jnp.where(ids == index - start, 1.0, 0.0).astype(BF16)
+        ids = (rows + start).astype(F32).astype(BF16)
+        for t in range(0, OBS, 128):
+            out[pl.ds(start, 16), t : t + 128] = jnp.where(ids == here[:, t : t + 128], one, zero)
         return carry
 
-    lax.fori_loop(0, WIDE // 16, step, 0)
+    lax.fori_loop(0, WIDE // 16, step, 0, unroll=4)
 
 
 def per_lane(x):
@@ -103,8 +107,7 @@
 
 def position(where, regions):
     device = where[0]
-    region = device & (regions - 1)
-    return device >> (regions.bit_length() - 1), region, region & 1
+    return device >> (regions.bit_length() - 1), device & (regions - 1)
 
 
 def indices(regions, region, camera):
@@ -113,32 +116,14 @@
     return low, (owners & (regions - 1)) - region + 1
 
 
-def split_frames(group, odd, blocks, keep, send):
-    even = odd == 0
-    zero = jnp.zeros_like(blocks[0])
-    frames = [
-        jnp.where(even, blocks[0], zero),
-        jnp.where(even, blocks[1], blocks[0]),
-        jnp.where(even, blocks[2], blocks[1]),
-        jnp.where(even, zero, blocks[2]),
-    ]
-    first = group == odd
-    for k in range(2):
-        keep[k] = jnp.where(first, frames[2 + k], frames[k])
-        send[k] = jnp.where(first, frames[k], frames[2 + k])
-
-
-def to_tiles(tiles, group, odd, here, there):
-    first = group == odd
-    rows = here.shape[1]
-    for k in range(2):
-        mine, other = here[k], there[k]
-        lower = jnp.where(first, other, mine)
-        upper = jnp.where(first, mine, other)
+def to_tiles(tiles, chip, near, far):
+    rows = chip.shape[1]
+    for k in range(3):
+        sums = chip[k] + (near[k] + far[k])
         for h in range(2):
-            lanes = slice(128 * h, 128 * h + 128)
-            tiles[pl.ds(2 * k + h, rows, stride=8), :] = lower[:, lanes]
-            tiles[pl.ds(4 + 2 * k + h, rows, stride=8), :] = upper[:, lanes]
+            tiles[pl.ds(2 * k + h, rows, stride=8), :] = sums[:, 128 * h : 128 * h + 128]
+    for k in (6, 7):
+        tiles[pl.ds(k, rows, stride=8), :] = jnp.zeros((rows, 128), F32)
 
 
 def tile(tiles, k):
@@ -147,13 +132,13 @@
 
 def first_kernel(
     regions, where, cam_hbm, pnt_hbm, res_hbm, camera_hbm, points_hbm,
-    keep, send, jx, px, vinv_out, gres_out, block_out, hot_p, hot_c, res, cam, pnt, camera, points, sems,
+    part, jx, px, vinv_out, gres_out, block_out, hot_p, hot_c, res, cam, pnt, camera, points, sems,
 ):
     pairs = [(points_hbm, points), (pnt_hbm, pnt), (res_hbm, res), (camera_hbm, camera), (cam_hbm, cam)]
     copies = [pltpu.make_async_copy(a, b, sems.at[k]) for k, (a, b) in enumerate(pairs)]
     for copy in copies:
         copy.start()
-    group, region, odd = position(where, regions)
+    group, region = position(where, regions)
     copies[0].wait()
     write_onehot(hot_p, points[...])
     for copy in copies[1:]:
@@ -210,11 +195,9 @@
     edge = a[0] * last[0] + a[1] * last[1]
     gradient = a[0] * rem[0] + a[1] * rem[1]
     terms = stacked(jnp.concatenate(rolled + [edge, gradient], 0))
-    blocks = []
     for k in range(3):
         mask = jnp.where(block == k, 1.0, 0.0).astype(BF16)
-        blocks.append(folded(put(terms * mask, hot_c)))
-    split_frames(group, odd, blocks, keep, send)
+        part[k] = folded(put(terms * mask, hot_c))
 
 
 def solve_camera(low, inv, b):
@@ -269,18 +252,17 @@
     return low, [tile(factor, at + k) for k in range(9)]
 
 
-def apply_body(group, odd, x, field, block, hot_p, hot_c, jx, px, vinv):
+def apply_body(group, x, field, block, hot_p, hot_c, jx, px, vinv):
     for k in range(9):
         field[8 * k : 8 * k + 8, :] = x[k]
     for k in range(9, 16):
         field[8 * k : 8 * k + 8, :] = jnp.zeros((8, 128), F32)
     frames = [
         jnp.concatenate([field[pl.ds(2 * f + h, 16, stride=8), :] for h in range(2)], 1)
-        for f in range(4)
+        for f in range(3)
     ]
-    seen = [jnp.where(odd == 0, frames[k], frames[k + 1]) for k in range(3)]
-    v = jnp.where(group == 0, seen[1][:, 0:128], seen[1][:, 128:256])
-    picked = pick(jnp.concatenate([stacked(f) for f in seen], 0), hot_c[...])
+    v = jnp.where(group == 0, frames[1][:, 0:128], frames[1][:, 128:256])
+    picked = pick(jnp.concatenate([stacked(f) for f in frames], 0), hot_c[...])
     blocks = [folded(picked[48 * k : 48 * k + 48]) for k in range(3)]
     values = jnp.where(block == 0, blocks[0], jnp.where(block == 1, blocks[1], blocks[2]))
     u = [jnp.sum(jx[i] * values, 0, keepdims=True) for i in range(2)]
@@ -289,15 +271,14 @@
     return v, u, g, s, ps
 
 
-def finish(group, odd, hot_c, block, jx, ps, keep, send):
+def finish(hot_c, block, jx, ps, part):
     terms = stacked(jx[0] * ps[0] + jx[1] * ps[1])
     lhs = jnp.concatenate(
         [terms * jnp.where(block == k, 1.0, 0.0).astype(BF16) for k in range(3)], 0
     )
     out = put(lhs, hot_c)
-    split_frames(
-        group, odd, [folded(out[48 * k : 48 * k + 48]) for k in range(3)], keep, send
-    )
+    for k in range(3):
+        part[k] = folded(out[48 * k : 48 * k + 48])
 
 
 def scalar_rows(pairs):
@@ -317,24 +298,24 @@
 
 
 def start_kernel(
-    regions, where, here, there, block_in, hot_p, hot_c, jx, px, vinv,
-    keep, send, factor, v_out, g_out, s_out, rem_out, scal, tiles, field,
+    regions, where, chip, near, far, block_in, hot_p, hot_c, jx, px, vinv,
+    part, factor, v_out, g_out, s_out, rem_out, scal, tiles, field,
 ):
-    group, region, odd = position(where, regions)
+    group, region = position(where, regions)
     block = block_in[...]
-    to_tiles(tiles, group, odd, here, there)
+    to_tiles(tiles, chip, near, far)
     lower, inv = factor_camera(tiles, factor)
     b = [-tile(tiles, 48 + k) for k in range(8)] + [-tile(tiles, 37)]
     x = solve_camera(lower, inv, b)
     dots = functools.reduce(lambda p, q: p + q, [b[k] * x[k] for k in range(9)])
-    own = lax.broadcasted_iota(jnp.int32, (8, 128), 0) == 2 * (1 + odd) + group
+    own = lax.broadcasted_iota(jnp.int32, (8, 128), 0) == 2 + group
     v, u, g, s, ps = apply_body(
-        group, odd, x, field, block, hot_p, hot_c, jx, px, vinv
+        group, x, field, block, hot_p, hot_c, jx, px, vinv
     )
     rem = [u[i] - ps[i] for i in range(2)]
     v_out[...], g_out[...], s_out[...] = v, g, s
     rem_out[...] = jnp.concatenate(rem + [jnp.zeros((6, OBS), F32)], 0)
-    finish(group, odd, hot_c, block, jx, ps, keep, send)
+    finish(hot_c, block, jx, ps, part)
     scal[...] = scalar_rows(
         [
             (jnp.where(own, dots, 0.0),),
@@ -345,33 +326,33 @@
 
 
 def next_kernel(
-    regions, where, here, there, factor, block_in, hot_p, hot_c, jx, px, vinv, v_old, s_old, rem_old,
-    keep, send, v_out, g_out, s_out, rem_out, scal, tiles, field,
+    regions, where, chip, near, far, factor, block_in, hot_p, hot_c, jx, px, vinv, v_old, s_old, rem_old,
+    part, v_out, g_out, s_out, rem_out, scal, tiles, field,
 ):
-    group, region, odd = position(where, regions)
+    group, region = position(where, regions)
     block = block_in[...]
-    to_tiles(tiles, group, odd, here, there)
+    to_tiles(tiles, chip, near, far)
     x = solve_camera(*read_factor(factor), [tile(tiles, k) for k in range(9)])
     v, u, g, s, ps = apply_body(
-        group, odd, x, field, block, hot_p, hot_c, jx, px, vinv
+        group, x, field, block, hot_p, hot_c, jx, px, vinv
     )
     rem = [u[i] - ps[i] for i in range(2)]
     v_out[...], g_out[...], s_out[...] = v, g, s
     rem_out[...] = jnp.concatenate(rem + [jnp.zeros((6, OBS), F32)], 0)
-    finish(group, odd, hot_c, block, jx, ps, keep, send)
+    finish(hot_c, block, jx, ps, part)
     scal[...] = scalars(v, v_old[...], u, rem, rem_old, g, s, s_old[...])
 
 
 def last_kernel(
-    regions, where, here, there, factor, block_in, hot_p, hot_c, jx, px, vinv, v_old, s_old, rem_old,
+    regions, where, chip, near, far, factor, block_in, hot_p, hot_c, jx, px, vinv, v_old, s_old, rem_old,
     scal0, scal1, v_out, g_out, sums, tiles, field,
 ):
-    group, region, odd = position(where, regions)
+    group, region = position(where, regions)
     block = block_in[...]
-    to_tiles(tiles, group, odd, here, there)
+    to_tiles(tiles, chip, near, far)
     x = solve_camera(*read_factor(factor), [tile(tiles, k) for k in range(9)])
     v, u, g, s, ps = apply_body(
-        group, odd, x, field, block, hot_p, hot_c, jx, px, vinv
+        group, x, field, block, hot_p, hot_c, jx, px, vinv
     )
     rem = [u[i] - ps[i] for i in range(2)]
     v_out[...], g_out[...] = v, g
@@ -452,47 +433,64 @@
     def both_ways(pairs):
         return pairs + [(b, a) for a, b in pairs]
 
-    def device(left, region):
-        return ((region & 1) ^ left) * regions + region
-
-    cores = both_ways([(r, regions + r) for r in range(regions)])
-    pair = both_ways(
-        [(device(h, r), device(h, r + 1)) for h in range(2) for r in range(0, regions, 2)]
-    )
-    ends = [(device(1, 0), device(1, 1)), (device(0, regions - 2), device(0, regions - 1))]
-    next_pair = both_ways(
-        [
-            (device(0, r + i), device(1, r + 3 - i))
-            for r in range(0, regions - 2, 2)
+    def device(core, region):
+        return core * regions + region
+
+    cores = both_ways([(device(0, r), device(1, r)) for r in range(regions)])
+    inner = both_ways(
+        [(device(0, r), device(0, r + 1)) for r in range(0, regions, 2)]
+        + [(device(1, r + i), device(1, r + i + 2)) for r in range(0, regions, 4) for i in range(2)]
+    )
+    first, last = 0, regions - 1
+    outer = both_ways(
+        [(device(0, r + 1), device(0, r + 2)) for r in range(0, regions - 2, 2)]
+        + [
+            (device(1, r + i + 2), device(1, r + i + 4))
+            for r in range(0, regions - 4, 4)
             for i in range(2)
         ]
-        + ends
-    )
+    )
+    for ring in (
+        [device(0, first), device(1, first), device(1, first + 1)],
+        [device(0, last), device(1, last), device(1, last - 1)],
+    ):
+        outer += [(ring[k], ring[(k + 1) % 3]) for k in range(3)]
     group, region = lax.axis_index("grp"), lax.axis_index(REG)
-    right = group == region % 2
-    alone = jnp.where(right, region >= regions - 2, region < 2)
+    near_core = group == 0
+    rises = jnp.where(near_core, region % 2 == 0, region % 4 < 2)
+    reach = jnp.where(near_core, 1, 2)
+    above, below = region + reach <= last, region - reach >= first
 
     def swap(x, pairs):
         return lax.ppermute(x, GRP_REG, pairs)
 
-    def totals(keep, send):
-        half = keep + swap(send, cores)
-        half = half + swap(half, pair)
-        got = swap(half, next_pair)
-        half = half + jnp.where(alone, 0.0, got)
-        return half, swap(half, cores)
-
-    def halves(rows):
-        return [shape(2, rows, WIDE)] * 2
+    def totals(part):
+        chip = part + swap(part, cores)
+        lower, upper = chip[0:2], chip[1:3]
+        from_outer = swap(jnp.where(rises, lower, upper), outer)
+        from_inner = swap(jnp.where(rises, upper, lower), inner)
+        up = jnp.where(above, jnp.where(rises, from_inner, from_outer), 0.0)
+        down = jnp.where(below, jnp.where(rises, from_outer, from_inner), 0.0)
+        came = jnp.stack(
+            [
+                jnp.where(near_core, down[0], down[1]),
+                jnp.where(near_core, down[1] + up[0], 0.0),
+                jnp.where(near_core, up[1], up[0]),
+            ]
+        )
+        return chip, came, swap(came, cores)
+
+    def sums(rows):
+        return [shape(3, rows, WIDE)]
 
     run = functools.partial(call, scalar=True, regions=regions)
     field = pltpu.VMEM((128, 128), F32)
     per_point = shape(8, P_DEV)
     rest = [shape(16, 128), per_point, per_point, shape(8, OBS), shape(8, 128)]
 
-    keep, send, jx, px, vinv, gres, block, hot_p, hot_c = run(
+    part, jx, px, vinv, gres, block, hot_p, hot_c = run(
         first_kernel,
-        halves(ROWS)
+        sums(ROWS)
         + [shape(2, 16, OBS), shape(2, 8, OBS), per_point, per_point]
         + [shape(1, OBS, dtype=jnp.int32)]
         + [shape(WIDE, OBS, dtype=BF16)] * 2,
@@ -505,25 +503,25 @@
         inputs=HBM,
     )
     common = (block, hot_p, hot_c, jx, px, vinv)
-    keep, send, factor, v0, g0, s0, rem0, scal0 = run(
+    part, factor, v0, g0, s0, rem0, scal0 = run(
         start_kernel,
-        halves(16) + [shape(45 * 8, 128)] + rest,
-        where, *totals(keep, send), *common,
+        sums(16) + [shape(45 * 8, 128)] + rest,
+        where, *totals(part), *common,
         scratch=[pltpu.VMEM((8 * ROWS, 128), F32), field],
     )
-    keep, send, v1, g1, s1, rem1, scal1 = run(
+    part, v1, g1, s1, rem1, scal1 = run(
         next_kernel,
-        halves(16) + rest,
-        where, *totals(keep, send), factor, *common, v0, s0, rem0,
+        sums(16) + rest,
+        where, *totals(part), factor, *common, v0, s0, rem0,
         scratch=[field, field],
     )
-    v2, g2, sums = run(
+    v2, g2, scalar_sums = run(
         last_kernel,
         [shape(16, 128), per_point, shape(128, 32)],
-        where, *totals(keep, send), factor, *common, v1, s1, rem1, scal0, scal1,
+        where, *totals(part), factor, *common, v1, s1, rem1, scal0, scal1,
         scratch=[field, field],
     )
-    back = lax.all_to_all(sums, GRP_REG, 0, 0, tiled=True)
+    back = lax.all_to_all(scalar_sums, GRP_REG, 0, 0, tiled=True)
     return call(
         final_kernel,
         [shape(9, C_DEV), shape(3, P_DEV)],

time: 71 us -> 64 us (0.901)
  waiting for transfers between devices: 24.7 us -> 13.4 us
  starting transfers between devices: 13.7 us -> 16.9 us
  blocking collectives: 23.2 us -> 24.3 us
    ppermute x12, waiting for transfers between devices: 24.7 us -> 13.4 us  [swap(): return lax.ppermute(x, GRP_REG, pairs)]
    ppermute x12, starting transfers between devices: 13.7 us -> 16.9 us  [swap(): return lax.ppermute(x, GRP_REG, pairs)]
    all_to_all x1, blocking collectives: 23.2 us -> 24.3 us  [local(): back = lax.all_to_all(scalar_sums, GRP_REG, 0, 0, tiled=True)]
  transfers between devices with their start and end apart: 12 -> 12, of which waited for: 12 -> 9; matrix products, arithmetic and copies ran while one was open for 0% -> 0% of each run, Pallas kernels for 0% -> 0%
where the time goes in v6:
time: 64 us; the launch traced here: 63.9 us
  blocking collectives  24.3 us (38%)
  starting transfers between devices  16.9 us (26%)
  waiting for transfers between devices  13.4 us (21%)
  Pallas kernels  8.28 us (13%)
  between operations  0.78 us (1%)
    all_to_all x1, blocking collectives, local(): back = lax.all_to_all(scalar_sums, GRP_REG, 0, 0, tiled=True)  24.3 us
    ppermute x12, starting transfers between devices, swap(): return lax.ppermute(x, GRP_REG, pairs)  16.9 us
    ppermute x12, waiting for transfers between devices, swap(): return lax.ppermute(x, GRP_REG, pairs)  13.4 us
    pallas_call x5, Pallas kernels, call(): pl.pallas_call(kernel if regions is None else functools.partial(kernel, r...  8.28 us
  transfers between devices with their start and end apart: 12, of which 9 were waited for; matrix products, arithmetic and copies ran while one was open for 0% of the time, Pallas kernels for 0%

profile of v6, /device:TPU:1, one launch (start us, length us, event | category | flops | bytes accessed | tf_op | source)
XLA Modules:
  0.0 63.9 jit_solution(12819287422357733199)
XLA Ops:
  0.6 3.0 %first_kernel.1 = (f32[3,56,256]{2,1,0:T(8,128)S(1)}, f32[2,16,2048]{2,1,0:T(8,128)S(1)}, f32[2,8,2048]{2,1,0:T(8,128)S(1)}, f32[8,256]{1,0:T(8,128)S(1)}, f32[8...) custom-call(s32[1]{0:T(128)} %bitcast.where, ...), custom_call_target="tpu_custom_call" | custom-call | tf_op jit(solution)/shard_map/first_kernel/pallas_call | solution.py:416
  3.6 1.5 %collective-permute-start = (f32[3,56,256]{2,1,0:T(8,128)S(1)}, f32[3,56,256]{2,1,0:T(8,128)S(1)}, u32[]{:S(2)}, u32[]{:S(2)}) collective-permute-start(f32[3,56,256]{2,1,0:T(8,128)S(1)} %get-tuple-element.26), channel_id=1, source_target_pairs={{0,64},{1,65},{2,66},{3,67},{4,68},{5,69},{6,70},{7,71},{8,72},{9,... | collective-permute-start | bytes 516104 | tf_op jit(solution)/shard_map/ppermute | solution.py:465
  5.1 1.0 %collective-permute-done = f32[3,56,256]{2,1,0:T(8,128)S(1)} collective-permute-done((f32[3,56,256]{2,1,0:T(8,128)S(1)}, f32[3,56,256]{2,1,0:T(8,128)S(1)}, u32[]{:S(2)}, u32[]{:S(2)}) %collective-permute-start) | collective-permute-done | bytes 172064 | tf_op jit(solution)/shard_map/ppermute | solution.py:465
  6.2 1.5 %collective-permute-start.1 = (f32[2,56,256]{2,1,0:T(8,128)S(1)}, f32[2,56,256]{2,1,0:T(8,128)S(1)}, u32[]{:S(2)}, u32[]{:S(2)}) collective-permute-start(f32[2,56,256]{2,1,0:T(8,128)S(1)} %get-tuple-element.52), channel_id=1, source_target_pairs={{1,2},{3,4},{5,6},{7,8},{9,10},{11,12},{13,14},{15,16},{17,18},{19... | collective-permute-start | bytes 344072 | tf_op jit(solution)/shard_map/ppermute | solution.py:465
  7.7 2.6 %collective-permute-start.2 = (f32[2,56,256]{2,1,0:T(8,128)S(1)}, f32[2,56,256]{2,1,0:T(8,128)S(1)}, u32[]{:S(2)}, u32[]{:S(2)}) collective-permute-start(f32[2,56,256]{2,1,0:T(8,128)S(1)} %get-tuple-element.53), channel_id=1, source_target_pairs={{0,1},{2,3},{4,5},{6,7},{8,9},{10,11},{12,13},{14,15},{16,17},{18,... | collective-permute-start | bytes 344072 | tf_op jit(solution)/shard_map/ppermute | solution.py:465
  10.3 0.0 collective-permute-done.1
  10.3 4.0 %collective-permute-done.2 = f32[2,56,256]{2,1,0:T(8,128)S(1)} collective-permute-done((f32[2,56,256]{2,1,0:T(8,128)S(1)}, f32[2,56,256]{2,1,0:T(8,128)S(1)}, u32[]{:S(2)}, u32[]{:S(2)}) %collective-permute-start.2) | collective-permute-done | bytes 114720 | tf_op jit(solution)/shard_map/ppermute | solution.py:465
  14.3 0.3 collective-permute-start.3
  14.6 1.2 %collective-permute-done.3.far = f32[3,56,256]{2,1,0:T(8,128)S(1)} collective-permute-done((f32[3,56,256]{2,1,0:T(8,128)S(1)}, f32[3,56,256]{2,1,0:T(8,128)S(1)}, u32[]{:S(2)}, u32[]{:S(2)}) %collective-permute-start.3) | collective-permute-done | bytes 172064 | tf_op jit(solution)/shard_map/ppermute | solution.py:465
  15.8 1.5 %start_kernel.1 = (f32[3,16,256]{2,1,0:T(8,128)S(1)}, f32[360,128]{1,0:T(8,128)S(1)}, f32[16,128]{1,0:T(8,128)S(1)}, f32[8,256]{1,0:T(8,128)S(1)}, f32[8,256]{1,...) custom-call(s32[1]{0:T(128)} %bitcast.where, f32[3,56,256]{2,1,0:T(8,128)S(1)} %add.45.chip, ...), custom_call_target="tpu_custom_call" | custom-call | tf_op jit(solution)/shard_map/start_kernel/pallas_call | solution.py:416
  17.4 0.3 collective-permute-start.4
  17.6 1.1 %collective-permute-done.4 = f32[3,16,256]{2,1,0:T(8,128)S(1)} collective-permute-done((f32[3,16,256]{2,1,0:T(8,128)S(1)}, f32[3,16,256]{2,1,0:T(8,128)S(1)}, u32[]{:S(2)}, u32[]{:S(2)}) %collective-permute-start.4) | collective-permute-done | bytes 49184 | tf_op jit(solution)/shard_map/ppermute | solution.py:465
  18.7 2.1 %collective-permute-start.5 = (f32[2,16,256]{2,1,0:T(8,128)S(1)}, f32[2,16,256]{2,1,0:T(8,128)S(1)}, u32[]{:S(2)}, u32[]{:S(2)}) collective-permute-start(f32[2,16,256]{2,1,0:T(8,128)S(1)} %get-tuple-element.63), channel_id=1, source_target_pairs={{1,2},{3,4},{5,6},{7,8},{9,10},{11,12},{13,14},{15,16},{17,18},{19... | collective-permute-start | bytes 98312 | tf_op jit(solution)/shard_map/ppermute | solution.py:465
  20.8 3.2 %collective-permute-start.6 = (f32[2,16,256]{2,1,0:T(8,128)S(1)}, f32[2,16,256]{2,1,0:T(8,128)S(1)}, u32[]{:S(2)}, u32[]{:S(2)}) collective-permute-start(f32[2,16,256]{2,1,0:T(8,128)S(1)} %get-tuple-element.64), channel_id=1, source_target_pairs={{0,1},{2,3},{4,5},{6,7},{8,9},{10,11},{12,13},{14,15},{16,17},{18,... | collective-permute-start | bytes 98312 | tf_op jit(solution)/shard_map/ppermute | solution.py:465
  24.0 0.0 collective-permute-done.5
  24.0 1.3 %collective-permute-done.6 = f32[2,16,256]{2,1,0:T(8,128)S(1)} collective-permute-done((f32[2,16,256]{2,1,0:T(8,128)S(1)}, f32[2,16,256]{2,1,0:T(8,128)S(1)}, u32[]{:S(2)}, u32[]{:S(2)}) %collective-permute-start.6) | collective-permute-done | bytes 32800 | tf_op jit(solution)/shard_map/ppermute | solution.py:465
  25.3 0.1 collective-permute-start.7
  25.4 1.2 %collective-permute-done.7.far = f32[3,16,256]{2,1,0:T(8,128)S(1)} collective-permute-done((f32[3,16,256]{2,1,0:T(8,128)S(1)}, f32[3,16,256]{2,1,0:T(8,128)S(1)}, u32[]{:S(2)}, u32[]{:S(2)}) %collective-permute-start.7) | collective-permute-done | bytes 49184 | tf_op jit(solution)/shard_map/ppermute | solution.py:465
  26.6 1.4 %next_kernel.1 = (f32[3,16,256]{2,1,0:T(8,128)S(1)}, f32[16,128]{1,0:T(8,128)S(1)}, f32[8,256]{1,0:T(8,128)S(1)}, f32[8,256]{1,0:T(8,128)S(1)}, f32[8,2048]{1,0:T(8,128)S(1)}, /*index=5*/f32[8,128]{1,0:T(8,128)S(1)}) custom-call(s32[1]{0:T(128)} %bitcast.where, f32[3,16,256]{2,1,0:T(8,128)S(1)} %add.50.chip, f32[3,16,256]{2,1,0:T(8,128)S(1)} %pad_maximum_fusion.1.near, ...), custom_call_target="tpu_custom_call" | custom-call | tf_op jit(solution)/shard_map/next_kernel/pallas_call | solution.py:416
  28.0 0.2 collective-permute-start.8
  28.2 1.1 %collective-permute-done.8 = f32[3,16,256]{2,1,0:T(8,128)S(1)} collective-permute-done((f32[3,16,256]{2,1,0:T(8,128)S(1)}, f32[3,16,256]{2,1,0:T(8,128)S(1)}, u32[]{:S(2)}, u32[]{:S(2)}) %collective-permute-start.8) | collective-permute-done | bytes 49184 | tf_op jit(solution)/shard_map/ppermute | solution.py:465
  29.3 0.8 %collective-permute-start.9 = (f32[2,16,256]{2,1,0:T(8,128)S(1)}, f32[2,16,256]{2,1,0:T(8,128)S(1)}, u32[]{:S(2)}, u32[]{:S(2)}) collective-permute-start(f32[2,16,256]{2,1,0:T(8,128)S(1)} %get-tuple-element.61), channel_id=1, source_target_pairs={{1,2},{3,4},{5,6},{7,8},{9,10},{11,12},{13,14},{15,16},{17,18},{19... | collective-permute-start | bytes 98312 | tf_op jit(solution)/shard_map/ppermute | solution.py:465
  30.2 4.3 %collective-permute-start.10 = (f32[2,16,256]{2,1,0:T(8,128)S(1)}, f32[2,16,256]{2,1,0:T(8,128)S(1)}, u32[]{:S(2)}, u32[]{:S(2)}) collective-permute-start(f32[2,16,256]{2,1,0:T(8,128)S(1)} %get-tuple-element.62), channel_id=1, source_target_pairs={{0,1},{2,3},{4,5},{6,7},{8,9},{10,11},{12,13},{14,15},{16,17},{18,... | collective-permute-start | bytes 98312 | tf_op jit(solution)/shard_map/ppermute | solution.py:465
  34.5 0.0 collective-permute-done.9
  34.5 1.3 %collective-permute-done.10 = f32[2,16,256]{2,1,0:T(8,128)S(1)} collective-permute-done((f32[2,16,256]{2,1,0:T(8,128)S(1)}, f32[2,16,256]{2,1,0:T(8,128)S(1)}, u32[]{:S(2)}, u32[]{:S(2)}) %collective-permute-start.10) | collective-permute-done | bytes 32800 | tf_op jit(solution)/shard_map/ppermute | solution.py:465
  35.8 0.1 collective-permute-start.11
  35.9 1.2 %collective-permute-done.11.far = f32[3,16,256]{2,1,0:T(8,128)S(1)} collective-permute-done((f32[3,16,256]{2,1,0:T(8,128)S(1)}, f32[3,16,256]{2,1,0:T(8,128)S(1)}, u32[]{:S(2)}, u32[]{:S(2)}) %collective-permute-start.11) | collective-permute-done | bytes 49184 | tf_op jit(solution)/shard_map/ppermute | solution.py:465
  37.1 1.2 %last_kernel.1 = (f32[16,128]{1,0:T(8,128)S(1)}, f32[8,256]{1,0:T(8,128)S(1)}, f32[128,32]{1,0:T(8,128)S(1)}) custom-call(s32[1]{0:T(128)} %bitcast.where, f32[3,16,256]{2,1,0:T(8,128)S(1)} %add.52.chip, f32[3,16,256]{2,1,0:T(8,128)S(1)} %pad_maximum_fusion.2.near, f32[3,16,256]{2,1,0:T(8,128)S(1)} %collective-permute-done.11.far, ...), custom_call_target="tpu_custom_call" | custom-call | tf_op jit(solution)/shard_map/last_kernel/pallas_call | solution.py:416
  38.4 24.3 %all_to_all.11 = f32[128,1,32]{2,1,0:T(1,128)S(1)} all-to-all(f32[128,1,32]{2,1,0:T(1,128)S(1)} %bitcast.8), channel_id=1, replica_groups=mesh['grp'=2,'reg_0'=4,'reg_1'=4,'reg_2'=4] {'grp','reg_0','reg_1','reg_2'}, dimensions={0} | all-to-all | bytes 32768 | tf_op jit(solution)/shard_map/all_to_all | solution.py:524
  62.7 1.2 %final_kernel.1 = (f32[9,128]{1,0:T(8,128)}, f32[3,256]{1,0:T(4,128)}) custom-call(f32[128,32]{1,0:T(8,128)S(1)} %bitcast.7, f32[16,128]{1,0:T(8,128)S(1)} %get-tuple-element.35.v_old.v0, f32[16,128]{1,0:T(8,128)S(1)} %get-tuple-element.39.v_old.v1, f32[16,128]{1,0:T(8,128)S(1)} %get-tuple-element.45.v2, f32[8,256]{1,0:T(8,128)S(1)} %get-tuple-element.46.g0, ...), custom_call_target="tpu_custom_call" | custom-call | tf_op jit(solution)/shard_map/final_kernel/pallas_call | solution.py:416
  (15 shorter events, 0.2 us)
Async XLA Ops:
  3.6 2.5 %collective-permute-start = (f32[3,56,256]{2,1,0:T(8,128)S(1)}, f32[3,56,256]{2,1,0:T(8,128)S(1)}, u32[]{:S(2)}, u32[]{:S(2)}) collective-permute-start(f32[3,56,256]{2,1,0:T(8,128)S(1)} %get-tuple-element.26), channel_id=1, source_target_pairs={{0,64},{1,65},{2,66},{3,67},{4,68},{5,69},{6,70},{7,71},{8,72},{9,... | collective-permute-start | bytes 516104 | tf_op jit(solution)/shard_map/ppermute | solution.py:465
  6.2 4.1 %collective-permute-start.1 = (f32[2,56,256]{2,1,0:T(8,128)S(1)}, f32[2,56,256]{2,1,0:T(8,128)S(1)}, u32[]{:S(2)}, u32[]{:S(2)}) collective-permute-start(f32[2,56,256]{2,1,0:T(8,128)S(1)} %get-tuple-element.52), channel_id=1, source_target_pairs={{1,2},{3,4},{5,6},{7,8},{9,10},{11,12},{13,14},{15,16},{17,18},{19... | collective-permute-start | bytes 344072 | tf_op jit(solution)/shard_map/ppermute | solution.py:465
  7.7 6.6 %collective-permute-start.2 = (f32[2,56,256]{2,1,0:T(8,128)S(1)}, f32[2,56,256]{2,1,0:T(8,128)S(1)}, u32[]{:S(2)}, u32[]{:S(2)}) collective-permute-start(f32[2,56,256]{2,1,0:T(8,128)S(1)} %get-tuple-element.53), channel_id=1, source_target_pairs={{0,1},{2,3},{4,5},{6,7},{8,9},{10,11},{12,13},{14,15},{16,17},{18,... | collective-permute-start | bytes 344072 | tf_op jit(solution)/shard_map/ppermute | solution.py:465
  14.3 1.5 %collective-permute-start.3 = (f32[3,56,256]{2,1,0:T(8,128)S(1)}, f32[3,56,256]{2,1,0:T(8,128)S(1)}, u32[]{:S(2)}, u32[]{:S(2)}) collective-permute-start(f32[3,56,256]{2,1,0:T(8,128)S(1)} %pad_maximum_fusion.near), channel_id=1, source_target_pairs={{0,64},{1,65},{2,66},{3,67},{4,68},{5,69},{6,70},{7,71},{8,72},{9,... | collective-permute-start | bytes 516104 | tf_op jit(solution)/shard_map/ppermute | solution.py:465
  17.4 1.3 %collective-permute-start.4 = (f32[3,16,256]{2,1,0:T(8,128)S(1)}, f32[3,16,256]{2,1,0:T(8,128)S(1)}, u32[]{:S(2)}, u32[]{:S(2)}) collective-permute-start(f32[3,16,256]{2,1,0:T(8,128)S(1)} %get-tuple-element.33), channel_id=1, source_target_pairs={{0,64},{1,65},{2,66},{3,67},{4,68},{5,69},{6,70},{7,71},{8,72},{9,... | collective-permute-start | bytes 147464 | tf_op jit(solution)/shard_map/ppermute | solution.py:465
  18.7 5.3 %collective-permute-start.5 = (f32[2,16,256]{2,1,0:T(8,128)S(1)}, f32[2,16,256]{2,1,0:T(8,128)S(1)}, u32[]{:S(2)}, u32[]{:S(2)}) collective-permute-start(f32[2,16,256]{2,1,0:T(8,128)S(1)} %get-tuple-element.63), channel_id=1, source_target_pairs={{1,2},{3,4},{5,6},{7,8},{9,10},{11,12},{13,14},{15,16},{17,18},{19... | collective-permute-start | bytes 98312 | tf_op jit(solution)/shard_map/ppermute | solution.py:465
  20.8 4.5 %collective-permute-start.6 = (f32[2,16,256]{2,1,0:T(8,128)S(1)}, f32[2,16,256]{2,1,0:T(8,128)S(1)}, u32[]{:S(2)}, u32[]{:S(2)}) collective-permute-start(f32[2,16,256]{2,1,0:T(8,128)S(1)} %get-tuple-element.64), channel_id=1, source_target_pairs={{0,1},{2,3},{4,5},{6,7},{8,9},{10,11},{12,13},{14,15},{16,17},{18,... | collective-permute-start | bytes 98312 | tf_op jit(solution)/shard_map/ppermute | solution.py:465
  25.3 1.3 %collective-permute-start.7 = (f32[3,16,256]{2,1,0:T(8,128)S(1)}, f32[3,16,256]{2,1,0:T(8,128)S(1)}, u32[]{:S(2)}, u32[]{:S(2)}) collective-permute-start(f32[3,16,256]{2,1,0:T(8,128)S(1)} %pad_maximum_fusion.1.near), channel_id=1, source_target_pairs={{0,64},{1,65},{2,66},{3,67},{4,68},{5,69},{6,70},{7,71},{8,72},{9,... | collective-permute-start | bytes 147464 | tf_op jit(solution)/shard_map/ppermute | solution.py:465
  28.0 1.3 %collective-permute-start.8 = (f32[3,16,256]{2,1,0:T(8,128)S(1)}, f32[3,16,256]{2,1,0:T(8,128)S(1)}, u32[]{:S(2)}, u32[]{:S(2)}) collective-permute-start(f32[3,16,256]{2,1,0:T(8,128)S(1)} %get-tuple-element.38), channel_id=1, source_target_pairs={{0,64},{1,65},{2,66},{3,67},{4,68},{5,69},{6,70},{7,71},{8,72},{9,... | collective-permute-start | bytes 147464 | tf_op jit(solution)/shard_map/ppermute | solution.py:465
  29.3 5.1 %collective-permute-start.9 = (f32[2,16,256]{2,1,0:T(8,128)S(1)}, f32[2,16,256]{2,1,0:T(8,128)S(1)}, u32[]{:S(2)}, u32[]{:S(2)}) collective-permute-start(f32[2,16,256]{2,1,0:T(8,128)S(1)} %get-tuple-element.61), channel_id=1, source_target_pairs={{1,2},{3,4},{5,6},{7,8},{9,10},{11,12},{13,14},{15,16},{17,18},{19... | collective-permute-start | bytes 98312 | tf_op jit(solution)/shard_map/ppermute | solution.py:465
  30.2 5.6 %collective-permute-start.10 = (f32[2,16,256]{2,1,0:T(8,128)S(1)}, f32[2,16,256]{2,1,0:T(8,128)S(1)}, u32[]{:S(2)}, u32[]{:S(2)}) collective-permute-start(f32[2,16,256]{2,1,0:T(8,128)S(1)} %get-tuple-element.62), channel_id=1, source_target_pairs={{0,1},{2,3},{4,5},{6,7},{8,9},{10,11},{12,13},{14,15},{16,17},{18,... | collective-permute-start | bytes 98312 | tf_op jit(solution)/shard_map/ppermute | solution.py:465
  35.8 1.3 %collective-permute-start.11 = (f32[3,16,256]{2,1,0:T(8,128)S(1)}, f32[3,16,256]{2,1,0:T(8,128)S(1)}, u32[]{:S(2)}, u32[]{:S(2)}) collective-permute-start(f32[3,16,256]{2,1,0:T(8,128)S(1)} %pad_maximum_fusion.2.near), channel_id=1, source_target_pairs={{0,64},{1,65},{2,66},{3,67},{4,68},{5,69},{6,70},{7,71},{8,72},{9,... | collective-permute-start | bytes 147464 | tf_op jit(solution)/shard_map/ppermute | solution.py:465

commit v7 on v6

--- a/solution.py
+++ b/solution.py
@@ -116,12 +116,18 @@
     return low, (owners & (regions - 1)) - region + 1
 
 
+def write_part(part, k, block):
+    rows = part.shape[0] // 6
+    for h in range(2):
+        at = (2 * k + h) * rows
+        part[at : at + rows, :] = block[0:rows, 128 * h : 128 * h + 128]
+
+
 def to_tiles(tiles, chip, near, far):
-    rows = chip.shape[1]
-    for k in range(3):
-        sums = chip[k] + (near[k] + far[k])
-        for h in range(2):
-            tiles[pl.ds(2 * k + h, rows, stride=8), :] = sums[:, 128 * h : 128 * h + 128]
+    rows = chip.shape[0] // 6
+    for k in range(6):
+        run = slice(k * rows, k * rows + rows)
+        tiles[pl.ds(k, rows, stride=8), :] = chip[run, :] + (near[run, :] + far[run, :])
     for k in (6, 7):
         tiles[pl.ds(k, rows, stride=8), :] = jnp.zeros((rows, 128), F32)
 
@@ -195,9 +201,12 @@
     edge = a[0] * last[0] + a[1] * last[1]
     gradient = a[0] * rem[0] + a[1] * rem[1]
     terms = stacked(jnp.concatenate(rolled + [edge, gradient], 0))
+    lhs = jnp.concatenate(
+        [terms * jnp.where(block == k, 1.0, 0.0).astype(BF16) for k in range(3)], 0
+    )
+    out = put(lhs, hot_c)
     for k in range(3):
-        mask = jnp.where(block == k, 1.0, 0.0).astype(BF16)
-        part[k] = folded(put(terms * mask, hot_c))
+        write_part(part, k, folded(out[3 * ROWS * k : 3 * ROWS * k + 3 * ROWS]))
 
 
 def solve_camera(low, inv, b):
@@ -278,7 +287,7 @@
     )
     out = put(lhs, hot_c)
     for k in range(3):
-        part[k] = folded(out[48 * k : 48 * k + 48])
+        write_part(part, k, folded(out[48 * k : 48 * k + 48]))
 
 
 def scalar_rows(pairs):
@@ -466,22 +475,23 @@
 
     def totals(part):
         chip = part + swap(part, cores)
-        lower, upper = chip[0:2], chip[1:3]
+        size = part.shape[0] // 3
+        lower, upper = chip[: 2 * size], chip[size:]
         from_outer = swap(jnp.where(rises, lower, upper), outer)
         from_inner = swap(jnp.where(rises, upper, lower), inner)
         up = jnp.where(above, jnp.where(rises, from_inner, from_outer), 0.0)
         down = jnp.where(below, jnp.where(rises, from_outer, from_inner), 0.0)
-        came = jnp.stack(
+        came = jnp.concatenate(
             [
-                jnp.where(near_core, down[0], down[1]),
-                jnp.where(near_core, down[1] + up[0], 0.0),
-                jnp.where(near_core, up[1], up[0]),
+                jnp.where(near_core, down[:size], down[size:]),
+                jnp.where(near_core, down[size:] + up[:size], 0.0),
+                jnp.where(near_core, up[size:], up[:size]),
             ]
         )
         return chip, came, swap(came, cores)
 
     def sums(rows):
-        return [shape(3, rows, WIDE)]
+        return [shape(6 * rows, 128)]
 
     run = functools.partial(call, scalar=True, regions=regions)
     field = pltpu.VMEM((128, 128), F32)
@@ -505,13 +515,13 @@
     common = (block, hot_p, hot_c, jx, px, vinv)
     part, factor, v0, g0, s0, rem0, scal0 = run(
         start_kernel,
-        sums(16) + [shape(45 * 8, 128)] + rest,
+        sums(9) + [shape(45 * 8, 128)] + rest,
         where, *totals(part), *common,
         scratch=[pltpu.VMEM((8 * ROWS, 128), F32), field],
     )
     part, v1, g1, s1, rem1, scal1 = run(
         next_kernel,
-        sums(16) + rest,
+        sums(9) + rest,
         where, *totals(part), factor, *common, v0, s0, rem0,
         scratch=[field, field],
     )

time: 64 us -> 63.3 us (0.989)
  no operation moved by 1% of the time
where the time goes in v7:
time: 63.3 us; the launch traced here: 63.2 us
  blocking collectives  24.4 us (39%)
  starting transfers between devices  16.9 us (27%)
  waiting for transfers between devices  13 us (21%)
  Pallas kernels  8.01 us (13%)
  between operations  0.74 us (1%)
    all_to_all x1, blocking collectives, local(): back = lax.all_to_all(scalar_sums, GRP_REG, 0, 0, tiled=True)  24.4 us
    ppermute x12, starting transfers between devices, swap(): return lax.ppermute(x, GRP_REG, pairs)  16.9 us
    ppermute x12, waiting for transfers between devices, swap(): return lax.ppermute(x, GRP_REG, pairs)  13 us
    pallas_call x5, Pallas kernels, call(): pl.pallas_call(kernel if regions is None else functools.partial(kernel, r...  8.01 us
  transfers between devices with their start and end apart: 12, of which 9 were waited for; matrix products, arithmetic and copies ran while one was open for 0% of the time, Pallas kernels for 0%

profile of v7, /device:TPU:1, one launch (start us, length us, event | category | flops | bytes accessed | tf_op | source)
XLA Modules:
  0.0 63.2 jit_solution(1298605263047440735)
XLA Ops:
  0.6 2.7 %first_kernel.1 = (f32[336,128]{1,0:T(8,128)S(1)}, f32[2,16,2048]{2,1,0:T(8,128)S(1)}, f32[2,8,2048]{2,1,0:T(8,128)S(1)}, f32[8,256]{1,0:T(8,128)S(1)}, f32[8,25...) custom-call(s32[1]{0:T(128)} %bitcast.where, ...), custom_call_target="tpu_custom_call" | custom-call | tf_op jit(solution)/shard_map/first_kernel/pallas_call | solution.py:425
  3.4 1.5 %collective-permute-start = (f32[336,128]{1,0:T(8,128)S(1)}, f32[336,128]{1,0:T(8,128)S(1)}, u32[]{:S(2)}, u32[]{:S(2)}) collective-permute-start(f32[336,128]{1,0:T(8,128)S(1)} %get-tuple-element.26), channel_id=1, source_target_pairs={{0,64},{1,65},{2,66},{3,67},{4,68},{5,69},{6,70},{7,71},{8,72},{9,... | collective-permute-start | bytes 516104 | tf_op jit(solution)/shard_map/ppermute | solution.py:474
  4.8 1.0 %collective-permute-done = f32[336,128]{1,0:T(8,128)S(1)} collective-permute-done((f32[336,128]{1,0:T(8,128)S(1)}, f32[336,128]{1,0:T(8,128)S(1)}, u32[]{:S(2)}, u32[]{:S(2)}) %collective-permute-start) | collective-permute-done | bytes 172064 | tf_op jit(solution)/shard_map/ppermute | solution.py:474
  5.9 1.5 %collective-permute-start.1 = (f32[224,128]{1,0:T(8,128)S(1)}, f32[224,128]{1,0:T(8,128)S(1)}, u32[]{:S(2)}, u32[]{:S(2)}) collective-permute-start(f32[224,128]{1,0:T(8,128)S(1)} %get-tuple-element.52), channel_id=1, source_target_pairs={{1,2},{3,4},{5,6},{7,8},{9,10},{11,12},{13,14},{15,16},{17,18},{19... | collective-permute-start | bytes 344072 | tf_op jit(solution)/shard_map/ppermute | solution.py:474
  7.4 2.6 %collective-permute-start.2 = (f32[224,128]{1,0:T(8,128)S(1)}, f32[224,128]{1,0:T(8,128)S(1)}, u32[]{:S(2)}, u32[]{:S(2)}) collective-permute-start(f32[224,128]{1,0:T(8,128)S(1)} %get-tuple-element.53), channel_id=1, source_target_pairs={{0,1},{2,3},{4,5},{6,7},{8,9},{10,11},{12,13},{14,15},{16,17},{18,... | collective-permute-start | bytes 344072 | tf_op jit(solution)/shard_map/ppermute | solution.py:474
  10.0 0.0 collective-permute-done.1
  10.0 4.0 %collective-permute-done.2 = f32[224,128]{1,0:T(8,128)S(1)} collective-permute-done((f32[224,128]{1,0:T(8,128)S(1)}, f32[224,128]{1,0:T(8,128)S(1)}, u32[]{:S(2)}, u32[]{:S(2)}) %collective-permute-start.2) | collective-permute-done | bytes 114720 | tf_op jit(solution)/shard_map/ppermute | solution.py:474
  14.0 0.3 collective-permute-start.3
  14.3 1.2 %collective-permute-done.3.far = f32[336,128]{1,0:T(8,128)S(1)} collective-permute-done((f32[336,128]{1,0:T(8,128)S(1)}, f32[336,128]{1,0:T(8,128)S(1)}, u32[]{:S(2)}, u32[]{:S(2)}) %collective-permute-start.3) | collective-permute-done | bytes 172064 | tf_op jit(solution)/shard_map/ppermute | solution.py:474
  15.5 1.5 %start_kernel.1 = (f32[54,128]{1,0:T(8,128)S(1)}, f32[360,128]{1,0:T(8,128)S(1)}, f32[16,128]{1,0:T(8,128)S(1)}, f32[8,256]{1,0:T(8,128)S(1)}, f32[8,256]{1,0:T(...) custom-call(s32[1]{0:T(128)} %bitcast.where, f32[336,128]{1,0:T(8,128)S(1)} %add.42.chip, ...), custom_call_target="tpu_custom_call" | custom-call | tf_op jit(solution)/shard_map/start_kernel/pallas_call | solution.py:425
  17.1 0.3 collective-permute-start.4
  17.3 1.0 %collective-permute-done.4 = f32[54,128]{1,0:T(8,128)S(1)} collective-permute-done((f32[54,128]{1,0:T(8,128)S(1)}, f32[54,128]{1,0:T(8,128)S(1)}, u32[]{:S(2)}, u32[]{:S(2)}) %collective-permute-start.4) | collective-permute-done | bytes 27680 | tf_op jit(solution)/shard_map/ppermute | solution.py:474
  18.4 2.1 %collective-permute-start.5 = (f32[36,128]{1,0:T(8,128)S(1)}, f32[36,128]{1,0:T(8,128)S(1)}, u32[]{:S(2)}, u32[]{:S(2)}) collective-permute-start(f32[36,128]{1,0:T(8,128)S(1)} %get-tuple-element.63), channel_id=1, source_target_pairs={{1,2},{3,4},{5,6},{7,8},{9,10},{11,12},{13,14},{15,16},{17,18},{19... | collective-permute-start | bytes 55304 | tf_op jit(solution)/shard_map/ppermute | solution.py:474
  20.5 3.2 %collective-permute-start.6 = (f32[36,128]{1,0:T(8,128)S(1)}, f32[36,128]{1,0:T(8,128)S(1)}, u32[]{:S(2)}, u32[]{:S(2)}) collective-permute-start(f32[36,128]{1,0:T(8,128)S(1)} %get-tuple-element.64), channel_id=1, source_target_pairs={{0,1},{2,3},{4,5},{6,7},{8,9},{10,11},{12,13},{14,15},{16,17},{18,... | collective-permute-start | bytes 55304 | tf_op jit(solution)/shard_map/ppermute | solution.py:474
  23.7 0.0 collective-permute-done.5
  23.7 1.2 %collective-permute-done.6 = f32[36,128]{1,0:T(8,128)S(1)} collective-permute-done((f32[36,128]{1,0:T(8,128)S(1)}, f32[36,128]{1,0:T(8,128)S(1)}, u32[]{:S(2)}, u32[]{:S(2)}) %collective-permute-start.6) | collective-permute-done | bytes 18464 | tf_op jit(solution)/shard_map/ppermute | solution.py:474
  24.9 0.1 collective-permute-start.7
  25.0 1.2 %collective-permute-done.7.far = f32[54,128]{1,0:T(8,128)S(1)} collective-permute-done((f32[54,128]{1,0:T(8,128)S(1)}, f32[54,128]{1,0:T(8,128)S(1)}, u32[]{:S(2)}, u32[]{:S(2)}) %collective-permute-start.7) | collective-permute-done | bytes 27680 | tf_op jit(solution)/shard_map/ppermute | solution.py:474
  26.1 1.4 %next_kernel.1 = (f32[54,128]{1,0:T(8,128)S(1)}, f32[16,128]{1,0:T(8,128)S(1)}, f32[8,256]{1,0:T(8,128)S(1)}, f32[8,256]{1,0:T(8,128)S(1)}, f32[8,2048]{1,0:T(8,128)S(1)}, /*index=5*/f32[8,128]{1,0:T(8,128)S(1)}) custom-call(s32[1]{0:T(128)} %bitcast.where, f32[54,128]{1,0:T(8,128)S(1)} %add.47.chip, f32[54,128]{1,0:T(8,128)S(1)} %pad_maximum_fusion.1.near, ...), custom_call_target="tpu_custom_call" | custom-call | tf_op jit(solution)/shard_map/next_kernel/pallas_call | solution.py:425
  27.5 0.2 collective-permute-start.8
  27.8 1.0 %collective-permute-done.8 = f32[54,128]{1,0:T(8,128)S(1)} collective-permute-done((f32[54,128]{1,0:T(8,128)S(1)}, f32[54,128]{1,0:T(8,128)S(1)}, u32[]{:S(2)}, u32[]{:S(2)}) %collective-permute-start.8) | collective-permute-done | bytes 27680 | tf_op jit(solution)/shard_map/ppermute | solution.py:474
  28.8 0.8 %collective-permute-start.9 = (f32[36,128]{1,0:T(8,128)S(1)}, f32[36,128]{1,0:T(8,128)S(1)}, u32[]{:S(2)}, u32[]{:S(2)}) collective-permute-start(f32[36,128]{1,0:T(8,128)S(1)} %get-tuple-element.61), channel_id=1, source_target_pairs={{1,2},{3,4},{5,6},{7,8},{9,10},{11,12},{13,14},{15,16},{17,18},{19... | collective-permute-start | bytes 55304 | tf_op jit(solution)/shard_map/ppermute | solution.py:474
  29.7 4.3 %collective-permute-start.10 = (f32[36,128]{1,0:T(8,128)S(1)}, f32[36,128]{1,0:T(8,128)S(1)}, u32[]{:S(2)}, u32[]{:S(2)}) collective-permute-start(f32[36,128]{1,0:T(8,128)S(1)} %get-tuple-element.62), channel_id=1, source_target_pairs={{0,1},{2,3},{4,5},{6,7},{8,9},{10,11},{12,13},{14,15},{16,17},{18,... | collective-permute-start | bytes 55304 | tf_op jit(solution)/shard_map/ppermute | solution.py:474
  33.9 0.0 collective-permute-done.9
  33.9 1.2 %collective-permute-done.10 = f32[36,128]{1,0:T(8,128)S(1)} collective-permute-done((f32[36,128]{1,0:T(8,128)S(1)}, f32[36,128]{1,0:T(8,128)S(1)}, u32[]{:S(2)}, u32[]{:S(2)}) %collective-permute-start.10) | collective-permute-done | bytes 18464 | tf_op jit(solution)/shard_map/ppermute | solution.py:474
  35.1 0.1 collective-permute-start.11
  35.2 1.2 %collective-permute-done.11.far = f32[54,128]{1,0:T(8,128)S(1)} collective-permute-done((f32[54,128]{1,0:T(8,128)S(1)}, f32[54,128]{1,0:T(8,128)S(1)}, u32[]{:S(2)}, u32[]{:S(2)}) %collective-permute-start.11) | collective-permute-done | bytes 27680 | tf_op jit(solution)/shard_map/ppermute | solution.py:474
  36.4 1.2 %last_kernel.1 = (f32[16,128]{1,0:T(8,128)S(1)}, f32[8,256]{1,0:T(8,128)S(1)}, f32[128,32]{1,0:T(8,128)S(1)}) custom-call(s32[1]{0:T(128)} %bitcast.where, f32[54,128]{1,0:T(8,128)S(1)} %add.49.chip, f32[54,128]{1,0:T(8,128)S(1)} %pad_maximum_fusion.2.near, f32[54,128]{1,0:T(8,128)S(1)} %collective-permute-done.11.far, ...), custom_call_target="tpu_custom_call" | custom-call | tf_op jit(solution)/shard_map/last_kernel/pallas_call | solution.py:425
  37.7 24.4 %all_to_all.11 = f32[128,1,32]{2,1,0:T(1,128)S(1)} all-to-all(f32[128,1,32]{2,1,0:T(1,128)S(1)} %bitcast.8), channel_id=1, replica_groups=mesh['grp'=2,'reg_0'=4,'reg_1'=4,'reg_2'=4] {'grp','reg_0','reg_1','reg_2'}, dimensions={0} | all-to-all | bytes 32768 | tf_op jit(solution)/shard_map/all_to_all | solution.py:534
  62.0 1.2 %final_kernel.1 = (f32[9,128]{1,0:T(8,128)}, f32[3,256]{1,0:T(4,128)}) custom-call(f32[128,32]{1,0:T(8,128)S(1)} %bitcast.7, f32[16,128]{1,0:T(8,128)S(1)} %get-tuple-element.35.v_old.v0, f32[16,128]{1,0:T(8,128)S(1)} %get-tuple-element.39.v_old.v1, f32[16,128]{1,0:T(8,128)S(1)} %get-tuple-element.45.v2, f32[8,256]{1,0:T(8,128)S(1)} %get-tuple-element.46.g0, ...), custom_call_target="tpu_custom_call" | custom-call | tf_op jit(solution)/shard_map/final_kernel/pallas_call | solution.py:425
  (15 shorter events, 0.2 us)
Async XLA Ops:
  3.4 2.5 %collective-permute-start = (f32[336,128]{1,0:T(8,128)S(1)}, f32[336,128]{1,0:T(8,128)S(1)}, u32[]{:S(2)}, u32[]{:S(2)}) collective-permute-start(f32[336,128]{1,0:T(8,128)S(1)} %get-tuple-element.26), channel_id=1, source_target_pairs={{0,64},{1,65},{2,66},{3,67},{4,68},{5,69},{6,70},{7,71},{8,72},{9,... | collective-permute-start | bytes 516104 | tf_op jit(solution)/shard_map/ppermute | solution.py:474
  5.9 4.1 %collective-permute-start.1 = (f32[224,128]{1,0:T(8,128)S(1)}, f32[224,128]{1,0:T(8,128)S(1)}, u32[]{:S(2)}, u32[]{:S(2)}) collective-permute-start(f32[224,128]{1,0:T(8,128)S(1)} %get-tuple-element.52), channel_id=1, source_target_pairs={{1,2},{3,4},{5,6},{7,8},{9,10},{11,12},{13,14},{15,16},{17,18},{19... | collective-permute-start | bytes 344072 | tf_op jit(solution)/shard_map/ppermute | solution.py:474
  7.4 6.6 %collective-permute-start.2 = (f32[224,128]{1,0:T(8,128)S(1)}, f32[224,128]{1,0:T(8,128)S(1)}, u32[]{:S(2)}, u32[]{:S(2)}) collective-permute-start(f32[224,128]{1,0:T(8,128)S(1)} %get-tuple-element.53), channel_id=1, source_target_pairs={{0,1},{2,3},{4,5},{6,7},{8,9},{10,11},{12,13},{14,15},{16,17},{18,... | collective-permute-start | bytes 344072 | tf_op jit(solution)/shard_map/ppermute | solution.py:474
  14.0 1.5 %collective-permute-start.3 = (f32[336,128]{1,0:T(8,128)S(1)}, f32[336,128]{1,0:T(8,128)S(1)}, u32[]{:S(2)}, u32[]{:S(2)}) collective-permute-start(f32[336,128]{1,0:T(8,128)S(1)} %pad_maximum_fusion.near), channel_id=1, source_target_pairs={{0,64},{1,65},{2,66},{3,67},{4,68},{5,69},{6,70},{7,71},{8,72},{9,... | collective-permute-start | bytes 516104 | tf_op jit(solution)/shard_map/ppermute | solution.py:474
  17.1 1.3 %collective-permute-start.4 = (f32[54,128]{1,0:T(8,128)S(1)}, f32[54,128]{1,0:T(8,128)S(1)}, u32[]{:S(2)}, u32[]{:S(2)}) collective-permute-start(f32[54,128]{1,0:T(8,128)S(1)} %get-tuple-element.33), channel_id=1, source_target_pairs={{0,64},{1,65},{2,66},{3,67},{4,68},{5,69},{6,70},{7,71},{8,72},{9,... | collective-permute-start | bytes 82952 | tf_op jit(solution)/shard_map/ppermute | solution.py:474
  18.4 5.3 %collective-permute-start.5 = (f32[36,128]{1,0:T(8,128)S(1)}, f32[36,128]{1,0:T(8,128)S(1)}, u32[]{:S(2)}, u32[]{:S(2)}) collective-permute-start(f32[36,128]{1,0:T(8,128)S(1)} %get-tuple-element.63), channel_id=1, source_target_pairs={{1,2},{3,4},{5,6},{7,8},{9,10},{11,12},{13,14},{15,16},{17,18},{19... | collective-permute-start | bytes 55304 | tf_op jit(solution)/shard_map/ppermute | solution.py:474
  20.5 4.3 %collective-permute-start.6 = (f32[36,128]{1,0:T(8,128)S(1)}, f32[36,128]{1,0:T(8,128)S(1)}, u32[]{:S(2)}, u32[]{:S(2)}) collective-permute-start(f32[36,128]{1,0:T(8,128)S(1)} %get-tuple-element.64), channel_id=1, source_target_pairs={{0,1},{2,3},{4,5},{6,7},{8,9},{10,11},{12,13},{14,15},{16,17},{18,... | collective-permute-start | bytes 55304 | tf_op jit(solution)/shard_map/ppermute | solution.py:474
  24.9 1.3 %collective-permute-start.7 = (f32[54,128]{1,0:T(8,128)S(1)}, f32[54,128]{1,0:T(8,128)S(1)}, u32[]{:S(2)}, u32[]{:S(2)}) collective-permute-start(f32[54,128]{1,0:T(8,128)S(1)} %pad_maximum_fusion.1.near), channel_id=1, source_target_pairs={{0,64},{1,65},{2,66},{3,67},{4,68},{5,69},{6,70},{7,71},{8,72},{9,... | collective-permute-start | bytes 82952 | tf_op jit(solution)/shard_map/ppermute | solution.py:474
  27.5 1.3 %collective-permute-start.8 = (f32[54,128]{1,0:T(8,128)S(1)}, f32[54,128]{1,0:T(8,128)S(1)}, u32[]{:S(2)}, u32[]{:S(2)}) collective-permute-start(f32[54,128]{1,0:T(8,128)S(1)} %get-tuple-element.38), channel_id=1, source_target_pairs={{0,64},{1,65},{2,66},{3,67},{4,68},{5,69},{6,70},{7,71},{8,72},{9,... | collective-permute-start | bytes 82952 | tf_op jit(solution)/shard_map/ppermute | solution.py:474
  28.8 5.1 %collective-permute-start.9 = (f32[36,128]{1,0:T(8,128)S(1)}, f32[36,128]{1,0:T(8,128)S(1)}, u32[]{:S(2)}, u32[]{:S(2)}) collective-permute-start(f32[36,128]{1,0:T(8,128)S(1)} %get-tuple-element.61), channel_id=1, source_target_pairs={{1,2},{3,4},{5,6},{7,8},{9,10},{11,12},{13,14},{15,16},{17,18},{19... | collective-permute-start | bytes 55304 | tf_op jit(solution)/shard_map/ppermute | solution.py:474
  29.7 5.4 %collective-permute-start.10 = (f32[36,128]{1,0:T(8,128)S(1)}, f32[36,128]{1,0:T(8,128)S(1)}, u32[]{:S(2)}, u32[]{:S(2)}) collective-permute-start(f32[36,128]{1,0:T(8,128)S(1)} %get-tuple-element.62), channel_id=1, source_target_pairs={{0,1},{2,3},{4,5},{6,7},{8,9},{10,11},{12,13},{14,15},{16,17},{18,... | collective-permute-start | bytes 55304 | tf_op jit(solution)/shard_map/ppermute | solution.py:474
  35.1 1.3 %collective-permute-start.11 = (f32[54,128]{1,0:T(8,128)S(1)}, f32[54,128]{1,0:T(8,128)S(1)}, u32[]{:S(2)}, u32[]{:S(2)}) collective-permute-start(f32[54,128]{1,0:T(8,128)S(1)} %pad_maximum_fusion.2.near), channel_id=1, source_target_pairs={{0,64},{1,65},{2,66},{3,67},{4,68},{5,69},{6,70},{7,71},{8,72},{9,... | collective-permute-start | bytes 82952 | tf_op jit(solution)/shard_map/ppermute | solution.py:474

commit v8 on v7

--- a/solution.py
+++ b/solution.py
@@ -261,20 +261,30 @@
     return low, [tile(factor, at + k) for k in range(9)]
 
 
+def parts_of(x):
+    return [part.astype(F32) for part in three_parts(x)]
+
+
 def apply_body(group, x, field, block, hot_p, hot_c, jx, px, vinv):
     for k in range(9):
         field[8 * k : 8 * k + 8, :] = x[k]
-    for k in range(9, 16):
-        field[8 * k : 8 * k + 8, :] = jnp.zeros((8, 128), F32)
     frames = [
-        jnp.concatenate([field[pl.ds(2 * f + h, 16, stride=8), :] for h in range(2)], 1)
+        jnp.concatenate([field[pl.ds(2 * f + h, 8, stride=8), :] for h in range(2)], 1)
         for f in range(3)
     ]
-    v = jnp.where(group == 0, frames[1][:, 0:128], frames[1][:, 128:256])
-    picked = pick(jnp.concatenate([stacked(f) for f in frames], 0), hot_c[...])
-    blocks = [folded(picked[48 * k : 48 * k + 48]) for k in range(3)]
+    ends = jnp.concatenate([field[pl.ds(64 + h, 4, stride=2), :] for h in range(2)], 1)
+    frames.append(jnp.concatenate([ends, jnp.zeros((4, WIDE), F32)], 0))
+    own = jnp.concatenate([frames[1], ends[1:2], jnp.zeros((7, WIDE), F32)], 0)
+    v = jnp.where(group == 0, own[:, 0:128], own[:, 128:256])
+    rows = [part for f in frames for part in parts_of(f)]
+    picked = pick(jnp.concatenate(rows, 0).astype(BF16), hot_c[...])
+    blocks = [folded(picked[24 * k : 24 * k + 24]) for k in range(4)]
     values = jnp.where(block == 0, blocks[0], jnp.where(block == 1, blocks[1], blocks[2]))
-    u = [jnp.sum(jx[i] * values, 0, keepdims=True) for i in range(2)]
+    end = jnp.where(lax.broadcasted_iota(jnp.int32, (8, OBS), 0) == block, blocks[3], 0.0)
+    u = [
+        jnp.sum(jx[i, 0:8, :] * values + jx[i, 8:9, :] * end, 0, keepdims=True)
+        for i in range(2)
+    ]
     p = [px[0], px[1]]
     g, s, ps = point_part(u, p, hot_p, vinv[...])
     return v, u, g, s, ps
@@ -375,50 +385,70 @@
     )
 
 
-def final_kernel(back, v0, v1, v2, g0, g1, g2, gres, vinv, cam, pnt):
+def final_kernel(back, v0, v1, v2, g0, g1, g2, gres, vinv, cam_hbm, pnt_hbm, cam, pnt, sems):
     sums = jnp.sum(back[...], 0, keepdims=True)
 
     def value(k):
-        return sums[:, k : k + 1]
+        return jnp.broadcast_to(sums[:, k : k + 1], (1, 128))
 
     m = [value(k) for k in (0, 2, 10, 11, 18)]
     s = [value(k) for k in (1, 8, 9, 16, 17)]
 
+    def added(terms):
+        while len(terms) > 1:
+            pairs = [terms[k] + terms[k + 1] for k in range(0, len(terms) - 1, 2)]
+            terms = pairs + terms[len(pairs) * 2 :]
+        return terms[0]
+
     def form(h, x):
-        terms = [x[i] * x[j] * h[i + j] for i in range(3) for j in range(3)]
-        return functools.reduce(lambda p, q: p + q, terms)
+        n = len(x)
+        squares = [
+            added([x[i] * x[k - i] for i in range(n) if 0 <= k - i < n]) for k in range(2 * n - 1)
+        ]
+        return added([h[k] * squares[k] for k in range(2 * n - 1)])
 
     def ratio(x, y):
         return jnp.where(y > 0, x / jnp.where(y > 0, y, 1.0), 0.0)
 
-    one, zero = jnp.ones((1, 1), F32), jnp.zeros((1, 1), F32)
-    y = [zero, zero, zero]
-    z = [one, zero, zero]
-    d = list(z)
+    step = ratio(m[0], s[0])
+    y = [step]
+    z = [1.0 - step, step]
+    d = [jnp.ones((1, 128), F32)]
     current = m[0]
-    for turn in range(3):
+    for turn in range(2):
+        following = form(m, z)
+        beta = ratio(following, current)
+        d = [p + beta * q for p, q in zip(z, d)] + [z[-1]]
+        current = following
         step = ratio(current, form(s, d))
-        y = [y[k] + step * d[k] for k in range(3)]
-        if turn < 2:
-            image = [d[0], d[1] - d[0], d[2] - d[1]]
-            z = [z[k] - step * image[k] for k in range(3)]
-            following = form(m, z)
-            beta = ratio(following, current)
-            d = [z[k] + beta * d[k] for k in range(3)]
-            current = following
+        y = [p + step * q for p, q in zip(y, d)] + [step * d[-1]]
+        if turn == 0:
+            image = [d[0], d[1] - d[0], -d[1]]
+            z = [p - step * q for p, q in zip(z + [0.0], image)]
     x = y[0] * v0[...] + y[1] * v1[...] + y[2] * v2[...]
     cam[...] = x[0:9]
+    copies = [
+        pltpu.make_async_copy(a, b, sems.at[k])
+        for k, (a, b) in enumerate([(cam, cam_hbm), (pnt, pnt_hbm)])
+    ]
+    copies[0].start()
+    y = [jnp.concatenate([c, c], 1) for c in y]
     g = gres[...] + (y[0] * g0[...] + y[1] * g1[...] + y[2] * g2[...])
     rows = solve_points(vinv[...], g)
     for k in range(3):
         pnt[k : k + 1, :] = -rows[k]
+    copies[1].start()
+    for copy in copies:
+        copy.wait()
 
 
 def shape(*dims, dtype=F32):
     return jax.ShapeDtypeStruct(dims, dtype)
 
 
-def call(kernel, outs, *args, scalar=False, scratch=(), regions=None, inputs=VMEM):
+def call(
+    kernel, outs, *args, scalar=False, scratch=(), regions=None, inputs=VMEM, outputs=VMEM
+):
     specs = [inputs] * len(args)
     if scalar:
         specs[0] = SMEM
@@ -426,7 +456,7 @@
         kernel if regions is None else functools.partial(kernel, regions),
         out_shape=outs,
         in_specs=specs,
-        out_specs=[VMEM] * len(outs),
+        out_specs=[outputs] * len(outs),
         scratch_shapes=scratch,
         compiler_params=pltpu.CompilerParams(vmem_limit_bytes=VMEM_LIMIT),
         name=kernel.__name__,
@@ -536,6 +566,11 @@
         final_kernel,
         [shape(9, C_DEV), shape(3, P_DEV)],
         back, v0, v1, v2, g0, g1, g2, gres, vinv,
+        scratch=[
+            pltpu.VMEM((9, C_DEV), F32), pltpu.VMEM((3, P_DEV), F32),
+            pltpu.SemaphoreType.DMA((2,)),
+        ],
+        outputs=HBM,
     )
 
 

time: 63.3 us -> 62.8 us (level)
  no operation moved by 1% of the time
where the time goes in v8:
time: 62.8 us; the launch traced here: 62.6 us
  blocking collectives  24.4 us (39%)
  starting transfers between devices  16.9 us (27%)
  waiting for transfers between devices  13 us (21%)
  Pallas kernels  7.46 us (12%)
  between operations  0.74 us (1%)
    all_to_all x1, blocking collectives, local(): back = lax.all_to_all(scalar_sums, GRP_REG, 0, 0, tiled=True)  24.4 us
    ppermute x12, starting transfers between devices, swap(): return lax.ppermute(x, GRP_REG, pairs)  16.9 us
    ppermute x12, waiting for transfers between devices, swap(): return lax.ppermute(x, GRP_REG, pairs)  13 us
    pallas_call x5, Pallas kernels, call(): pl.pallas_call(kernel if regions is None else functools.partial(kernel, r...  7.46 us
  transfers between devices with their start and end apart: 12, of which 9 were waited for; matrix products, arithmetic and copies ran while one was open for 0% of the time, Pallas kernels for 0%

profile of v8, /device:TPU:1, one launch (start us, length us, event | category | flops | bytes accessed | tf_op | source)
XLA Modules:
  0.0 62.6 jit_solution(7001700100177194746)
XLA Ops:
  0.6 2.7 %first_kernel.1 = (f32[336,128]{1,0:T(8,128)S(1)}, f32[2,16,2048]{2,1,0:T(8,128)S(1)}, f32[2,8,2048]{2,1,0:T(8,128)S(1)}, f32[8,256]{1,0:T(8,128)S(1)}, f32[8,25...) custom-call(s32[1]{0:T(128)} %bitcast.where, ...), custom_call_target="tpu_custom_call" | custom-call | tf_op jit(solution)/shard_map/first_kernel/pallas_call | solution.py:455
  3.4 1.5 %collective-permute-start = (f32[336,128]{1,0:T(8,128)S(1)}, f32[336,128]{1,0:T(8,128)S(1)}, u32[]{:S(2)}, u32[]{:S(2)}) collective-permute-start(f32[336,128]{1,0:T(8,128)S(1)} %get-tuple-element.26), channel_id=1, source_target_pairs={{0,64},{1,65},{2,66},{3,67},{4,68},{5,69},{6,70},{7,71},{8,72},{9,... | collective-permute-start | bytes 516104 | tf_op jit(solution)/shard_map/ppermute | solution.py:504
  4.8 1.0 %collective-permute-done = f32[336,128]{1,0:T(8,128)S(1)} collective-permute-done((f32[336,128]{1,0:T(8,128)S(1)}, f32[336,128]{1,0:T(8,128)S(1)}, u32[]{:S(2)}, u32[]{:S(2)}) %collective-permute-start) | collective-permute-done | bytes 172064 | tf_op jit(solution)/shard_map/ppermute | solution.py:504
  5.9 1.5 %collective-permute-start.1 = (f32[224,128]{1,0:T(8,128)S(1)}, f32[224,128]{1,0:T(8,128)S(1)}, u32[]{:S(2)}, u32[]{:S(2)}) collective-permute-start(f32[224,128]{1,0:T(8,128)S(1)} %get-tuple-element.52), channel_id=1, source_target_pairs={{1,2},{3,4},{5,6},{7,8},{9,10},{11,12},{13,14},{15,16},{17,18},{19... | collective-permute-start | bytes 344072 | tf_op jit(solution)/shard_map/ppermute | solution.py:504
  7.4 2.6 %collective-permute-start.2 = (f32[224,128]{1,0:T(8,128)S(1)}, f32[224,128]{1,0:T(8,128)S(1)}, u32[]{:S(2)}, u32[]{:S(2)}) collective-permute-start(f32[224,128]{1,0:T(8,128)S(1)} %get-tuple-element.53), channel_id=1, source_target_pairs={{0,1},{2,3},{4,5},{6,7},{8,9},{10,11},{12,13},{14,15},{16,17},{18,... | collective-permute-start | bytes 344072 | tf_op jit(solution)/shard_map/ppermute | solution.py:504
  10.0 0.0 collective-permute-done.1
  10.0 4.0 %collective-permute-done.2 = f32[224,128]{1,0:T(8,128)S(1)} collective-permute-done((f32[224,128]{1,0:T(8,128)S(1)}, f32[224,128]{1,0:T(8,128)S(1)}, u32[]{:S(2)}, u32[]{:S(2)}) %collective-permute-start.2) | collective-permute-done | bytes 114720 | tf_op jit(solution)/shard_map/ppermute | solution.py:504
  14.0 0.3 collective-permute-start.3
  14.3 1.2 %collective-permute-done.3.far = f32[336,128]{1,0:T(8,128)S(1)} collective-permute-done((f32[336,128]{1,0:T(8,128)S(1)}, f32[336,128]{1,0:T(8,128)S(1)}, u32[]{:S(2)}, u32[]{:S(2)}) %collective-permute-start.3) | collective-permute-done | bytes 172064 | tf_op jit(solution)/shard_map/ppermute | solution.py:504
  15.5 1.5 %start_kernel.1 = (f32[54,128]{1,0:T(8,128)S(1)}, f32[360,128]{1,0:T(8,128)S(1)}, f32[16,128]{1,0:T(8,128)S(1)}, f32[8,256]{1,0:T(8,128)S(1)}, f32[8,256]{1,0:T(...) custom-call(s32[1]{0:T(128)} %bitcast.where, f32[336,128]{1,0:T(8,128)S(1)} %add.42.chip, ...), custom_call_target="tpu_custom_call" | custom-call | tf_op jit(solution)/shard_map/start_kernel/pallas_call | solution.py:455
  17.0 0.3 collective-permute-start.4
  17.3 1.0 %collective-permute-done.4 = f32[54,128]{1,0:T(8,128)S(1)} collective-permute-done((f32[54,128]{1,0:T(8,128)S(1)}, f32[54,128]{1,0:T(8,128)S(1)}, u32[]{:S(2)}, u32[]{:S(2)}) %collective-permute-start.4) | collective-permute-done | bytes 27680 | tf_op jit(solution)/shard_map/ppermute | solution.py:504
  18.3 2.1 %collective-permute-start.5 = (f32[36,128]{1,0:T(8,128)S(1)}, f32[36,128]{1,0:T(8,128)S(1)}, u32[]{:S(2)}, u32[]{:S(2)}) collective-permute-start(f32[36,128]{1,0:T(8,128)S(1)} %get-tuple-element.63), channel_id=1, source_target_pairs={{1,2},{3,4},{5,6},{7,8},{9,10},{11,12},{13,14},{15,16},{17,18},{19... | collective-permute-start | bytes 55304 | tf_op jit(solution)/shard_map/ppermute | solution.py:504
  20.5 3.2 %collective-permute-start.6 = (f32[36,128]{1,0:T(8,128)S(1)}, f32[36,128]{1,0:T(8,128)S(1)}, u32[]{:S(2)}, u32[]{:S(2)}) collective-permute-start(f32[36,128]{1,0:T(8,128)S(1)} %get-tuple-element.64), channel_id=1, source_target_pairs={{0,1},{2,3},{4,5},{6,7},{8,9},{10,11},{12,13},{14,15},{16,17},{18,... | collective-permute-start | bytes 55304 | tf_op jit(solution)/shard_map/ppermute | solution.py:504
  23.6 0.0 collective-permute-done.5
  23.6 1.2 %collective-permute-done.6 = f32[36,128]{1,0:T(8,128)S(1)} collective-permute-done((f32[36,128]{1,0:T(8,128)S(1)}, f32[36,128]{1,0:T(8,128)S(1)}, u32[]{:S(2)}, u32[]{:S(2)}) %collective-permute-start.6) | collective-permute-done | bytes 18464 | tf_op jit(solution)/shard_map/ppermute | solution.py:504
  24.8 0.1 collective-permute-start.7
  24.9 1.2 %collective-permute-done.7.far = f32[54,128]{1,0:T(8,128)S(1)} collective-permute-done((f32[54,128]{1,0:T(8,128)S(1)}, f32[54,128]{1,0:T(8,128)S(1)}, u32[]{:S(2)}, u32[]{:S(2)}) %collective-permute-start.7) | collective-permute-done | bytes 27680 | tf_op jit(solution)/shard_map/ppermute | solution.py:504
  26.1 1.4 %next_kernel.1 = (f32[54,128]{1,0:T(8,128)S(1)}, f32[16,128]{1,0:T(8,128)S(1)}, f32[8,256]{1,0:T(8,128)S(1)}, f32[8,256]{1,0:T(8,128)S(1)}, f32[8,2048]{1,0:T(8,128)S(1)}, /*index=5*/f32[8,128]{1,0:T(8,128)S(1)}) custom-call(s32[1]{0:T(128)} %bitcast.where, f32[54,128]{1,0:T(8,128)S(1)} %add.47.chip, f32[54,128]{1,0:T(8,128)S(1)} %pad_maximum_fusion.1.near, ...), custom_call_target="tpu_custom_call" | custom-call | tf_op jit(solution)/shard_map/next_kernel/pallas_call | solution.py:455
  27.5 0.2 collective-permute-start.8
  27.7 1.0 %collective-permute-done.8 = f32[54,128]{1,0:T(8,128)S(1)} collective-permute-done((f32[54,128]{1,0:T(8,128)S(1)}, f32[54,128]{1,0:T(8,128)S(1)}, u32[]{:S(2)}, u32[]{:S(2)}) %collective-permute-start.8) | collective-permute-done | bytes 27680 | tf_op jit(solution)/shard_map/ppermute | solution.py:504
  28.8 0.8 %collective-permute-start.9 = (f32[36,128]{1,0:T(8,128)S(1)}, f32[36,128]{1,0:T(8,128)S(1)}, u32[]{:S(2)}, u32[]{:S(2)}) collective-permute-start(f32[36,128]{1,0:T(8,128)S(1)} %get-tuple-element.61), channel_id=1, source_target_pairs={{1,2},{3,4},{5,6},{7,8},{9,10},{11,12},{13,14},{15,16},{17,18},{19... | collective-permute-start | bytes 55304 | tf_op jit(solution)/shard_map/ppermute | solution.py:504
  29.6 4.3 %collective-permute-start.10 = (f32[36,128]{1,0:T(8,128)S(1)}, f32[36,128]{1,0:T(8,128)S(1)}, u32[]{:S(2)}, u32[]{:S(2)}) collective-permute-start(f32[36,128]{1,0:T(8,128)S(1)} %get-tuple-element.62), channel_id=1, source_target_pairs={{0,1},{2,3},{4,5},{6,7},{8,9},{10,11},{12,13},{14,15},{16,17},{18,... | collective-permute-start | bytes 55304 | tf_op jit(solution)/shard_map/ppermute | solution.py:504
  33.9 0.0 collective-permute-done.9
  33.9 1.2 %collective-permute-done.10 = f32[36,128]{1,0:T(8,128)S(1)} collective-permute-done((f32[36,128]{1,0:T(8,128)S(1)}, f32[36,128]{1,0:T(8,128)S(1)}, u32[]{:S(2)}, u32[]{:S(2)}) %collective-permute-start.10) | collective-permute-done | bytes 18464 | tf_op jit(solution)/shard_map/ppermute | solution.py:504
  35.1 0.1 collective-permute-start.11
  35.2 1.2 %collective-permute-done.11.far = f32[54,128]{1,0:T(8,128)S(1)} collective-permute-done((f32[54,128]{1,0:T(8,128)S(1)}, f32[54,128]{1,0:T(8,128)S(1)}, u32[]{:S(2)}, u32[]{:S(2)}) %collective-permute-start.11) | collective-permute-done | bytes 27680 | tf_op jit(solution)/shard_map/ppermute | solution.py:504
  36.4 1.1 %last_kernel.1 = (f32[16,128]{1,0:T(8,128)S(1)}, f32[8,256]{1,0:T(8,128)S(1)}, f32[128,32]{1,0:T(8,128)S(1)}) custom-call(s32[1]{0:T(128)} %bitcast.where, f32[54,128]{1,0:T(8,128)S(1)} %add.49.chip, f32[54,128]{1,0:T(8,128)S(1)} %pad_maximum_fusion.2.near, f32[54,128]{1,0:T(8,128)S(1)} %collective-permute-done.11.far, ...), custom_call_target="tpu_custom_call" | custom-call | tf_op jit(solution)/shard_map/last_kernel/pallas_call | solution.py:455
  37.5 24.4 %all_to_all.11 = f32[128,1,32]{2,1,0:T(1,128)S(1)} all-to-all(f32[128,1,32]{2,1,0:T(1,128)S(1)} %bitcast.8), channel_id=1, replica_groups=mesh['grp'=2,'reg_0'=4,'reg_1'=4,'reg_2'=4] {'grp','reg_0','reg_1','reg_2'}, dimensions={0} | all-to-all | bytes 32768 | tf_op jit(solution)/shard_map/all_to_all | solution.py:564
  61.9 0.8 %final_kernel.1 = (f32[9,128]{1,0:T(8,128)}, f32[3,256]{1,0:T(4,128)}) custom-call(f32[128,32]{1,0:T(8,128)S(1)} %bitcast.7, f32[16,128]{1,0:T(8,128)S(1)} %get-tuple-element.35.v_old.v0, f32[16,128]{1,0:T(8,128)S(1)} %get-tuple-element.39.v_old.v1, f32[16,128]{1,0:T(8,128)S(1)} %get-tuple-element.45.v2, f32[8,256]{1,0:T(8,128)S(1)} %get-tuple-element.46.g0, ...), custom_call_target="tpu_custom_call" | custom-call | tf_op jit(solution)/shard_map/final_kernel/pallas_call | solution.py:455
  (15 shorter events, 0.2 us)
Async XLA Ops:
  3.4 2.5 %collective-permute-start = (f32[336,128]{1,0:T(8,128)S(1)}, f32[336,128]{1,0:T(8,128)S(1)}, u32[]{:S(2)}, u32[]{:S(2)}) collective-permute-start(f32[336,128]{1,0:T(8,128)S(1)} %get-tuple-element.26), channel_id=1, source_target_pairs={{0,64},{1,65},{2,66},{3,67},{4,68},{5,69},{6,70},{7,71},{8,72},{9,... | collective-permute-start | bytes 516104 | tf_op jit(solution)/shard_map/ppermute | solution.py:504
  5.9 4.1 %collective-permute-start.1 = (f32[224,128]{1,0:T(8,128)S(1)}, f32[224,128]{1,0:T(8,128)S(1)}, u32[]{:S(2)}, u32[]{:S(2)}) collective-permute-start(f32[224,128]{1,0:T(8,128)S(1)} %get-tuple-element.52), channel_id=1, source_target_pairs={{1,2},{3,4},{5,6},{7,8},{9,10},{11,12},{13,14},{15,16},{17,18},{19... | collective-permute-start | bytes 344072 | tf_op jit(solution)/shard_map/ppermute | solution.py:504
  7.4 6.6 %collective-permute-start.2 = (f32[224,128]{1,0:T(8,128)S(1)}, f32[224,128]{1,0:T(8,128)S(1)}, u32[]{:S(2)}, u32[]{:S(2)}) collective-permute-start(f32[224,128]{1,0:T(8,128)S(1)} %get-tuple-element.53), channel_id=1, source_target_pairs={{0,1},{2,3},{4,5},{6,7},{8,9},{10,11},{12,13},{14,15},{16,17},{18,... | collective-permute-start | bytes 344072 | tf_op jit(solution)/shard_map/ppermute | solution.py:504
  14.0 1.5 %collective-permute-start.3 = (f32[336,128]{1,0:T(8,128)S(1)}, f32[336,128]{1,0:T(8,128)S(1)}, u32[]{:S(2)}, u32[]{:S(2)}) collective-permute-start(f32[336,128]{1,0:T(8,128)S(1)} %pad_maximum_fusion.near), channel_id=1, source_target_pairs={{0,64},{1,65},{2,66},{3,67},{4,68},{5,69},{6,70},{7,71},{8,72},{9,... | collective-permute-start | bytes 516104 | tf_op jit(solution)/shard_map/ppermute | solution.py:504
  17.0 1.3 %collective-permute-start.4 = (f32[54,128]{1,0:T(8,128)S(1)}, f32[54,128]{1,0:T(8,128)S(1)}, u32[]{:S(2)}, u32[]{:S(2)}) collective-permute-start(f32[54,128]{1,0:T(8,128)S(1)} %get-tuple-element.33), channel_id=1, source_target_pairs={{0,64},{1,65},{2,66},{3,67},{4,68},{5,69},{6,70},{7,71},{8,72},{9,... | collective-permute-start | bytes 82952 | tf_op jit(solution)/shard_map/ppermute | solution.py:504
  18.3 5.3 %collective-permute-start.5 = (f32[36,128]{1,0:T(8,128)S(1)}, f32[36,128]{1,0:T(8,128)S(1)}, u32[]{:S(2)}, u32[]{:S(2)}) collective-permute-start(f32[36,128]{1,0:T(8,128)S(1)} %get-tuple-element.63), channel_id=1, source_target_pairs={{1,2},{3,4},{5,6},{7,8},{9,10},{11,12},{13,14},{15,16},{17,18},{19... | collective-permute-start | bytes 55304 | tf_op jit(solution)/shard_map/ppermute | solution.py:504
  20.5 4.3 %collective-permute-start.6 = (f32[36,128]{1,0:T(8,128)S(1)}, f32[36,128]{1,0:T(8,128)S(1)}, u32[]{:S(2)}, u32[]{:S(2)}) collective-permute-start(f32[36,128]{1,0:T(8,128)S(1)} %get-tuple-element.64), channel_id=1, source_target_pairs={{0,1},{2,3},{4,5},{6,7},{8,9},{10,11},{12,13},{14,15},{16,17},{18,... | collective-permute-start | bytes 55304 | tf_op jit(solution)/shard_map/ppermute | solution.py:504
  24.8 1.3 %collective-permute-start.7 = (f32[54,128]{1,0:T(8,128)S(1)}, f32[54,128]{1,0:T(8,128)S(1)}, u32[]{:S(2)}, u32[]{:S(2)}) collective-permute-start(f32[54,128]{1,0:T(8,128)S(1)} %pad_maximum_fusion.1.near), channel_id=1, source_target_pairs={{0,64},{1,65},{2,66},{3,67},{4,68},{5,69},{6,70},{7,71},{8,72},{9,... | collective-permute-start | bytes 82952 | tf_op jit(solution)/shard_map/ppermute | solution.py:504
  27.5 1.3 %collective-permute-start.8 = (f32[54,128]{1,0:T(8,128)S(1)}, f32[54,128]{1,0:T(8,128)S(1)}, u32[]{:S(2)}, u32[]{:S(2)}) collective-permute-start(f32[54,128]{1,0:T(8,128)S(1)} %get-tuple-element.38), channel_id=1, source_target_pairs={{0,64},{1,65},{2,66},{3,67},{4,68},{5,69},{6,70},{7,71},{8,72},{9,... | collective-permute-start | bytes 82952 | tf_op jit(solution)/shard_map/ppermute | solution.py:504
  28.8 5.1 %collective-permute-start.9 = (f32[36,128]{1,0:T(8,128)S(1)}, f32[36,128]{1,0:T(8,128)S(1)}, u32[]{:S(2)}, u32[]{:S(2)}) collective-permute-start(f32[36,128]{1,0:T(8,128)S(1)} %get-tuple-element.61), channel_id=1, source_target_pairs={{1,2},{3,4},{5,6},{7,8},{9,10},{11,12},{13,14},{15,16},{17,18},{19... | collective-permute-start | bytes 55304 | tf_op jit(solution)/shard_map/ppermute | solution.py:504
  29.6 5.4 %collective-permute-start.10 = (f32[36,128]{1,0:T(8,128)S(1)}, f32[36,128]{1,0:T(8,128)S(1)}, u32[]{:S(2)}, u32[]{:S(2)}) collective-permute-start(f32[36,128]{1,0:T(8,128)S(1)} %get-tuple-element.62), channel_id=1, source_target_pairs={{0,1},{2,3},{4,5},{6,7},{8,9},{10,11},{12,13},{14,15},{16,17},{18,... | collective-permute-start | bytes 55304 | tf_op jit(solution)/shard_map/ppermute | solution.py:504
  35.1 1.3 %collective-permute-start.11 = (f32[54,128]{1,0:T(8,128)S(1)}, f32[54,128]{1,0:T(8,128)S(1)}, u32[]{:S(2)}, u32[]{:S(2)}) collective-permute-start(f32[54,128]{1,0:T(8,128)S(1)} %pad_maximum_fusion.2.near), channel_id=1, source_target_pairs={{0,64},{1,65},{2,66},{3,67},{4,68},{5,69},{6,70},{7,71},{8,72},{9,... | collective-permute-start | bytes 82952 | tf_op jit(solution)/shard_map/ppermute | solution.py:504

commit v9 on v8

--- a/solution.py
+++ b/solution.py
@@ -92,15 +92,12 @@
 
 
 def solve_points(vinv, g):
-    a, b, c, d, e, f = [vinv[k : k + 1] for k in range(6)]
-    x, y, z = [g[k : k + 1] for k in range(3)]
-    rows = [a * x + b * y + c * z, b * x + d * y + e * z, c * x + e * y + f * z]
-    return rows + [jnp.zeros((8 - 3, g.shape[1]), F32)]
+    return vinv[0:8] * g[0:1] + vinv[8:16] * g[1:2] + vinv[16:24] * g[2:3]
 
 
 def point_part(u, p, hot_p, vinv):
     g = folded(put_few(stacked(p[0] * u[0] + p[1] * u[1]), hot_p))
-    s = jnp.concatenate(solve_points(vinv, g), 0)
+    s = solve_points(vinv, g)
     back = folded(pick(stacked(s), hot_p[...]))
     return g, s, [jnp.sum(p[i] * back, 0, keepdims=True) for i in range(2)]
 
@@ -182,13 +179,13 @@
     c12 = v01 * v02 - v00 * v12
     c22 = v00 * v11 - v01 * v01
     scale = 1.0 / (v00 * c00 + v01 * c01 + v02 * c02)
-    cofactors = jnp.concatenate(
-        [c00, c01, c02, c11, c12, c22, jnp.zeros((2, P_DEV), F32)], 0
-    )
+    rest = [jnp.zeros((5, P_DEV), F32)]
+    columns = [c00, c01, c02] + rest + [c01, c11, c12] + rest + [c02, c12, c22] + rest
+    cofactors = jnp.concatenate(columns, 0)
     vinv = cofactors * scale
     vinv_out[...] = vinv
     gres_out[...] = g
-    s = jnp.concatenate(solve_points(vinv, g), 0)
+    s = solve_points(vinv, g)
     back = folded(pick(stacked(s), hot_p[...]))
     rem = [r[i] - jnp.sum(p[i] * back, 0, keepdims=True) for i in range(2)]
     rolled = []
@@ -434,9 +431,7 @@
     copies[0].start()
     y = [jnp.concatenate([c, c], 1) for c in y]
     g = gres[...] + (y[0] * g0[...] + y[1] * g1[...] + y[2] * g2[...])
-    rows = solve_points(vinv[...], g)
-    for k in range(3):
-        pnt[k : k + 1, :] = -rows[k]
+    pnt[...] = -solve_points(vinv[...], g)[0:3]
     copies[1].start()
     for copy in copies:
         copy.wait()
@@ -531,7 +526,7 @@
     part, jx, px, vinv, gres, block, hot_p, hot_c = run(
         first_kernel,
         sums(ROWS)
-        + [shape(2, 16, OBS), shape(2, 8, OBS), per_point, per_point]
+        + [shape(2, 16, OBS), shape(2, 8, OBS), shape(24, P_DEV), per_point]
         + [shape(1, OBS, dtype=jnp.int32)]
         + [shape(WIDE, OBS, dtype=BF16)] * 2,
         where, *arrays,

time: 62.8 us -> 62.8 us (level)
  no operation moved by 1% of the time
where the time goes in v9:
time: 62.8 us; the launch traced here: 62.6 us
  blocking collectives  24.4 us (39%)
  starting transfers between devices  16.9 us (27%)
  waiting for transfers between devices  13 us (21%)
  Pallas kernels  7.44 us (12%)
  between operations  0.74 us (1%)
    all_to_all x1, blocking collectives, local(): back = lax.all_to_all(scalar_sums, GRP_REG, 0, 0, tiled=True)  24.4 us
    ppermute x12, starting transfers between devices, swap(): return lax.ppermute(x, GRP_REG, pairs)  16.9 us
    ppermute x12, waiting for transfers between devices, swap(): return lax.ppermute(x, GRP_REG, pairs)  13 us
    pallas_call x5, Pallas kernels, call(): pl.pallas_call(kernel if regions is None else functools.partial(kernel, r...  7.44 us
  transfers between devices with their start and end apart: 12, of which 9 were waited for; matrix products, arithmetic and copies ran while one was open for 0% of the time, Pallas kernels for 0%

profile of v9, /device:TPU:1, one launch (start us, length us, event | category | flops | bytes accessed | tf_op | source)
XLA Modules:
  0.0 62.6 jit_solution(13110740975596466410)
XLA Ops:
  0.6 2.7 %first_kernel.1 = (f32[336,128]{1,0:T(8,128)S(1)}, f32[2,16,2048]{2,1,0:T(8,128)S(1)}, f32[2,8,2048]{2,1,0:T(8,128)S(1)}, f32[24,256]{1,0:T(8,128)S(1)}, f32[8,2...) custom-call(s32[1]{0:T(128)} %bitcast.where, ...), custom_call_target="tpu_custom_call" | custom-call | tf_op jit(solution)/shard_map/first_kernel/pallas_call | solution.py:450
  3.3 1.5 %collective-permute-start = (f32[336,128]{1,0:T(8,128)S(1)}, f32[336,128]{1,0:T(8,128)S(1)}, u32[]{:S(2)}, u32[]{:S(2)}) collective-permute-start(f32[336,128]{1,0:T(8,128)S(1)} %get-tuple-element.26), channel_id=1, source_target_pairs={{0,64},{1,65},{2,66},{3,67},{4,68},{5,69},{6,70},{7,71},{8,72},{9,... | collective-permute-start | bytes 516104 | tf_op jit(solution)/shard_map/ppermute | solution.py:499
  4.8 1.0 %collective-permute-done = f32[336,128]{1,0:T(8,128)S(1)} collective-permute-done((f32[336,128]{1,0:T(8,128)S(1)}, f32[336,128]{1,0:T(8,128)S(1)}, u32[]{:S(2)}, u32[]{:S(2)}) %collective-permute-start) | collective-permute-done | bytes 172064 | tf_op jit(solution)/shard_map/ppermute | solution.py:499
  5.9 1.5 %collective-permute-start.1 = (f32[224,128]{1,0:T(8,128)S(1)}, f32[224,128]{1,0:T(8,128)S(1)}, u32[]{:S(2)}, u32[]{:S(2)}) collective-permute-start(f32[224,128]{1,0:T(8,128)S(1)} %get-tuple-element.52), channel_id=1, source_target_pairs={{1,2},{3,4},{5,6},{7,8},{9,10},{11,12},{13,14},{15,16},{17,18},{19... | collective-permute-start | bytes 344072 | tf_op jit(solution)/shard_map/ppermute | solution.py:499
  7.4 2.6 %collective-permute-start.2 = (f32[224,128]{1,0:T(8,128)S(1)}, f32[224,128]{1,0:T(8,128)S(1)}, u32[]{:S(2)}, u32[]{:S(2)}) collective-permute-start(f32[224,128]{1,0:T(8,128)S(1)} %get-tuple-element.53), channel_id=1, source_target_pairs={{0,1},{2,3},{4,5},{6,7},{8,9},{10,11},{12,13},{14,15},{16,17},{18,... | collective-permute-start | bytes 344072 | tf_op jit(solution)/shard_map/ppermute | solution.py:499
  10.0 0.0 collective-permute-done.1
  10.0 4.0 %collective-permute-done.2 = f32[224,128]{1,0:T(8,128)S(1)} collective-permute-done((f32[224,128]{1,0:T(8,128)S(1)}, f32[224,128]{1,0:T(8,128)S(1)}, u32[]{:S(2)}, u32[]{:S(2)}) %collective-permute-start.2) | collective-permute-done | bytes 114720 | tf_op jit(solution)/shard_map/ppermute | solution.py:499
  14.0 0.3 collective-permute-start.3
  14.3 1.2 %collective-permute-done.3.far = f32[336,128]{1,0:T(8,128)S(1)} collective-permute-done((f32[336,128]{1,0:T(8,128)S(1)}, f32[336,128]{1,0:T(8,128)S(1)}, u32[]{:S(2)}, u32[]{:S(2)}) %collective-permute-start.3) | collective-permute-done | bytes 172064 | tf_op jit(solution)/shard_map/ppermute | solution.py:499
  15.5 1.5 %start_kernel.1 = (f32[54,128]{1,0:T(8,128)S(1)}, f32[360,128]{1,0:T(8,128)S(1)}, f32[16,128]{1,0:T(8,128)S(1)}, f32[8,256]{1,0:T(8,128)S(1)}, f32[8,256]{1,0:T(...) custom-call(s32[1]{0:T(128)} %bitcast.where, f32[336,128]{1,0:T(8,128)S(1)} %add.42.chip, ...), custom_call_target="tpu_custom_call" | custom-call | tf_op jit(solution)/shard_map/start_kernel/pallas_call | solution.py:450
  17.0 0.3 collective-permute-start.4
  17.3 1.0 %collective-permute-done.4 = f32[54,128]{1,0:T(8,128)S(1)} collective-permute-done((f32[54,128]{1,0:T(8,128)S(1)}, f32[54,128]{1,0:T(8,128)S(1)}, u32[]{:S(2)}, u32[]{:S(2)}) %collective-permute-start.4) | collective-permute-done | bytes 27680 | tf_op jit(solution)/shard_map/ppermute | solution.py:499
  18.3 2.1 %collective-permute-start.5 = (f32[36,128]{1,0:T(8,128)S(1)}, f32[36,128]{1,0:T(8,128)S(1)}, u32[]{:S(2)}, u32[]{:S(2)}) collective-permute-start(f32[36,128]{1,0:T(8,128)S(1)} %get-tuple-element.63), channel_id=1, source_target_pairs={{1,2},{3,4},{5,6},{7,8},{9,10},{11,12},{13,14},{15,16},{17,18},{19... | collective-permute-start | bytes 55304 | tf_op jit(solution)/shard_map/ppermute | solution.py:499
  20.5 3.2 %collective-permute-start.6 = (f32[36,128]{1,0:T(8,128)S(1)}, f32[36,128]{1,0:T(8,128)S(1)}, u32[]{:S(2)}, u32[]{:S(2)}) collective-permute-start(f32[36,128]{1,0:T(8,128)S(1)} %get-tuple-element.64), channel_id=1, source_target_pairs={{0,1},{2,3},{4,5},{6,7},{8,9},{10,11},{12,13},{14,15},{16,17},{18,... | collective-permute-start | bytes 55304 | tf_op jit(solution)/shard_map/ppermute | solution.py:499
  23.6 0.0 collective-permute-done.5
  23.6 1.2 %collective-permute-done.6 = f32[36,128]{1,0:T(8,128)S(1)} collective-permute-done((f32[36,128]{1,0:T(8,128)S(1)}, f32[36,128]{1,0:T(8,128)S(1)}, u32[]{:S(2)}, u32[]{:S(2)}) %collective-permute-start.6) | collective-permute-done | bytes 18464 | tf_op jit(solution)/shard_map/ppermute | solution.py:499
  24.8 0.1 collective-permute-start.7
  24.9 1.2 %collective-permute-done.7.far = f32[54,128]{1,0:T(8,128)S(1)} collective-permute-done((f32[54,128]{1,0:T(8,128)S(1)}, f32[54,128]{1,0:T(8,128)S(1)}, u32[]{:S(2)}, u32[]{:S(2)}) %collective-permute-start.7) | collective-permute-done | bytes 27680 | tf_op jit(solution)/shard_map/ppermute | solution.py:499
  26.1 1.3 %next_kernel.1 = (f32[54,128]{1,0:T(8,128)S(1)}, f32[16,128]{1,0:T(8,128)S(1)}, f32[8,256]{1,0:T(8,128)S(1)}, f32[8,256]{1,0:T(8,128)S(1)}, f32[8,2048]{1,0:T(8,128)S(1)}, /*index=5*/f32[8,128]{1,0:T(8,128)S(1)}) custom-call(s32[1]{0:T(128)} %bitcast.where, f32[54,128]{1,0:T(8,128)S(1)} %add.47.chip, f32[54,128]{1,0:T(8,128)S(1)} %pad_maximum_fusion.1.near, ...), custom_call_target="tpu_custom_call" | custom-call | tf_op jit(solution)/shard_map/next_kernel/pallas_call | solution.py:450
  27.5 0.2 collective-permute-start.8
  27.7 1.0 %collective-permute-done.8 = f32[54,128]{1,0:T(8,128)S(1)} collective-permute-done((f32[54,128]{1,0:T(8,128)S(1)}, f32[54,128]{1,0:T(8,128)S(1)}, u32[]{:S(2)}, u32[]{:S(2)}) %collective-permute-start.8) | collective-permute-done | bytes 27680 | tf_op jit(solution)/shard_map/ppermute | solution.py:499
  28.8 0.8 %collective-permute-start.9 = (f32[36,128]{1,0:T(8,128)S(1)}, f32[36,128]{1,0:T(8,128)S(1)}, u32[]{:S(2)}, u32[]{:S(2)}) collective-permute-start(f32[36,128]{1,0:T(8,128)S(1)} %get-tuple-element.61), channel_id=1, source_target_pairs={{1,2},{3,4},{5,6},{7,8},{9,10},{11,12},{13,14},{15,16},{17,18},{19... | collective-permute-start | bytes 55304 | tf_op jit(solution)/shard_map/ppermute | solution.py:499
  29.6 4.3 %collective-permute-start.10 = (f32[36,128]{1,0:T(8,128)S(1)}, f32[36,128]{1,0:T(8,128)S(1)}, u32[]{:S(2)}, u32[]{:S(2)}) collective-permute-start(f32[36,128]{1,0:T(8,128)S(1)} %get-tuple-element.62), channel_id=1, source_target_pairs={{0,1},{2,3},{4,5},{6,7},{8,9},{10,11},{12,13},{14,15},{16,17},{18,... | collective-permute-start | bytes 55304 | tf_op jit(solution)/shard_map/ppermute | solution.py:499
  33.9 0.0 collective-permute-done.9
  33.9 1.2 %collective-permute-done.10 = f32[36,128]{1,0:T(8,128)S(1)} collective-permute-done((f32[36,128]{1,0:T(8,128)S(1)}, f32[36,128]{1,0:T(8,128)S(1)}, u32[]{:S(2)}, u32[]{:S(2)}) %collective-permute-start.10) | collective-permute-done | bytes 18464 | tf_op jit(solution)/shard_map/ppermute | solution.py:499
  35.1 0.1 collective-permute-start.11
  35.2 1.2 %collective-permute-done.11.far = f32[54,128]{1,0:T(8,128)S(1)} collective-permute-done((f32[54,128]{1,0:T(8,128)S(1)}, f32[54,128]{1,0:T(8,128)S(1)}, u32[]{:S(2)}, u32[]{:S(2)}) %collective-permute-start.11) | collective-permute-done | bytes 27680 | tf_op jit(solution)/shard_map/ppermute | solution.py:499
  36.4 1.1 %last_kernel.1 = (f32[16,128]{1,0:T(8,128)S(1)}, f32[8,256]{1,0:T(8,128)S(1)}, f32[128,32]{1,0:T(8,128)S(1)}) custom-call(s32[1]{0:T(128)} %bitcast.where, f32[54,128]{1,0:T(8,128)S(1)} %add.49.chip, f32[54,128]{1,0:T(8,128)S(1)} %pad_maximum_fusion.2.near, f32[54,128]{1,0:T(8,128)S(1)} %collective-permute-done.11.far, ...), custom_call_target="tpu_custom_call" | custom-call | tf_op jit(solution)/shard_map/last_kernel/pallas_call | solution.py:450
  37.5 24.4 %all_to_all.11 = f32[128,1,32]{2,1,0:T(1,128)S(1)} all-to-all(f32[128,1,32]{2,1,0:T(1,128)S(1)} %bitcast.8), channel_id=1, replica_groups=mesh['grp'=2,'reg_0'=4,'reg_1'=4,'reg_2'=4] {'grp','reg_0','reg_1','reg_2'}, dimensions={0} | all-to-all | bytes 32768 | tf_op jit(solution)/shard_map/all_to_all | solution.py:559
  61.8 0.8 %final_kernel.1 = (f32[9,128]{1,0:T(8,128)}, f32[3,256]{1,0:T(4,128)}) custom-call(f32[128,32]{1,0:T(8,128)S(1)} %bitcast.7, f32[16,128]{1,0:T(8,128)S(1)} %get-tuple-element.35.v_old.v0, f32[16,128]{1,0:T(8,128)S(1)} %get-tuple-element.39.v_old.v1, f32[16,128]{1,0:T(8,128)S(1)} %get-tuple-element.45.v2, f32[8,256]{1,0:T(8,128)S(1)} %get-tuple-element.46.g0, ...), custom_call_target="tpu_custom_call" | custom-call | tf_op jit(solution)/shard_map/final_kernel/pallas_call | solution.py:450
  (15 shorter events, 0.2 us)
Async XLA Ops:
  3.3 2.5 %collective-permute-start = (f32[336,128]{1,0:T(8,128)S(1)}, f32[336,128]{1,0:T(8,128)S(1)}, u32[]{:S(2)}, u32[]{:S(2)}) collective-permute-start(f32[336,128]{1,0:T(8,128)S(1)} %get-tuple-element.26), channel_id=1, source_target_pairs={{0,64},{1,65},{2,66},{3,67},{4,68},{5,69},{6,70},{7,71},{8,72},{9,... | collective-permute-start | bytes 516104 | tf_op jit(solution)/shard_map/ppermute | solution.py:499
  5.9 4.1 %collective-permute-start.1 = (f32[224,128]{1,0:T(8,128)S(1)}, f32[224,128]{1,0:T(8,128)S(1)}, u32[]{:S(2)}, u32[]{:S(2)}) collective-permute-start(f32[224,128]{1,0:T(8,128)S(1)} %get-tuple-element.52), channel_id=1, source_target_pairs={{1,2},{3,4},{5,6},{7,8},{9,10},{11,12},{13,14},{15,16},{17,18},{19... | collective-permute-start | bytes 344072 | tf_op jit(solution)/shard_map/ppermute | solution.py:499
  7.4 6.6 %collective-permute-start.2 = (f32[224,128]{1,0:T(8,128)S(1)}, f32[224,128]{1,0:T(8,128)S(1)}, u32[]{:S(2)}, u32[]{:S(2)}) collective-permute-start(f32[224,128]{1,0:T(8,128)S(1)} %get-tuple-element.53), channel_id=1, source_target_pairs={{0,1},{2,3},{4,5},{6,7},{8,9},{10,11},{12,13},{14,15},{16,17},{18,... | collective-permute-start | bytes 344072 | tf_op jit(solution)/shard_map/ppermute | solution.py:499
  14.0 1.5 %collective-permute-start.3 = (f32[336,128]{1,0:T(8,128)S(1)}, f32[336,128]{1,0:T(8,128)S(1)}, u32[]{:S(2)}, u32[]{:S(2)}) collective-permute-start(f32[336,128]{1,0:T(8,128)S(1)} %pad_maximum_fusion.near), channel_id=1, source_target_pairs={{0,64},{1,65},{2,66},{3,67},{4,68},{5,69},{6,70},{7,71},{8,72},{9,... | collective-permute-start | bytes 516104 | tf_op jit(solution)/shard_map/ppermute | solution.py:499
  17.0 1.3 %collective-permute-start.4 = (f32[54,128]{1,0:T(8,128)S(1)}, f32[54,128]{1,0:T(8,128)S(1)}, u32[]{:S(2)}, u32[]{:S(2)}) collective-permute-start(f32[54,128]{1,0:T(8,128)S(1)} %get-tuple-element.33), channel_id=1, source_target_pairs={{0,64},{1,65},{2,66},{3,67},{4,68},{5,69},{6,70},{7,71},{8,72},{9,... | collective-permute-start | bytes 82952 | tf_op jit(solution)/shard_map/ppermute | solution.py:499
  18.3 5.3 %collective-permute-start.5 = (f32[36,128]{1,0:T(8,128)S(1)}, f32[36,128]{1,0:T(8,128)S(1)}, u32[]{:S(2)}, u32[]{:S(2)}) collective-permute-start(f32[36,128]{1,0:T(8,128)S(1)} %get-tuple-element.63), channel_id=1, source_target_pairs={{1,2},{3,4},{5,6},{7,8},{9,10},{11,12},{13,14},{15,16},{17,18},{19... | collective-permute-start | bytes 55304 | tf_op jit(solution)/shard_map/ppermute | solution.py:499
  20.5 4.3 %collective-permute-start.6 = (f32[36,128]{1,0:T(8,128)S(1)}, f32[36,128]{1,0:T(8,128)S(1)}, u32[]{:S(2)}, u32[]{:S(2)}) collective-permute-start(f32[36,128]{1,0:T(8,128)S(1)} %get-tuple-element.64), channel_id=1, source_target_pairs={{0,1},{2,3},{4,5},{6,7},{8,9},{10,11},{12,13},{14,15},{16,17},{18,... | collective-permute-start | bytes 55304 | tf_op jit(solution)/shard_map/ppermute | solution.py:499
  24.8 1.3 %collective-permute-start.7 = (f32[54,128]{1,0:T(8,128)S(1)}, f32[54,128]{1,0:T(8,128)S(1)}, u32[]{:S(2)}, u32[]{:S(2)}) collective-permute-start(f32[54,128]{1,0:T(8,128)S(1)} %pad_maximum_fusion.1.near), channel_id=1, source_target_pairs={{0,64},{1,65},{2,66},{3,67},{4,68},{5,69},{6,70},{7,71},{8,72},{9,... | collective-permute-start | bytes 82952 | tf_op jit(solution)/shard_map/ppermute | solution.py:499
  27.5 1.3 %collective-permute-start.8 = (f32[54,128]{1,0:T(8,128)S(1)}, f32[54,128]{1,0:T(8,128)S(1)}, u32[]{:S(2)}, u32[]{:S(2)}) collective-permute-start(f32[54,128]{1,0:T(8,128)S(1)} %get-tuple-element.38), channel_id=1, source_target_pairs={{0,64},{1,65},{2,66},{3,67},{4,68},{5,69},{6,70},{7,71},{8,72},{9,... | collective-permute-start | bytes 82952 | tf_op jit(solution)/shard_map/ppermute | solution.py:499
  28.8 5.1 %collective-permute-start.9 = (f32[36,128]{1,0:T(8,128)S(1)}, f32[36,128]{1,0:T(8,128)S(1)}, u32[]{:S(2)}, u32[]{:S(2)}) collective-permute-start(f32[36,128]{1,0:T(8,128)S(1)} %get-tuple-element.61), channel_id=1, source_target_pairs={{1,2},{3,4},{5,6},{7,8},{9,10},{11,12},{13,14},{15,16},{17,18},{19... | collective-permute-start | bytes 55304 | tf_op jit(solution)/shard_map/ppermute | solution.py:499
  29.6 5.4 %collective-permute-start.10 = (f32[36,128]{1,0:T(8,128)S(1)}, f32[36,128]{1,0:T(8,128)S(1)}, u32[]{:S(2)}, u32[]{:S(2)}) collective-permute-start(f32[36,128]{1,0:T(8,128)S(1)} %get-tuple-element.62), channel_id=1, source_target_pairs={{0,1},{2,3},{4,5},{6,7},{8,9},{10,11},{12,13},{14,15},{16,17},{18,... | collective-permute-start | bytes 55304 | tf_op jit(solution)/shard_map/ppermute | solution.py:499
  35.1 1.3 %collective-permute-start.11 = (f32[54,128]{1,0:T(8,128)S(1)}, f32[54,128]{1,0:T(8,128)S(1)}, u32[]{:S(2)}, u32[]{:S(2)}) collective-permute-start(f32[54,128]{1,0:T(8,128)S(1)} %pad_maximum_fusion.2.near), channel_id=1, source_target_pairs={{0,64},{1,65},{2,66},{3,67},{4,68},{5,69},{6,70},{7,71},{8,72},{9,... | collective-permute-start | bytes 82952 | tf_op jit(solution)/shard_map/ppermute | solution.py:499
